TPU v7x, 32 devices: a whole 2x2x4 slice. The times are simulated.
32 devices in a mesh: dp: 8 (over y, x, core), tensor: 4 (over z).
Axes of the slice: x: 2, y: 2, z: 4, core: 2. Of those that a mesh axis runs over, the one named last changes fastest.
Arguments:
- hidden_in: bfloat16 [32768, 768], P('dp'), may hold values from -6 to 6
- lengths: int32 [8], P('dp'), may hold values from 1024 to 4096, as said below
- labels: int32 [8], P('dp'), may hold values from 0 to 13
- out_cotangent: bfloat16 [32768, 768], P('dp'), may hold values from -6 to 6
- w_query: bfloat16 [768, 768], P(None, 'tensor'), may hold values from -0.21875 to 0.21875
- b_query: float32 [768], P('tensor'), may hold values from -1.75 to 1.75
- w_key: bfloat16 [768, 768], P(None, 'tensor'), may hold values from -0.21875 to 0.21875
- w_value: bfloat16 [768, 768], P(None, 'tensor'), may hold values from -0.21875 to 0.21875
- b_value: float32 [768], P('tensor'), may hold values from -1.75 to 1.75
- w_out: bfloat16 [768, 768], P('tensor'), may hold values from -6 to 6
- b_out: float32 [768], replicated, may hold values from -1.75 to 1.75
- ln1_gain: float32 [768], replicated, may hold values from 0.5 to 1.5
- ln1_bias: float32 [768], replicated, may hold values from -1.75 to 1.75
- w_in: bfloat16 [768, 3072], P(None, 'tensor'), may hold values from -0.21875 to 0.21875
- b_in: bfloat16 [3072], P('tensor'), may hold values from -1.75 to 1.75
- w_down: bfloat16 [3072, 768], P('tensor'), may hold values from -0.109375 to 0.109375
- b_down: float32 [768], replicated, may hold values from -1.75 to 1.75
- ln2_gain: float32 [768], replicated, may hold values from 0.5 to 1.5
- ln2_bias: float32 [768], replicated, may hold values from -1.75 to 1.75
- w_student: bfloat16 [768, 128], P(None, 'tensor'), may hold values from -0.21875 to 0.21875
- b_student: bfloat16 [128], P('tensor'), may hold values from -1.75 to 1.75
- pool_query: float32 [128], replicated, may hold values from -8 to 8
- w_pool: float32 [128, 128], replicated, may hold values from -0.5 to 0.5
- b_pool: float32 [128], replicated, may hold values from -1.75 to 1.75
- w_class: float32 [128, 14], replicated, may hold values from -1 to 1
- b_class: float32 [14], replicated, may hold values from -1.75 to 1.75
Outputs:
- hidden_out: bfloat16 [32768, 768], P('dp')
- logits: float32 [8, 14], P('dp')
- grad_in: bfloat16 [32768, 768], P('dp')
- grad_w_query: float32 [768, 768], P(None, 'tensor')
- grad_b_query: float32 [768], P('tensor')
- grad_w_key: float32 [768, 768], P(None, 'tensor')
- grad_w_value: float32 [768, 768], P(None, 'tensor')
- grad_b_value: float32 [768], P('tensor')
- grad_w_out: float32 [768, 768], P('tensor')
- grad_b_out: float32 [768], replicated
- grad_ln1_gain: float32 [768], replicated
- grad_ln1_bias: float32 [768], replicated
- grad_w_in: float32 [768, 3072], P(None, 'tensor')
- grad_b_in: float32 [3072], P('tensor')
- grad_w_down: float32 [3072, 768], P('tensor')
- grad_b_down: float32 [768], replicated
- grad_ln2_gain: float32 [768], replicated
- grad_ln2_bias: float32 [768], replicated
- grad_w_student: float32 [768, 128], P(None, 'tensor')
- grad_b_student: float32 [128], P('tensor')
- grad_pool_query: float32 [128], replicated
- grad_w_pool: float32 [128, 128], replicated
- grad_b_pool: float32 [128], replicated
- grad_w_class: float32 [128, 14], replicated
- grad_b_class: float32 [14], replicated
Inputs may be any that keep to these rules, and one draw needn't show every extreme that they name: Slot s holds one sequence in its first lengths[s] positions; some slot has all 4096 positions valid and some other has exactly 1024.
All inputs are finite; a program needn't handle non-finite values.
Results may differ from a plain program's by a relative error of at most 0.023.
Values may be sent and summed in bfloat16 or wider, within the bound.
No kernel may reach another device: no remote copies, remote signals or barrier semaphores. Data moves between devices by JAX's collectives and lax.ppermute only.
A program may use at most 256 MiB of HBM per device.

v0:
```python
import math

import jax
import jax.numpy as jnp
from jax import lax
from jax.sharding import PartitionSpec as P

HD = 64
POOL_HEADS = 2


epsilon = 1e-06
mask_fill = -1e30
highest = lax.Precision.HIGHEST


def matmul(left, right):
    return jnp.dot(left, right, preferred_element_type=jnp.float32)


def across_rows(left, right):
    return lax.dot_general(
        left, right, (((0,), (0,)), ((), ())), preferred_element_type=jnp.float32
    )


def against(left, right):
    return lax.dot_general(
        left, right, (((1,), (1,)), ((), ())), preferred_element_type=jnp.float32
    )


def gelu_exact(values):
    return jax.nn.gelu(values, approximate=False)


def normalize(resid, gain, shift):
    center = resid - jnp.mean(resid, axis=-1, keepdims=True)
    invstd = lax.rsqrt(jnp.mean(center * center, axis=-1, keepdims=True) + epsilon)
    normed = center * invstd
    return (normed * gain + shift, normed, invstd)


def normalize_back(grad, normed, invstd, gain):
    scaled = grad * gain
    inner = (
        scaled
        - jnp.mean(scaled, axis=-1, keepdims=True)
        - normed * jnp.mean(scaled * normed, axis=-1, keepdims=True)
    )
    return (invstd * inner, jnp.sum(grad * normed, axis=0), jnp.sum(grad, axis=0))


def student_tail(student, valid_keys, labels, pool_query, w_pool, b_pool, w_class, b_class):
    seq_count, slot_len, student_width = student.shape
    head_width = student_width // POOL_HEADS
    split_heads = student.reshape(seq_count, slot_len, POOL_HEADS, head_width)
    probes = pool_query.reshape(POOL_HEADS, head_width)
    scores = jnp.einsum("nthd,hd->nht", split_heads, probes, precision=highest) * (
        1.0 / math.sqrt(head_width)
    )
    scores = jnp.where(valid_keys[:, None, :], scores, mask_fill)
    weights = jax.nn.softmax(scores, axis=-1)
    pooled = jnp.einsum("nht,nthd->nhd", weights, split_heads, precision=highest).reshape(
        seq_count, student_width
    )
    squashed = jnp.tanh(jnp.dot(pooled, w_pool, precision=highest) + b_pool)
    logits = jnp.dot(squashed, w_class, precision=highest) + b_class
    classes = jnp.arange(logits.shape[1], dtype=jnp.int32)
    picked = jnp.sum(jnp.where(classes[None, :] == labels[:, None], logits, 0.0), axis=1)
    return (jnp.sum(jax.nn.logsumexp(logits, axis=1) - picked), logits)


def masked_scores(query_block, keys, valid_keys, score_scale):
    scores = (
        jnp.einsum("qhd,khd->hqk", query_block, keys, preferred_element_type=jnp.float32)
        * score_scale
    )
    return jnp.where(valid_keys[None, None, :], scores, mask_fill)


def attend_forward(queries, keys, values, valid_keys, block_len):
    slot_len, head_count, head_dim = queries.shape
    score_scale = 1.0 / math.sqrt(head_dim)

    def one_block(query_block):
        scores = masked_scores(query_block, keys, valid_keys, score_scale)
        row_max = jnp.max(scores, axis=-1, keepdims=True)
        log_total = row_max + jnp.log(jnp.sum(jnp.exp(scores - row_max), axis=-1, keepdims=True))
        weights_low = jnp.exp(scores - log_total).astype(jnp.bfloat16)
        mixed = jnp.einsum("hqk,khd->qhd", weights_low, values, preferred_element_type=jnp.float32)
        return (mixed.astype(jnp.bfloat16), log_total[..., 0])

    mixed, log_totals = lax.map(
        one_block, queries.reshape(slot_len // block_len, block_len, head_count, head_dim)
    )
    return (mixed.reshape(slot_len, head_count * head_dim), log_totals)


def attend_backward(queries, keys, values, valid_keys, log_totals, grad_mixed, block_len):
    slot_len, head_count, head_dim = queries.shape
    score_scale = 1.0 / math.sqrt(head_dim)
    block_count = slot_len // block_len

    def one_block(running, block_item):
        grad_keys, grad_values = running
        query_block, log_total, grad_block = block_item
        scores = masked_scores(query_block, keys, valid_keys, score_scale)
        weights = jnp.exp(scores - log_total[..., None])
        grad_values = grad_values + jnp.einsum(
            "hqk,qhd->khd",
            weights.astype(jnp.bfloat16),
            grad_block,
            preferred_element_type=jnp.float32,
        )
        grad_weights = jnp.einsum(
            "qhd,khd->hqk", grad_block, values, preferred_element_type=jnp.float32
        )
        centered = grad_weights - jnp.sum(weights * grad_weights, axis=-1, keepdims=True)
        grad_scores = (weights * centered).astype(jnp.bfloat16)
        grad_query = (
            jnp.einsum("hqk,khd->qhd", grad_scores, keys, preferred_element_type=jnp.float32)
            * score_scale
        )
        grad_keys = (
            grad_keys
            + jnp.einsum(
                "hqk,qhd->khd", grad_scores, query_block, preferred_element_type=jnp.float32
            )
            * score_scale
        )
        return ((grad_keys, grad_values), grad_query)

    zeros = jnp.zeros((slot_len, head_count, head_dim), jnp.float32)
    block_shape = (block_count, block_len, head_count, head_dim)
    (grad_keys, grad_values), grad_queries = lax.scan(
        one_block,
        (zeros, zeros),
        (queries.reshape(block_shape), log_totals, grad_mixed.reshape(block_shape)),
    )
    flat_shape = (slot_len, head_count * head_dim)
    return (
        grad_queries.reshape(flat_shape),
        grad_keys.reshape(flat_shape),
        grad_values.reshape(flat_shape),
    )


def body(
    hidden_in,
    lengths,
    labels,
    out_cotangent,
    w_query,
    b_query,
    w_key,
    w_value,
    b_value,
    w_out,
    b_out,
    ln1_gain,
    ln1_bias,
    w_in,
    b_in,
    w_down,
    b_down,
    ln2_gain,
    ln2_bias,
    w_student,
    b_student,
    pool_query,
    w_pool,
    b_pool,
    w_class,
    b_class,
):
    row_count = hidden_in.shape[0]
    seq_count = lengths.shape[0]
    slot_len = row_count // seq_count
    group_size = lax.axis_size("tensor")
    own_count = row_count // group_size
    tensor_rank = lax.axis_index("tensor")
    own_start = tensor_rank * own_count
    local_width = w_query.shape[1]
    head_count = local_width // HD
    block_len = min(512, slot_len)
    positions = jnp.arange(slot_len, dtype=jnp.int32)
    valid_keys = positions[None, :] < lengths[:, None]
    own_rows = own_start + jnp.arange(own_count, dtype=jnp.int32)
    seq_index = jnp.arange(seq_count, dtype=jnp.int32)
    own_length = jnp.sum(
        jnp.where((own_rows // slot_len)[:, None] == seq_index[None, :], lengths[None, :], 0),
        axis=1,
    )
    row_valid = (own_rows % slot_len < own_length).astype(jnp.float32)
    hidden_own = lax.dynamic_slice_in_dim(hidden_in, own_start, own_count, 0)
    cot_own = lax.dynamic_slice_in_dim(out_cotangent, own_start, own_count, 0)
    w_project = jnp.concatenate([w_query, w_key, w_value], axis=1)
    bias_project = jnp.concatenate([b_query, jnp.zeros_like(b_query), b_value])
    projected = (matmul(hidden_in, w_project) + bias_project).astype(jnp.bfloat16)
    head_shape = (slot_len, head_count, HD)
    sequence = 0
    queries = projected[:, :local_width].reshape(head_shape)
    keys = projected[:, local_width : 2 * local_width].reshape(head_shape)
    values = projected[:, 2 * local_width :].reshape(head_shape)
    mixed, log_totals = attend_forward(queries, keys, values, valid_keys[sequence], block_len)
    per_sequence = [(queries, keys, values, log_totals)]
    attention_own = lax.psum_scatter(
        matmul(mixed, w_out), "tensor", scatter_dimension=0, tiled=True
    )
    resid1 = attention_own + b_out + hidden_own.astype(jnp.float32)
    first, normed1, invstd1 = normalize(resid1, ln1_gain, ln1_bias)
    first_low = first.astype(jnp.bfloat16)
    first_all = lax.all_gather(first_low, "tensor", axis=0, tiled=True)
    pre = matmul(first_all, w_in) + b_in
    act, act_back = jax.vjp(gelu_exact, pre)
    act_low = act.astype(jnp.bfloat16)
    ffn_own = lax.psum_scatter(
        matmul(act_low, w_down).astype(jnp.bfloat16), "tensor", scatter_dimension=0, tiled=True
    ).astype(jnp.float32)
    resid2 = ffn_own + b_down + first_low.astype(jnp.float32)
    second, normed2, invstd2 = normalize(resid2, ln2_gain, ln2_bias)
    second_low = second.astype(jnp.bfloat16)
    w_stud_all, b_stud_all = (
        lax.all_gather(w_student, "tensor", axis=1, tiled=True),
        lax.all_gather(b_student.reshape(1, -1), "tensor", axis=1, tiled=True),
    )
    student_low = (matmul(second_low, w_stud_all) + b_stud_all).astype(jnp.bfloat16)
    hidden_out, student_all = (
        lax.all_gather(second_low, "tensor", axis=0, tiled=True),
        lax.all_gather(student_low, "tensor", axis=0, tiled=True),
    )

    def tail_function(student_rows, probe_rows, pool_matrix, pool_shift, class_matrix, class_shift):
        return student_tail(
            student_rows,
            valid_keys,
            labels,
            probe_rows,
            pool_matrix,
            pool_shift,
            class_matrix,
            class_shift,
        )

    student_seq = student_all.astype(jnp.float32).reshape(seq_count, slot_len, -1)
    seq_loss, tail_back, logits = jax.vjp(
        tail_function, student_seq, pool_query, w_pool, b_pool, w_class, b_class, has_aux=True
    )
    grad_student, grad_pool_query, grad_w_pool, grad_b_pool, grad_w_class, grad_b_class = tail_back(
        jnp.ones_like(seq_loss)
    )
    grad_stud_own = lax.dynamic_slice_in_dim(
        grad_student.reshape(row_count, -1), own_start, own_count, 0
    ).astype(jnp.bfloat16)
    grad_second = cot_own.astype(jnp.float32) * row_valid[:, None] + against(
        grad_stud_own, w_stud_all
    )
    grad_stud_weight = across_rows(second_low, grad_stud_own)
    grad_stud_bias = jnp.sum(grad_stud_own, axis=0, dtype=jnp.float32)
    grad_resid2, grad_ln2_gain, grad_ln2_bias = normalize_back(
        grad_second, normed2, invstd2, ln2_gain
    )
    grad_b_down = jnp.sum(grad_resid2, axis=0)
    grad_ffn_low = grad_resid2.astype(jnp.bfloat16)
    grad_ffn_all = lax.all_gather(grad_ffn_low, "tensor", axis=0, tiled=True)
    grad_w_down = across_rows(act_low, grad_ffn_all)
    grad_act = against(grad_ffn_all, w_down)
    grad_pre = act_back(grad_act)[0].astype(jnp.bfloat16)
    grad_w_in = across_rows(first_all, grad_pre)
    grad_b_in = jnp.sum(grad_pre, axis=0, dtype=jnp.float32)
    grad_first = (
        lax.psum_scatter(
            against(grad_pre, w_in).astype(jnp.bfloat16), "tensor", scatter_dimension=0, tiled=True
        ).astype(jnp.float32)
        + grad_resid2
    )
    grad_resid1, grad_ln1_gain, grad_ln1_bias = normalize_back(
        grad_first, normed1, invstd1, ln1_gain
    )
    grad_b_out = jnp.sum(grad_resid1, axis=0)
    grad_mix_all = lax.all_gather(grad_resid1.astype(jnp.bfloat16), "tensor", axis=0, tiled=True)
    grad_w_out = across_rows(mixed, grad_mix_all)
    grad_att = against(grad_mix_all, w_out).astype(jnp.bfloat16)
    sequence = 0
    queries, keys, values, log_totals = per_sequence[sequence]
    grad_here = grad_att[sequence * slot_len : (sequence + 1) * slot_len].reshape(head_shape)
    grad_queries, grad_keys, grad_values = attend_backward(
        queries, keys, values, valid_keys[sequence], log_totals, grad_here, block_len
    )
    grad_parts = jnp.concatenate([grad_queries, grad_keys, grad_values], axis=1).astype(
        jnp.bfloat16
    )
    grad_w_project = across_rows(hidden_in, grad_parts)
    grad_b_project = jnp.sum(grad_parts, axis=0, dtype=jnp.float32)
    grad_in_own = (
        lax.psum_scatter(
            against(grad_parts, w_project).astype(jnp.bfloat16),
            "tensor",
            scatter_dimension=0,
            tiled=True,
        ).astype(jnp.float32)
        + grad_resid1
    )
    grad_in = lax.all_gather(grad_in_own.astype(jnp.bfloat16), "tensor", axis=0, tiled=True)
    summed = lax.psum(
        (
            grad_w_project[:, :local_width],
            grad_b_project[:local_width],
            grad_w_project[:, local_width : 2 * local_width],
            grad_w_project[:, 2 * local_width :],
            grad_b_project[2 * local_width :],
            grad_w_out,
            grad_w_in,
            grad_b_in,
            grad_w_down,
            grad_pool_query,
            grad_w_pool,
            grad_b_pool,
            grad_w_class,
            grad_b_class,
        ),
        "dp",
    )
    totals = lax.psum(
        (
            grad_b_out,
            grad_ln1_gain,
            grad_ln1_bias,
            grad_b_down,
            grad_ln2_gain,
            grad_ln2_bias,
            grad_stud_weight,
            grad_stud_bias,
        ),
        ("dp", "tensor"),
    )
    student_cols = w_student.shape[1]
    grad_w_student = lax.dynamic_slice_in_dim(
        totals[6], tensor_rank * student_cols, student_cols, 1
    )
    grad_b_student = lax.dynamic_slice_in_dim(
        totals[7], tensor_rank * student_cols, student_cols, 0
    )
    return (
        hidden_out,
        logits,
        grad_in,
        summed[0],
        summed[1],
        summed[2],
        summed[3],
        summed[4],
        summed[5],
        totals[0],
        totals[1],
        totals[2],
        summed[6],
        summed[7],
        summed[8],
        totals[3],
        totals[4],
        totals[5],
        grad_w_student,
        grad_b_student,
        summed[9],
        summed[10],
        summed[11],
        summed[12],
        summed[13],
    )


def solution(mesh):
    in_specs = (
        P("dp", None),
        P("dp"),
        P("dp"),
        P("dp", None),
        P(None, "tensor"),
        P("tensor"),
        P(None, "tensor"),
        P(None, "tensor"),
        P("tensor"),
        P("tensor", None),
        P(),
        P(),
        P(),
        P(None, "tensor"),
        P("tensor"),
        P("tensor", None),
        P(),
        P(),
        P(),
        P(None, "tensor"),
        P("tensor"),
        P(),
        P(),
        P(),
        P(),
        P(),
    )
    out_specs = (
        P("dp", None),
        P("dp", None),
        P("dp", None),
        P(None, "tensor"),
        P("tensor"),
        P(None, "tensor"),
        P(None, "tensor"),
        P("tensor"),
        P("tensor", None),
        P(),
        P(),
        P(),
        P(None, "tensor"),
        P("tensor"),
        P("tensor", None),
        P(),
        P(),
        P(),
        P(None, "tensor"),
        P("tensor"),
        P(),
        P(),
        P(),
        P(),
        P(),
    )
    return jax.shard_map(body, mesh=mesh, in_specs=in_specs, out_specs=out_specs, check_vma=False)
```

profile of v0, /device:TPU:0, one launch (start us, length us, event | category | flops | bytes accessed | tf_op | source)
XLA Modules:
  0.0 2484.8 jit_solution(983371729661630949)
XLA Ops:
  22.4 215.0 %while.28 = (s32[]{:T(128)}, bf16[8,512,3,64]{1,3,2,0:T(8,128)(2,1)}, f32[8,3,512]{2,1,0:T(4,128)}, bf16[8,512,3,64]{1,3,2,0:T(8,128)(2,1)}, bf16[4096,3,64]{0,2...) while((s32[]{:T(128)}, bf16[8,512,3,64]{1,3,2,0:T(8,128)(2,1)}, ...), condition=%wide.region_3.4_spmd.clone, body=%wide.region_0.3_spmd.clone.sunk | while | flops 1679919616 | bytes 179767440 | solution.py:94
  248.1 214.7 %reduce-scatter.5.cloned.1.call-done = f32[1024,768]{1,0:T(8,128)} async-done(((f32[4096,768]{1,0:T(8,128)}), f32[1024,768]{1,0:T(8,128)}) %reduce-scatter.5.cloned.1.call-update) | async-done | bytes 3145744 | tf_op jit(solution)/shard_map/reduce_scatter | solution.py:208
  469.1 116.5 %all-gather.8.cloned.1.call-done = bf16[4096,768]{1,0:T(8,128)(2,1)} async-done(((bf16[1024,768]{1,0:T(8,128)(2,1)}), bf16[4096,768]{1,0:T(8,128)(2,1)}) %all-gather.8.cloned.1.call-update) | async-done | bytes 6291472 | tf_op jit(solution)/shard_map/all_gather | solution.py:214
  585.6 34.0 %multiply_convert_fusion.1 = (bf16[4096,768]{1,0:T(8,128)(2,1)S(1)}, f32[4096,768]{1,0:T(8,128)}, f32[4096,768]{1,0:T(8,128)}) fusion(f32[768]{0:T(1024)S(1)} %convert_element_type.104, bf16[4096,768]{1,0:T(8,128)(2,1)} %all-gather.8.cloned.1.call-done, bf16[768,768]{1,0:T(8,128)(2,1)S(1)} %copy-done), kind=kOutput, calls=%fused_computation.56 | convolution fusion | flops 5039456256 | bytes 38931456 | tf_op jit(solution)/shard_map/dot_general | solution.py:18
  655.9 85.9 %reduce-scatter.7.cloned.1.call-done = bf16[1024,768]{1,0:T(8,128)(2,1)} async-done(((bf16[4096,768]{1,0:T(8,128)(2,1)}), bf16[1024,768]{1,0:T(8,128)(2,1)}) %reduce-scatter.7.cloned.1.call-update) | async-done | bytes 1572880 | tf_op jit(solution)/shard_map/reduce_scatter | solution.py:218
  753.2 26.9 %all-gather.12.cloned.1.call-done = bf16[4096,128]{1,0:T(8,128)(2,1)} async-done(((bf16[1024,128]{1,0:T(8,128)(2,1)}), bf16[4096,128]{1,0:T(8,128)(2,1)}) %all-gather.12.cloned.1.call-update) | async-done | bytes 1048592 | tf_op jit(solution)/shard_map/all_gather | solution.py:231
  804.7 114.8 %all-gather.14.cloned.1.call-done = bf16[4096,768]{1,0:T(8,128)(2,1)} async-done(((bf16[1024,768]{1,0:T(8,128)(2,1)}), bf16[4096,768]{1,0:T(8,128)(2,1)}) %all-gather.14.cloned.1.call-update) | async-done | bytes 6291472 | tf_op jit(solution)/shard_map/all_gather | solution.py:266
  919.5 17.4 convert_reduce_fusion
  946.8 109.1 %reduce-scatter.9.cloned.1.call-done = bf16[1024,768]{1,0:T(8,128)(2,1)} async-done(((bf16[4096,768]{1,0:T(8,128)(2,1)}), bf16[1024,768]{1,0:T(8,128)(2,1)}) %reduce-scatter.9.cloned.1.call-update) | async-done | bytes 1572880 | tf_op jit(solution)/shard_map/reduce_scatter | solution.py:273
  1066.3 115.9 %all-gather.16.cloned.1.call-done = bf16[4096,768]{1,0:T(8,128)(2,1)} async-done(((bf16[1024,768]{1,0:T(8,128)(2,1)}), bf16[4096,768]{1,0:T(8,128)(2,1)}) %all-gather.16.cloned.1.call-update) | async-done | bytes 6291472 | tf_op jit(solution)/shard_map/all_gather | solution.py:282
  1189.6 663.1 %while.29 = (s32[]{:T(128)}, f32[4096,3,64]{0,2,1:T(8,128)}, f32[4096,3,64]{0,2,1:T(8,128)}, bf16[8,512,3,64]{1,3,2,0:T(8,128)(2,1)}, bf16[8,512,3,64]{1,3,2,0:T...) while((s32[]{:T(128)}, f32[4096,3,64]{0,2,1:T(8,128)}, ...), condition=%wide.region_22.23_spmd.clone, body=%wide.region_20.22_spmd.clone.sunk | while | flops 4124936704 | bytes 207284384 | solution.py:136
  1214.6 17.0 multiply_reduce_fusion.10
  1231.6 21.4 multiply_convert_fusion.3
  1296.8 17.0 multiply_reduce_fusion.10
  1313.8 21.4 multiply_convert_fusion.3
  1379.9 17.0 multiply_reduce_fusion.10
  1396.9 21.4 multiply_convert_fusion.3
  1463.0 17.0 multiply_reduce_fusion.10
  1480.0 21.4 multiply_convert_fusion.3
  1546.2 17.0 multiply_reduce_fusion.10
  1563.1 21.4 multiply_convert_fusion.3
  1629.2 17.0 multiply_reduce_fusion.10
  1646.2 21.4 multiply_convert_fusion.3
  1729.3 21.4 multiply_convert_fusion.3
  1812.4 21.4 multiply_convert_fusion.3
  1870.6 105.9 %reduce-scatter.11.cloned.1.call-done = bf16[1024,768]{1,0:T(8,128)(2,1)} async-done(((bf16[4096,768]{1,0:T(8,128)(2,1)}), bf16[1024,768]{1,0:T(8,128)(2,1)}) %reduce-scatter.11.cloned.1.call-update) | async-done | bytes 1572880 | tf_op jit(solution)/shard_map/reduce_scatter | solution.py:297
  2012.2 97.6 %all-reduce.7.cloned.1.call-done = f32[768,128]{0,1:T(8,128)} async-done(((f32[768,128]{0,1:T(8,128)}), f32[768,128]{0,1:T(8,128)}) %all-reduce.7.cloned.1.call-update) | async-done | bytes 393232 | tf_op jit(solution)/shard_map/psum | solution.py:325
  2111.3 114.4 %all-gather.10.cloned.1.call-done = bf16[4096,768]{1,0:T(8,128)(2,1)} async-done(((bf16[1024,768]{1,0:T(8,128)(2,1)}), bf16[4096,768]{1,0:T(8,128)(2,1)}) %all-gather.10.cloned.1.call-update) | async-done | bytes 6291472 | tf_op jit(solution)/shard_map/all_gather | solution.py:230
  2225.7 42.8 %all-reduce.1 = (f32[768]{0:T(1024)}, f32[768]{0:T(1024)}, f32[768]{0:T(1024)}, f32[768]{0:T(1024)}, f32[768]{0:T(1024)}, /*index=5*/f32[768]{0:T(1024)}, f32[128]{0:T(128)S(1)}) all-reduce(f32[768]{0:T(1024)S(1)} %copy-done.50, f32[768]{0:T(1024)S(1)} %copy-done.47, ...), channel_id=1, replica_groups=mesh['dp'=8,'tensor'=4] {'dp','tensor'}, use_global_device_ids=true, to_apply=%region_32.33 | all-reduce | flops 4736 | bytes 37888 | tf_op jit(solution)/shard_map/psum | solution.py:325
  2271.4 25.6 %all-reduce.2 = (f32[192]{0:T(256)}, f32[192]{0:T(256)}, f32[768]{0:T(1024)}, f32[128]{0:T(128)}, f32[128]{0:T(128)}, /*index=5*/f32[128,14]{0,1:T(8,128)}, f32[14]{0:T(128)}) all-reduce(f32[192]{0:T(256)S(1)} %get-tuple-element.317, f32[192]{0:T(256)S(1)} %get-tuple-element.316, ...), channel_id=1, replica_groups=mesh['dp'=8,'tensor'=4] {'dp'}, use_global_device_ids=true, to_apply=%region_26.27 | all-reduce | flops 3214 | bytes 25712 | tf_op jit(solution)/shard_map/psum | solution.py:306
  2297.0 45.6 %all-gather.18.cloned.1.call-done = bf16[4096,768]{1,0:T(8,128)(2,1)} async-done(((bf16[1024,768]{1,0:T(8,128)(2,1)}), bf16[4096,768]{1,0:T(8,128)(2,1)}) %all-gather.18.cloned.1.call-update) | async-done | bytes 6291472 | tf_op jit(solution)/shard_map/all_gather | solution.py:305
  2342.6 119.6 %all-reduce.9.cloned.1.call-done = (f32[768,192]{0,1:T(8,128)}, f32[768,192]{0,1:T(8,128)}, f32[768,192]{0,1:T(8,128)}, f32[192,768]{1,0:T(8,128)}, f32[768,768]...) async-done(((f32[768,192]{0,1:T(8,128)}, f32[768,192]{0,1:T(8,128)}, f32[768,192]{0,1:T(8,128)}, f32[192,768]{1,0:T(8,128)}, f32[768,768]{1,0:T(8,128)}, ...) | async-done | bytes 7143440 | tf_op jit(solution)/shard_map/psum | solution.py:306
  (395 shorter events, 804.5 us)
Async XLA Ops:
  7.2 578.4 %copy-start = (bf16[768,768]{1,0:T(8,128)(2,1)S(1)}, bf16[768,768]{1,0:T(8,128)(2,1)}, u32[]{:S(2)}) copy-start(bf16[768,768]{1,0:T(8,128)(2,1)} %param.43) | copy-start | bytes 3538948
  7.2 455.6 %reduce-scatter.5.cloned.1.call-start = ((), (), s32[]{:S(2)}) async-start(), calls=%async_computation.4 | async-start | bytes 15728640 | tf_op jit(solution)/shard_map/reduce_scatter | solution.py:208
  248.1 214.7 %copy-start.58 = (f32[768]{0:T(1024)S(1)}, f32[768]{0:T(1024)}, u32[]{:S(2)}) copy-start(f32[768]{0:T(1024)} %param.40) | copy-start | bytes 9220
  248.1 337.5 %all-gather.8.cloned.1.call-start = ((), (), s32[]{:S(2)}) async-start(), calls=%async_computation.5 | async-start | bytes 7864320 | tf_op jit(solution)/shard_map/all_gather | solution.py:214
  469.0 272.7 %reduce-scatter.7.cloned.1.call-start = ((), (), s32[]{:S(2)}) async-start(), calls=%async_computation.6 | async-start | bytes 7864320 | tf_op jit(solution)/shard_map/reduce_scatter | solution.py:218
  469.1 153.1 %copy-start.68 = (bf16[768,768]{1,0:T(8,128)(2,1)S(1)}, bf16[768,768]{1,0:T(8,128)(2,1)}, u32[]{:S(2)}) copy-start(bf16[768,768]{1,0:T(8,128)(2,1)} %param.45) | copy-start | bytes 3538948
  629.2 112.5 %copy-start.44 = (f32[768]{0:T(1024)S(1)}, f32[768]{0:T(1024)}, u32[]{:S(2)}) copy-start(f32[768]{0:T(1024)} %param.46) | copy-start | bytes 9220
  629.2 150.9 %all-gather.12.cloned.1.call-start = ((), (), s32[]{:S(2)}) async-start(), calls=%async_computation.8 | async-start | bytes 1310720 | tf_op jit(solution)/shard_map/all_gather | solution.py:231
  750.3 36.5 %copy-start.11 = (bf16[1024,768]{1,0:T(8,128)(2,1)}, bf16[1024,768]{1,0:T(8,128)(2,1)S(1)}, u32[]{:S(2)}) copy-start(bf16[1024,768]{1,0:T(8,128)(2,1)S(1)} %add_convert_fusion.3) | copy-start | bytes 4718596
  750.3 37.2 %copy-start.36 = (f32[128,128]{1,0:T(8,128)S(1)}, f32[128,128]{1,0:T(8,128)}, u32[]{:S(2)}) copy-start(f32[128,128]{1,0:T(8,128)} %param.52) | copy-start | bytes 196612
  750.3 37.1 %copy-start.66 = (f32[128]{0:T(128)S(1)}, f32[128]{0:T(128)}, u32[]{:S(2)}) copy-start(f32[128]{0:T(128)} %param.53) | copy-start | bytes 1540
  750.3 37.3 %copy-start.46 = (f32[128,14]{0,1:T(8,128)S(1)}, f32[128,14]{0,1:T(8,128)}, u32[]{:S(2)}) copy-start(f32[128,14]{0,1:T(8,128)} %param.54) | copy-start | bytes 21508
  750.3 37.3 %copy-start.67 = (f32[14]{0:T(128)S(1)}, f32[14]{0:T(128)}, u32[]{:S(2)}) copy-start(f32[14]{0:T(128)} %param.55) | copy-start | bytes 172
  751.6 167.8 %all-gather.14.cloned.1.call-start = ((), (), s32[]{:S(2)}) async-start(), calls=%async_computation.9 | async-start | bytes 7864320 | tf_op jit(solution)/shard_map/all_gather | solution.py:266
  804.5 251.4 %reduce-scatter.9.cloned.1.call-start = ((), (), s32[]{:S(2)}) async-start(), calls=%async_computation.10 | async-start | bytes 7864320 | tf_op jit(solution)/shard_map/reduce_scatter | solution.py:273
  946.7 235.6 %all-gather.16.cloned.1.call-start = ((), (), s32[]{:S(2)}) async-start(), calls=%async_computation.11 | async-start | bytes 7864320 | tf_op jit(solution)/shard_map/all_gather | solution.py:282
  1064.9 117.4 %copy-start.35 = (bf16[192,768]{1,0:T(8,128)(2,1)S(1)}, bf16[192,768]{1,0:T(8,128)(2,1)}, u32[]{:S(2)}) copy-start(bf16[192,768]{1,0:T(8,128)(2,1)} %param.39) | copy-start | bytes 884740
  1066.3 910.2 %reduce-scatter.11.cloned.1.call-start = ((), (), s32[]{:S(2)}) async-start(), calls=%async_computation.12 | async-start | bytes 7864320 | tf_op jit(solution)/shard_map/reduce_scatter | solution.py:297
  1867.3 242.5 %all-reduce.7.cloned.1.call-start = ((), (), s32[]{:S(2)}) async-start(), calls=%async_computation.14 | async-start | bytes 786432 | tf_op jit(solution)/shard_map/psum | solution.py:325
  1869.9 355.8 %all-gather.10.cloned.1.call-start = ((), (), s32[]{:S(2)}) async-start(), calls=%async_computation.7 | async-start | bytes 7864320 | tf_op jit(solution)/shard_map/all_gather | solution.py:230
  1870.5 109.9 %copy-start.72 = (f32[2,1,64]{2,1,0:T(1,128)S(1)}, f32[2,1,64]{2,1,0:T(1,128)}, u32[]{:S(2)}) copy-start(f32[2,1,64]{2,1,0:T(1,128)} %copy-done.71) | copy-start | bytes 1540
  1870.5 110.0 %copy-start.53 = (f32[128]{0:T(128)S(1)}, f32[128]{0:T(128)}, u32[]{:S(2)}) copy-start(f32[128]{0:T(128)} %copy-done.52) | copy-start | bytes 1540
  1870.5 472.1 %all-gather.18.cloned.1.call-start = ((), (), s32[]{:S(2)}) async-start(), calls=%async_computation.13 | async-start | bytes 7864320 | tf_op jit(solution)/shard_map/all_gather | solution.py:305
  1980.3 481.9 %all-reduce.9.cloned.1.call-start = ((), (), s32[]{:S(2)}) async-start(), calls=%async_computation.15 | async-start | bytes 14286848 | tf_op jit(solution)/shard_map/psum | solution.py:306
  2009.9 215.8 %copy-start.47 = (f32[768]{0:T(1024)S(1)}, f32[768]{0:T(1024)}, u32[]{:S(2)}) copy-start(f32[768]{0:T(1024)} %get-tuple-element.226) | copy-start | bytes 9220
  2009.9 215.8 %copy-start.48 = (f32[768]{0:T(1024)S(1)}, f32[768]{0:T(1024)}, u32[]{:S(2)}) copy-start(f32[768]{0:T(1024)} %get-tuple-element.231) | copy-start | bytes 9220
  2009.9 215.8 %copy-start.49 = (f32[768]{0:T(1024)S(1)}, f32[768]{0:T(1024)}, u32[]{:S(2)}) copy-start(f32[768]{0:T(1024)} %get-tuple-element.234) | copy-start | bytes 9220
  2009.9 215.8 %copy-start.50 = (f32[768]{0:T(1024)S(1)}, f32[768]{0:T(1024)}, u32[]{:S(2)}) copy-start(f32[768]{0:T(1024)} %get-tuple-element.294) | copy-start | bytes 9220
  2009.9 215.8 %copy-start.59 = (f32[768]{0:T(1024)S(1)}, f32[768]{0:T(1024)}, u32[]{:S(2)}) copy-start(f32[768]{0:T(1024)} %get-tuple-element.228) | copy-start | bytes 9220
  2009.9 215.8 %copy-start.60 = (f32[768]{0:T(1024)S(1)}, f32[768]{0:T(1024)}, u32[]{:S(2)}) copy-start(f32[768]{0:T(1024)} %get-tuple-element.233) | copy-start | bytes 9220
  2009.9 215.8 %copy-start.65 = (f32[128]{0:T(128)S(1)}, f32[128]{0:T(128)}, u32[]{:S(2)}) copy-start(f32[128]{0:T(128)} %get-tuple-element.292) | copy-start | bytes 1540
  2010.0 261.4 %copy-start.61 = (f32[768]{0:T(1024)S(1)}, f32[768]{0:T(1024)}, u32[]{:S(2)}) copy-start(f32[768]{0:T(1024)} %get-tuple-element.296) | copy-start | bytes 9220
  (67 other events, 330.3 us)
Sparse Core Ops, SparseCore 0:
  248.2 214.5 reduce-scatter.4
  469.1 116.3 all-gather.7
  629.3 112.3 reduce-scatter.6
  751.7 28.3 all-gather.11
  804.6 114.8 all-gather.13
  946.8 108.9 reduce-scatter.8
  1066.4 115.8 all-gather.15
  1867.5 108.9 reduce-scatter.10
  1981.8 127.9 all-reduce.6
  2111.3 114.3 all-gather.9
  2227.9 114.6 all-gather.17
  2349.0 113.2 all-reduce.8
where the time goes:
time: 2490 us; the launch traced here: 2480 us
  waiting for transfers between devices  1270 us (51%)
  matrix products  750 us (30%)
  other arithmetic  274 us (11%)
  blocking collectives  92.9 us (4%)
  local copies, waits for them, and re-layouts  78.9 us (3%)
    reduce_scatter x1, waiting for transfers between devices, body(): lax.psum_scatter(matmul(mixed, w_out), 'tensor', scatter_dimension=0, til...  215 us
    convert_element_type x8, other arithmetic, one_block(): grad_scores = (weights * centered).astype(jnp.bfloat16)  171 us
    dot_general x8, matrix products, one_block(): jnp.einsum('qhd,khd->hqk', grad_block, values, preferred_element_type=jnp...  136 us
    dot_general x16, matrix products, masked_scores(): jnp.einsum('qhd,khd->hqk', query_block, keys, preferred_element_type=jnp....  130 us
    psum x1, waiting for transfers between devices, body(): lax.psum((grad_w_project[:, :local_width], grad_b_project[:local_width],...  120 us
    all_gather x1, waiting for transfers between devices, body(): first_all = lax.all_gather(first_low, 'tensor', axis=0, tiled=True)  116 us
    all_gather x1, waiting for transfers between devices, body(): lax.all_gather(grad_resid1.astype(jnp.bfloat16), 'tensor', axis=0, tiled=...  116 us
    all_gather x1, waiting for transfers between devices, body(): grad_ffn_all = lax.all_gather(grad_ffn_low, 'tensor', axis=0, tiled=True)  115 us
  transfers between devices with their start and end apart: 12, of which 12 were waited for; matrix products, arithmetic and copies ran while one was open for 2% of the time, Pallas kernels for 0%

commit v1 on v0

v1 whole, which is shorter than its diff:
```python
import functools
import math

import jax
import jax.numpy as jnp
from jax import lax
from jax.experimental import pallas as pl
from jax.experimental.pallas import tpu as pltpu
from jax.sharding import PartitionSpec as P

HD = 64
POOL_HEADS = 2

epsilon = 1e-06
mask_fill = -1e30
highest = lax.Precision.HIGHEST
bf16 = jnp.bfloat16
f32 = jnp.float32
SCORE_SCALE = 1.0 / math.sqrt(HD)
SCORE_SCALE_2 = math.log2(math.e) * SCORE_SCALE
PLANE = 256
VMEM_LIMIT = 60 * 1024 * 1024


def matmul(left, right):
    return jnp.dot(left, right, preferred_element_type=f32)


def across_rows(left, right):
    return lax.dot_general(left, right, (((0,), (0,)), ((), ())), preferred_element_type=f32)


def against(left, right):
    return lax.dot_general(left, right, (((1,), (1,)), ((), ())), preferred_element_type=f32)


def widen_keys(wide_ref, narrow_ref, length):
    rows, width = narrow_ref.shape
    wide_ref[:, :width] = narrow_ref[...]
    row = lax.broadcasted_iota(jnp.int32, (rows, PLANE - width), 0)
    lane = lax.broadcasted_iota(jnp.int32, (rows, PLANE - width), 1)
    wide_ref[:, width:] = jnp.where((lane == 0) & (row >= length), mask_fill, 0.0).astype(bf16)


def forward_kernel(
    bq, bk, heads, length_ref, k_ref, qt_ref, vt_ref, ot_ref, lse_ref, wide_k, head_q, acc
):
    width = k_ref.shape[1]
    length = length_ref[0]
    key_blocks = (length + bk - 1) // bk
    widen_keys(wide_k, k_ref, length)
    row = lax.broadcasted_iota(jnp.int32, (PLANE, bq), 0)
    for h in range(heads):
        head_q[h] = jnp.where(row == width, 1.0, 0.0).astype(bf16)

    def query_step(qb, unused):
        q0 = pl.multiple_of(qb * bq, bq)
        for h in range(heads):
            own = slice(HD * h, HD * h + HD)
            head_q[h, own, :] = qt_ref[own, pl.ds(q0, bq)]
        acc[...] = jnp.zeros_like(acc)

        def key_step(kb, carry):
            k0 = pl.multiple_of(kb * bk, bk)
            keys = wide_k[pl.ds(k0, bk), :]
            scores = [matmul(keys, head_q[h]) for h in range(heads)]
            kept = []
            for h in range(heads):
                top, total = carry[h]
                new_top = jnp.maximum(
                    top, jnp.max(scores[h], axis=0, keepdims=True) * SCORE_SCALE_2
                )
                weights = jnp.exp2(scores[h] * SCORE_SCALE_2 - new_top)
                fade = jnp.exp2(top - new_top)
                total = fade * total + jnp.sum(weights, axis=0, keepdims=True)
                values_t = vt_ref[HD * h : HD * h + HD, pl.ds(k0, bk)]
                acc[h] = fade * acc[h] + matmul(values_t, weights.astype(bf16))
                kept.append((new_top, total))
            return tuple(kept)

        start = tuple(
            (jnp.full((1, bq), mask_fill, f32), jnp.zeros((1, bq), f32)) for _ in range(heads)
        )
        done = lax.fori_loop(0, key_blocks, key_step, start)
        for h in range(heads):
            top, total = done[h]
            ot_ref[HD * h : HD * h + HD, pl.ds(q0, bq)] = (acc[h] * (1.0 / total)).astype(bf16)
            lse_ref[pl.ds(h, 1), pl.ds(q0, bq)] = top + jnp.log2(total)
        return unused

    lax.fori_loop(0, qt_ref.shape[1] // bq, query_step, 0)


def attend_forward(length, keys, queries_t, values_t):
    slot_len, width = keys.shape
    heads = width // HD
    query_count = queries_t.shape[1]
    bq, bk = min(512, query_count), min(2048, slot_len)
    vmem = pl.BlockSpec(memory_space=pltpu.VMEM)
    pairs = heads * query_count * slot_len
    return pl.pallas_call(
        functools.partial(forward_kernel, bq, bk, heads),
        out_shape=(
            jax.ShapeDtypeStruct((width, query_count), bf16),
            jax.ShapeDtypeStruct((8, query_count), f32),
        ),
        in_specs=[pl.BlockSpec(memory_space=pltpu.SMEM)] + [vmem] * 3,
        out_specs=[vmem] * 2,
        scratch_shapes=[
            pltpu.VMEM((slot_len, PLANE), bf16),
            pltpu.VMEM((heads, PLANE, bq), bf16),
            pltpu.VMEM((heads, HD, bq), f32),
        ],
        compiler_params=pltpu.CompilerParams(vmem_limit_bytes=VMEM_LIMIT),
        cost_estimate=pl.CostEstimate(
            flops=4 * HD * pairs * 4, bytes_accessed=slot_len * width * 8, transcendentals=pairs
        ),
        name="attend_forward",
    )(length, keys, queries_t, values_t)


def backward_kernel(
    bq,
    bk,
    heads,
    length_ref,
    k_ref,
    kt_ref,
    v_ref,
    qt_ref,
    got_ref,
    ot_ref,
    lse_ref,
    gqt_ref,
    gk_ref,
    gv_ref,
    wide_k,
    wide_v,
    head_q,
    head_go,
    gq_acc,
    gk_acc,
    gv_acc,
):
    rows, width = k_ref.shape
    length = length_ref[0]
    key_blocks = (length + bk - 1) // bk
    query_blocks = (length + bq - 1) // bq
    widen_keys(wide_k, k_ref, length)
    wide_v[:, :width] = v_ref[...]
    wide_v[:, width:] = jnp.zeros((rows, PLANE - width), bf16)
    row = lax.broadcasted_iota(jnp.int32, (PLANE, bq), 0)
    for h in range(heads):
        head_q[h] = jnp.where(row == width, 1.0, 0.0).astype(bf16)
        head_go[h] = jnp.zeros((PLANE, bq), bf16)
    gk_acc[...] = jnp.zeros_like(gk_acc)
    gv_acc[...] = jnp.zeros_like(gv_acc)
    gqt_ref[...] = jnp.zeros_like(gqt_ref)

    def query_step(qb, unused):
        q0 = pl.multiple_of(qb * bq, bq)
        span = pl.ds(q0, bq)
        deltas = []
        for h in range(heads):
            own = slice(HD * h, HD * h + HD)
            head_q[h, own, :] = qt_ref[own, span]
            grad_out = got_ref[own, span]
            head_go[h, own, :] = grad_out
            deltas.append(
                jnp.sum(
                    grad_out.astype(f32) * ot_ref[own, span].astype(f32), axis=0, keepdims=True
                )
            )
        gq_acc[...] = jnp.zeros_like(gq_acc)

        def key_step(kb, inner):
            k0 = pl.multiple_of(kb * bk, bk)
            keys = wide_k[pl.ds(k0, bk), :]
            values = wide_v[pl.ds(k0, bk), :]
            grad_v = None
            grad_k = None
            for h in range(heads):
                scores = matmul(keys, head_q[h])
                grad_weights = matmul(values, head_go[h])
                weights = jnp.exp2(scores * SCORE_SCALE_2 - lse_ref[pl.ds(h, 1), span])
                grad_scores = (weights * (grad_weights - deltas[h])).astype(bf16)
                more_v = against(weights.astype(bf16), head_go[h])
                more_k = against(grad_scores, head_q[h])
                grad_v = more_v if grad_v is None else grad_v + more_v
                grad_k = more_k if grad_k is None else grad_k + more_k
                gq_acc[h] += matmul(kt_ref[HD * h : HD * h + HD, pl.ds(k0, bk)], grad_scores)
            gk_acc[pl.ds(k0, bk), :] += grad_k
            gv_acc[pl.ds(k0, bk), :] += grad_v
            return inner

        lax.fori_loop(0, key_blocks, key_step, 0)
        for h in range(heads):
            gqt_ref[HD * h : HD * h + HD, span] = (gq_acc[h] * SCORE_SCALE).astype(bf16)
        return unused

    lax.fori_loop(0, query_blocks, query_step, 0)
    gk_ref[...] = (gk_acc[:, :width] * SCORE_SCALE).astype(bf16)
    gv_ref[...] = gv_acc[:, :width].astype(bf16)


def attend_backward(length, keys, keys_t, values, queries_t, grad_out_t, out_t, lse):
    slot_len, width = keys.shape
    heads = width // HD
    bq, bk = min(512, slot_len), min(1024, slot_len)
    vmem = pl.BlockSpec(memory_space=pltpu.VMEM)
    pairs = heads * slot_len * slot_len
    return pl.pallas_call(
        functools.partial(backward_kernel, bq, bk, heads),
        out_shape=(
            jax.ShapeDtypeStruct((width, slot_len), bf16),
            jax.ShapeDtypeStruct((slot_len, width), bf16),
            jax.ShapeDtypeStruct((slot_len, width), bf16),
        ),
        in_specs=[pl.BlockSpec(memory_space=pltpu.SMEM)] + [vmem] * 7,
        out_specs=[vmem] * 3,
        scratch_shapes=[
            pltpu.VMEM((slot_len, PLANE), bf16),
            pltpu.VMEM((slot_len, PLANE), bf16),
            pltpu.VMEM((heads, PLANE, bq), bf16),
            pltpu.VMEM((heads, PLANE, bq), bf16),
            pltpu.VMEM((heads, HD, bq), f32),
            pltpu.VMEM((slot_len, PLANE), f32),
            pltpu.VMEM((slot_len, PLANE), f32),
        ],
        compiler_params=pltpu.CompilerParams(vmem_limit_bytes=VMEM_LIMIT),
        cost_estimate=pl.CostEstimate(
            flops=10 * HD * pairs * 4, bytes_accessed=slot_len * width * 20, transcendentals=pairs
        ),
        name="attend_backward",
    )(length, keys, keys_t, values, queries_t, grad_out_t, out_t, lse)


def normalize(resid, gain, shift):
    center = resid - jnp.mean(resid, axis=-1, keepdims=True)
    invstd = lax.rsqrt(jnp.mean(center * center, axis=-1, keepdims=True) + epsilon)
    normed = center * invstd
    return (normed * gain + shift, normed, invstd)


def normalize_back(grad, normed, invstd, gain):
    scaled = grad * gain
    inner = (
        scaled
        - jnp.mean(scaled, axis=-1, keepdims=True)
        - normed * jnp.mean(scaled * normed, axis=-1, keepdims=True)
    )
    return (invstd * inner, jnp.sum(grad * normed, axis=0), jnp.sum(grad, axis=0))


def exchange(pieces, rank, group_size, shift_sign):
    arrived = [pieces[0]]
    for s in range(1, group_size):
        moves = [(i, (i + shift_sign * s) % group_size) for i in range(group_size)]
        arrived.append(lax.ppermute(pieces[s], "tensor", moves))
    return arrived


def ring_gather(own, rank, group_size):
    rows = own.shape[0]
    whole = jnp.zeros((group_size * rows,) + own.shape[1:], own.dtype)
    whole = lax.dynamic_update_slice_in_dim(whole, own, rank * rows, 0)
    moves = [(i, (i + 1) % group_size) for i in range(group_size)]
    held = own
    for s in range(1, group_size):
        held = lax.ppermute(held, "tensor", moves)
        source = (rank - s) % group_size
        whole = lax.dynamic_update_slice_in_dim(whole, held, source * rows, 0)
    return whole


def spread_gather(shard, row_unit):
    dp_size = lax.axis_size("dp")
    rows = shard.shape[0]
    unit = row_unit * dp_size
    padded = -(-rows // unit) * unit
    if padded != rows:
        shard = jnp.pad(shard, ((0, padded - rows), (0, 0)))
    part = padded // dp_size
    mine = lax.dynamic_slice_in_dim(shard, lax.axis_index("dp") * part, part, 0)
    whole = lax.all_gather(mine, ("tensor", "dp"), axis=0, tiled=True)
    return whole.reshape(lax.axis_size("tensor"), padded, shard.shape[1])


def body(
    hidden_in,
    lengths,
    labels,
    out_cotangent,
    w_query,
    b_query,
    w_key,
    w_value,
    b_value,
    w_out,
    b_out,
    ln1_gain,
    ln1_bias,
    w_in,
    b_in,
    w_down,
    b_down,
    ln2_gain,
    ln2_bias,
    w_student,
    b_student,
    pool_query,
    w_pool,
    b_pool,
    w_class,
    b_class,
):
    slot_len, model = hidden_in.shape
    group_size = lax.axis_size("tensor")
    dp_size = lax.axis_size("dp")
    own_count = slot_len // group_size
    rank = lax.axis_index("tensor")
    own_start = rank * own_count
    width = w_query.shape[1]
    hidden_width = w_in.shape[1]
    stu_cols = w_student.shape[1]
    length = lengths[0]

    early = spread_gather(jnp.concatenate([w_out, w_in, b_in[None, :]], axis=0), 16)
    w_out_all = early[:, :width].reshape(group_size * width, model)
    w_in_all = early[:, width : width + model]
    b_in_all = early[:, width + model]
    w_down_all = spread_gather(w_down, 16)[:, :hidden_width]
    stud = jnp.concatenate([w_student, b_student[None, :]], axis=0)
    stud_all = lax.all_gather(stud, "tensor", axis=1, tiled=True)
    w_stud_all = stud_all[:model]
    b_stud_all = stud_all[model:]

    hidden_own = lax.dynamic_slice_in_dim(hidden_in, own_start, own_count, 0)
    cot_own = lax.dynamic_slice_in_dim(out_cotangent, own_start, own_count, 0)
    w_project = jnp.concatenate([w_query, w_key, w_value], axis=1)
    bias_project = jnp.concatenate([b_query, jnp.zeros_like(b_query), b_value])
    projected_t = (
        lax.dot_general(w_project, hidden_in, (((0,), (1,)), ((), ())), preferred_element_type=f32)
        + bias_project[:, None]
    ).astype(bf16)
    key_value = (matmul(hidden_in, w_project[:, width:]) + bias_project[width:]).astype(bf16)
    queries_t = projected_t[:width]
    keys_t = projected_t[width : 2 * width]
    values_t = projected_t[2 * width :]
    keys = key_value[:, :width]
    values = key_value[:, width:]

    chunk_outs = [None] * group_size
    chunk_lses = [None] * group_size
    for s in list(range(1, group_size)) + [0]:
        target = (rank + s) % group_size
        query_chunk = lax.dynamic_slice_in_dim(queries_t, target * own_count, own_count, 1)
        chunk_outs[s], chunk_lses[s] = attend_forward(lengths, keys, query_chunk, values_t)
    arrived = exchange(chunk_outs, rank, group_size, 1)
    attended_t = jnp.zeros((group_size * width, own_count), bf16)
    out_t = jnp.zeros((width, slot_len), bf16)
    lse = jnp.zeros((8, slot_len), f32)
    for s in range(group_size):
        source = (rank - s) % group_size
        attended_t = lax.dynamic_update_slice_in_dim(attended_t, arrived[s], source * width, 0)
        target = (rank + s) % group_size
        out_t = lax.dynamic_update_slice_in_dim(out_t, chunk_outs[s], target * own_count, 1)
        lse = lax.dynamic_update_slice_in_dim(lse, chunk_lses[s], target * own_count, 1)

    resid1 = across_rows(attended_t, w_out_all) + b_out + hidden_own.astype(f32)
    first, normed1, invstd1 = normalize(resid1, ln1_gain, ln1_bias)
    first_low = first.astype(bf16)
    acts = []
    slopes = []
    ffn = None
    for b in range(group_size):
        pre = matmul(first_low, w_in_all[b]) + b_in_all[b].astype(f32)
        below = 0.5 * (1.0 + lax.erf(pre * math.sqrt(0.5)))
        density = jnp.exp(-0.5 * pre * pre) * (1.0 / math.sqrt(2.0 * math.pi))
        acts.append((pre * below).astype(bf16))
        slopes.append((below + pre * density).astype(bf16))
        more = matmul(acts[b], w_down_all[b])
        ffn = more if ffn is None else ffn + more
    resid2 = ffn + b_down + first_low.astype(f32)
    second, normed2, invstd2 = normalize(resid2, ln2_gain, ln2_bias)
    second_low = second.astype(bf16)
    hidden_out = ring_gather(second_low, rank, group_size)

    student_low = (matmul(second_low, w_stud_all) + b_stud_all.astype(f32)).astype(bf16)
    student = student_low.astype(f32)
    student_width = student.shape[1]
    head_width = student_width // POOL_HEADS
    probe_scale = 1.0 / math.sqrt(head_width)
    own_rows = own_start + lax.broadcasted_iota(jnp.int32, (own_count, 1), 0)
    row_valid = own_rows < length
    head_of = lax.broadcasted_iota(jnp.int32, (1, student_width), 1) // head_width

    def per_head(values_wide):
        whole = jnp.zeros_like(values_wide)
        for h in range(POOL_HEADS):
            part = jnp.sum(
                jnp.where(head_of == h, values_wide, 0.0), axis=-1, keepdims=True
            )
            whole = jnp.where(head_of == h, part, whole)
        return whole

    probes = pool_query[None, :]
    energies = jnp.where(row_valid, per_head(student * probes) * probe_scale, mask_fill)
    local_top = jnp.max(energies, axis=0, keepdims=True)
    local_weights = jnp.exp(energies - local_top)
    local_total = jnp.sum(local_weights, axis=0, keepdims=True)
    local_pooled = jnp.sum(local_weights * student, axis=0, keepdims=True)
    stats = jnp.concatenate(
        [local_top, local_total, local_pooled, jnp.zeros((5, student_width), f32)], axis=0
    )
    stats_all = lax.all_gather(stats[None], "tensor", axis=0, tiled=True)
    top = jnp.max(stats_all[:, 0], axis=0, keepdims=True)
    fade = jnp.exp(stats_all[:, 0] - top)
    inv_total = 1.0 / jnp.sum(fade * stats_all[:, 1], axis=0, keepdims=True)
    pooled = jnp.sum(fade * stats_all[:, 2], axis=0, keepdims=True) * inv_total
    squashed = jnp.tanh(jnp.dot(pooled, w_pool, precision=highest) + b_pool)
    logits = jnp.dot(squashed, w_class, precision=highest) + b_class
    classes = lax.broadcasted_iota(jnp.int32, logits.shape, 1)
    g_logits = jax.nn.softmax(logits, axis=-1) - (classes == labels[:, None]).astype(f32)
    grad_w_class = squashed.reshape(-1, 1) * g_logits
    grad_b_class = g_logits[0]
    g_u = lax.dot_general(
        g_logits, w_class, (((1,), (1,)), ((), ())), precision=highest
    ) * (1.0 - squashed * squashed)
    grad_w_pool = pooled.reshape(-1, 1) * g_u
    grad_b_pool = g_u[0]
    g_pooled = lax.dot_general(g_u, w_pool, (((1,), (1,)), ((), ())), precision=highest)
    inner = per_head(pooled * g_pooled)
    pool = jnp.exp(energies - top) * inv_total
    g_energy = pool * (per_head(student * g_pooled) - inner)
    g_stud_low = (pool * g_pooled + g_energy * probes * probe_scale).astype(bf16)
    grad_pool_query = jnp.sum(g_energy * student, axis=0) * probe_scale

    grad_second = jnp.where(row_valid, cot_own.astype(f32), 0.0) + against(g_stud_low, w_stud_all)
    grad_stud_weight = across_rows(second_low, g_stud_low)
    grad_stud_bias = jnp.sum(g_stud_low, axis=0, dtype=f32)
    grad_resid2, grad_ln2_gain, grad_ln2_bias = normalize_back(
        grad_second, normed2, invstd2, ln2_gain
    )
    grad_b_down = jnp.sum(grad_resid2, axis=0)
    grad_ffn_low = grad_resid2.astype(bf16)
    grad_first = grad_resid2
    grad_w_in = []
    grad_w_down = []
    grad_b_in = []
    for b in range(group_size):
        grad_pre = (against(grad_ffn_low, w_down_all[b]) * slopes[b].astype(f32)).astype(bf16)
        grad_w_down.append(across_rows(acts[b], grad_ffn_low).astype(bf16))
        grad_w_in.append(across_rows(first_low, grad_pre).astype(bf16))
        grad_b_in.append(jnp.sum(grad_pre, axis=0, dtype=f32))
        grad_first = grad_first + against(grad_pre, w_in_all[b])
    grad_resid1, grad_ln1_gain, grad_ln1_bias = normalize_back(
        grad_first, normed1, invstd1, ln1_gain
    )
    grad_b_out = jnp.sum(grad_resid1, axis=0)
    grad_mix = grad_resid1.astype(bf16)
    grad_att_t = against(w_out_all, grad_mix).astype(bf16)
    grad_pieces = [
        lax.dynamic_slice_in_dim(grad_att_t, ((rank + s) % group_size) * width, width, 0)
        for s in range(group_size)
    ]
    grad_arrived = exchange(grad_pieces, rank, group_size, 1)
    grad_out_t = jnp.zeros((width, slot_len), bf16)
    for s in range(group_size):
        source = (rank - s) % group_size
        grad_out_t = lax.dynamic_update_slice_in_dim(
            grad_out_t, grad_arrived[s], source * own_count, 1
        )
    grad_w_out = matmul(attended_t, grad_mix).astype(bf16)

    blocks = jnp.stack(
        [
            jnp.concatenate(
                [grad_w_in[b], grad_w_down[b], grad_w_out[b * width : (b + 1) * width]], axis=0
            )
            for b in range(group_size)
        ],
        axis=0,
    )
    block_rows = blocks.shape[1]
    part_rows = -(-block_rows // (8 * dp_size)) * 8
    if part_rows * dp_size != block_rows:
        blocks = jnp.pad(blocks, ((0, 0), (0, part_rows * dp_size - block_rows), (0, 0)))
    blocks = blocks.reshape(group_size, dp_size, part_rows, model).transpose(1, 0, 2, 3)
    reduced = lax.psum_scatter(
        blocks.reshape(dp_size * group_size, part_rows, model),
        "dp",
        scatter_dimension=0,
        tiled=True,
    )
    reduced = lax.psum_scatter(reduced, "tensor", scatter_dimension=0, tiled=True)
    reduced = lax.all_gather(reduced[0], "dp", axis=0, tiled=True)

    only_once = (rank == 0).astype(f32)
    small = lax.psum(
        (
            jnp.stack(grad_b_in),
            grad_pool_query,
            grad_w_pool * only_once,
            grad_b_pool * only_once,
            grad_w_class * only_once,
            grad_b_class * only_once,
            grad_b_out,
            grad_ln1_gain,
            grad_ln1_bias,
            grad_b_down,
            grad_ln2_gain,
            grad_ln2_bias,
            grad_stud_weight,
            grad_stud_bias,
        ),
        ("dp", "tensor"),
    )

    grad_q_t, grad_k, grad_v = attend_backward(
        lengths, keys, keys_t, values, queries_t, grad_out_t, out_t, lse
    )
    grad_kv = jnp.concatenate([grad_k, grad_v], axis=1)
    partial_in = (
        lax.dot_general(grad_q_t, w_query, (((0,), (1,)), ((), ())), preferred_element_type=f32)
        + against(grad_kv, w_project[:, width:])
    ).astype(bf16)
    grad_in_own = (
        lax.psum_scatter(partial_in, "tensor", scatter_dimension=0, tiled=True).astype(f32)
        + grad_resid1
    )
    grad_in = ring_gather(grad_in_own.astype(bf16), rank, group_size)
    grad_w_query = lax.dot_general(
        hidden_in, grad_q_t, (((0,), (1,)), ((), ())), preferred_element_type=f32
    )
    grad_w_kv = across_rows(hidden_in, grad_kv)
    late = lax.psum(
        (
            grad_w_query,
            grad_w_kv,
            jnp.sum(grad_q_t, axis=1, dtype=f32),
            jnp.sum(grad_v, axis=0, dtype=f32),
        ),
        "dp",
    )
    grad_w_student = lax.dynamic_slice_in_dim(small[12], rank * stu_cols, stu_cols, 1)
    grad_b_student = lax.dynamic_slice_in_dim(small[13], rank * stu_cols, stu_cols, 0)
    grad_b_in_own = lax.dynamic_index_in_dim(small[0], rank, 0, keepdims=False)
    return (
        hidden_out,
        logits,
        grad_in,
        late[0],
        late[2],
        late[1][:, :width],
        late[1][:, width:],
        late[3],
        reduced[model + hidden_width : model + hidden_width + width].astype(f32),
        small[6],
        small[7],
        small[8],
        reduced[:model].astype(f32),
        grad_b_in_own,
        reduced[model : model + hidden_width].astype(f32),
        small[9],
        small[10],
        small[11],
        grad_w_student,
        grad_b_student,
        small[1],
        small[2],
        small[3],
        small[4],
        small[5],
    )


def solution(mesh):
    by_dp = P("dp", None)
    cols = P(None, "tensor")
    rows = P("tensor", None)
    cut = P("tensor")
    in_specs = (
        (by_dp, P("dp"), P("dp"), by_dp, cols, cut, cols, cols, cut, rows, P(), P(), P(), cols)
        + (cut, rows, P(), P(), P(), cols, cut, P(), P(), P(), P(), P())
    )
    out_specs = (
        (by_dp, by_dp, by_dp, cols, cut, cols, cols, cut, rows, P(), P(), P(), cols, cut, rows)
        + (P(), P(), P(), cols, cut, P(), P(), P(), P(), P())
    )
    return jax.shard_map(body, mesh=mesh, in_specs=in_specs, out_specs=out_specs, check_vma=False)
```

time: 2490 us -> 983 us (0.39)
  waiting for transfers between devices: 1270 us -> 334 us
  matrix products: 750 us -> 117 us
  other arithmetic: 274 us -> 33.5 us
  Pallas kernels: 0 us -> 208 us
  blocking collectives: 92.9 us -> 159 us
    dot_general x69 -> x18, matrix products: 681 us -> 52.7 us  [the longest x11 36.4 us: matmul(): return jnp.dot(left, right, preferred_element_type=f32)]
    all_gather x6 -> x3, waiting for transfers between devices: 534 us -> 5.18 us  [the longest x1 5.18 us: body(): reduced = lax.all_gather(reduced[0], 'dp', axis=0, tiled=True)]
    reduce_scatter x4 -> x3, waiting for transfers between devices: 516 us -> 185 us  [the longest x1 122 us: body(): lax.psum_scatter(partial_in, 'tensor', scatter_dimension=0, tiled=True)]
    pallas_call x0 -> x5, Pallas kernels: none -> 208 us  [the longest x1 121 us: attend_backward(): pl.pallas_call(functools.partial(backward_kernel, bq, bk, heads), out_sha...]
    convert_element_type x15 -> x7, other arithmetic: 184 us -> 13.1 us  [the longest x1 4.23 us: body(): reduced[model:model + hidden_width].astype(f32)]
    psum x2, waiting for transfers between devices: 217 us -> 98.7 us  [the longest x1 54.3 us: body(): lax.psum((jnp.stack(grad_b_in), grad_pool_query, grad_w_pool * only_once,...]
    psum x2, blocking collectives: 68.4 us -> 127 us  [the longest x1 114 us: body(): lax.psum((jnp.stack(grad_b_in), grad_pool_query, grad_w_pool * only_once,...]
    reduce_sum x16 -> x8, other arithmetic: 63.5 us -> 9.4 us  [the longest x1 1.73 us: body(): grad_b_down = jnp.sum(grad_resid2, axis=0)]
  transfers between devices with their start and end apart: 12 -> 20, of which waited for: 12 -> 8; matrix products, arithmetic and copies ran while one was open for 2% -> 14% of each run, Pallas kernels for 0% -> 21%
where the time goes in v1:
time: 983 us; the launch traced here: 976 us
  waiting for transfers between devices  334 us (34%)
  Pallas kernels  208 us (21%)
  blocking collectives  159 us (16%)
  matrix products  117 us (12%)
  local copies, waits for them, and re-layouts  86.4 us (9%)
  other arithmetic  33.5 us (3%)
  starting transfers between devices  19.2 us (2%)
  between operations  17.7 us (2%)
    reduce_scatter x1, waiting for transfers between devices, body(): lax.psum_scatter(partial_in, 'tensor', scatter_dimension=0, tiled=True)  122 us
    pallas_call x1, Pallas kernels, attend_backward(): pl.pallas_call(functools.partial(backward_kernel, bq, bk, heads), out_sha...  121 us
    psum x1, blocking collectives, body(): lax.psum((jnp.stack(grad_b_in), grad_pool_query, grad_w_pool * only_once,...  114 us
    pallas_call x4, Pallas kernels, attend_forward(): pl.pallas_call(functools.partial(forward_kernel, bq, bk, heads), out_shap...  87 us
    reduce_scatter x1, waiting for transfers between devices, body(): lax.psum_scatter(reduced, 'tensor', scatter_dimension=0, tiled=True)  62.3 us
    psum x1, waiting for transfers between devices, body(): lax.psum((jnp.stack(grad_b_in), grad_pool_query, grad_w_pool * only_once,...  54.3 us
    psum x1, waiting for transfers between devices, body(): lax.psum((grad_w_query, grad_w_kv, jnp.sum(grad_q_t, axis=1, dtype=f32),...  44.5 us
    dot_general x11, matrix products, against(): lax.dot_general(left, right, (((1,), (1,)), ((), ())), preferred_element_...  38.3 us
  transfers between devices with their start and end apart: 20, of which 8 were waited for; matrix products, arithmetic and copies ran while one was open for 14% of the time, Pallas kernels for 21%

profile of v1, /device:TPU:0, one launch (start us, length us, event | category | flops | bytes accessed | tf_op | source)
XLA Modules:
  0.0 975.7 jit_solution(1421961117296596519)
XLA Ops:
  14.1 6.9 fusion
  24.3 4.1 add_convert_fusion.1
  31.6 21.5 %attend_forward.7 = (bf16[192,1024]{1,0:T(8,128)(2,1)}, f32[8,1024]{1,0:T(8,128)}) custom-call(s32[1]{0:T(128)} %copy.198.length_ref, bf16[4096,192]{1,0:T(8,128)(2,1)} %get-tuple-element.101.k_ref, bf16[192,1024]{1,0:T(8,128)(2,1)} %get-tuple-element.108.qt_ref, bf16[192,4096]{1,0:T(8,128)(2,1)} %get-tuple-element.98.vt_ref), custom_call_target="tpu_custom_call" | custom-call | flops 12884901888 | bytes 6291456 | tf_op jit(solution)/shard_map/attend_forward/pallas_call | solution.py:101
  53.2 5.5 collective-permute-start.2
  58.7 22.2 %attend_forward.6 = (bf16[192,1024]{1,0:T(8,128)(2,1)}, f32[8,1024]{1,0:T(8,128)}) custom-call(s32[1]{0:T(128)} %copy.198.length_ref, bf16[4096,192]{1,0:T(8,128)(2,1)} %get-tuple-element.101.k_ref, bf16[192,1024]{1,0:T(8,128)(2,1)} %get-tuple-element.109.qt_ref, bf16[192,4096]{1,0:T(8,128)(2,1)} %get-tuple-element.98.vt_ref), custom_call_target="tpu_custom_call" | custom-call | flops 12884901888 | bytes 6291456 | tf_op jit(solution)/shard_map/attend_forward/pallas_call | solution.py:101
  80.9 21.6 %attend_forward.5 = (bf16[192,1024]{1,0:T(8,128)(2,1)}, f32[8,1024]{1,0:T(8,128)}) custom-call(s32[1]{0:T(128)} %copy.198.length_ref, bf16[4096,192]{1,0:T(8,128)(2,1)} %get-tuple-element.101.k_ref, bf16[192,1024]{1,0:T(8,128)(2,1)} %get-tuple-element.110.qt_ref, bf16[192,4096]{1,0:T(8,128)(2,1)} %get-tuple-element.98.vt_ref), custom_call_target="tpu_custom_call" | custom-call | flops 12884901888 | bytes 6291456 | tf_op jit(solution)/shard_map/attend_forward/pallas_call | solution.py:101
  103.0 18.3 %all_gather.17 = bf16[769,128]{0,1:T(8,128)(2,1)S(1)} all-gather(bf16[769,32]{0,1:T(8,128)(2,1)S(1)} %pad_maximum_fusion.9), channel_id=1, replica_groups=mesh['dp'=8,'tensor'=4] {'tensor'}, dimensions={1}, use_global_device_ids=true | all-gather | bytes 246080 | tf_op jit(solution)/shard_map/all_gather | solution.py:334
  124.4 21.7 %attend_forward.4 = (bf16[192,1024]{1,0:T(8,128)(2,1)}, f32[8,1024]{1,0:T(8,128)}) custom-call(s32[1]{0:T(128)} %copy.198.length_ref, bf16[4096,192]{1,0:T(8,128)(2,1)} %get-tuple-element.101.k_ref, bf16[192,1024]{1,0:T(8,128)(2,1)} %get-tuple-element.111.qt_ref, bf16[192,4096]{1,0:T(8,128)(2,1)} %get-tuple-element.98.vt_ref), custom_call_target="tpu_custom_call" | custom-call | flops 12884901888 | bytes 6291456 | tf_op jit(solution)/shard_map/attend_forward/pallas_call | solution.py:101
  173.4 3.7 multiply_convert_fusion.6
  177.1 4.0 multiply_convert_fusion.7
  198.5 13.1 %all-gather = f32[32,128]{1,0:T(8,128)S(1)} all-gather(f32[8,128]{1,0:T(8,128)S(1)} %maximum_maximum_fusion), channel_id=2, replica_groups=mesh['dp'=8,'tensor'=4] {'tensor'}, dimensions={0}, use_global_device_ids=true | all-gather | bytes 20480 | tf_op jit(solution)/shard_map/all_gather | solution.py:416
  219.8 5.0 multiply_reduce_fusion
  249.1 5.1 convert_reduce_fusion.2
  257.1 4.2 convert_reduce_fusion.1
  262.7 4.6 multiply_reduce_fusion.1
  269.0 4.0 convolution_convert_fusion.7
  275.3 4.8 copy.152
  298.0 8.3 collective-permute-done.7
  309.5 121.2 %attend_backward.1 = (bf16[192,4096]{1,0:T(8,128)(2,1)}, bf16[4096,192]{1,0:T(8,128)(2,1)}, bf16[4096,192]{1,0:T(8,128)(2,1)}) custom-call(s32[1]{0:T(128)} %copy.198.length_ref, bf16[4096,192]{1,0:T(8,128)(2,1)} %get-tuple-element.101.k_ref, bf16[192,4096]{1,0:T(8,128)(2,1)} %get-tuple-element.97.kt_ref, bf16[4096,192]{1,0:T(8,128)(2,1)} %get-tuple-element.100.v_ref, ...), custom_call_target="tpu_custom_call" | custom-call | flops 128849018880 | bytes 15728640 | tf_op jit(solution)/shard_map/attend_backward/pallas_call | solution.py:212
  430.8 5.7 fusion.22
  436.5 4.7 add_convert_fusion
  446.2 7.3 fusion.23
  453.5 5.1 convolution_bitcast_fusion
  461.8 122.2 %reduce-scatter.4.cloned.1.call-done = bf16[1024,768]{0,1:T(8,128)(2,1)} async-done(((bf16[4096,768]{0,1:T(8,128)(2,1)}), bf16[1024,768]{0,1:T(8,128)(2,1)}) %reduce-scatter.4.cloned.1.call-update) | async-done | bytes 1572880 | tf_op jit(solution)/shard_map/reduce_scatter | solution.py:529
  587.8 62.3 %reduce-scatter.8.cloned.1.call-done = bf16[1,216,768]{2,1,0:T(8,128)(2,1)} async-done(((bf16[4,216,768]{2,1,0:T(8,128)(2,1)}), bf16[1,216,768]{2,1,0:T(8,128)(2,1)}) %reduce-scatter.8.cloned.1.call-update) | async-done | bytes 331792 | tf_op jit(solution)/shard_map/reduce_scatter | solution.py:496
  656.3 34.0 %collective-permute-done.4 = bf16[1024,768]{0,1:T(8,128)(2,1)} collective-permute-done((bf16[1024,768]{0,1:T(8,128)(2,1)}, bf16[1024,768]{0,1:T(8,128)(2,1)}, u32[]{:S(2)}, u32[]{:S(2)}) %collective-permute-start.4) | collective-permute-done | bytes 1572896 | tf_op jit(solution)/shard_map/ppermute | solution.py:270
  690.4 113.8 %all-reduce.2 = (f32[768]{0:T(1024)}, f32[768]{0:T(1024)}, f32[768]{0:T(1024)}, f32[4,768]{1,0:T(4,128)S(1)}, f32[768]{0:T(1024)}, /*index=5*/f32[768]{0:T(1024)...) all-reduce(f32[768]{0:T(1024)S(1)} %copy-done.53, ...), channel_id=1, replica_groups=mesh['dp'=8,'tensor'=4] {'dp','tensor'}, use_global_device_ids=true, to_apply=%region_32.33 | all-reduce | flops 9870 | bytes 78960 | tf_op jit(solution)/shard_map/psum | solution.py:500
  809.8 54.3 %all-reduce.9.cloned.1.call-done = (f32[768,128]{0,1:T(8,128)}, f32[128,128]{1,0:T(8,128)}) async-done(((f32[768,128]{0,1:T(8,128)}, f32[128,128]{1,0:T(8,128)}), (f32[768,128]{0,1:T(8,128)}, f32[128,128]{1,0:T(8,128)})) %all-reduce.9.cloned.1.call-update) | async-done | bytes 458768 | tf_op jit(solution)/shard_map/psum | solution.py:500
  871.2 13.7 %all-reduce.4 = (f32[192]{0:T(256)}, f32[192]{0:T(256)}) all-reduce(f32[192]{0:T(256)S(1)} %convert_reduce_fusion.5, f32[192]{0:T(256)S(1)} %convert_reduce_fusion), channel_id=1, replica_groups=mesh['dp'=8,'tensor'=4] {'dp'}, use_global_device_ids=true, to_apply=%region_25.26 | all-reduce | flops 384 | bytes 3072 | tf_op jit(solution)/shard_map/psum | solution.py:537
  884.9 44.5 %all-reduce.11.cloned.1.call-done = (f32[768,192]{0,1:T(8,128)}, f32[768,384]{0,1:T(8,128)}) async-done(((f32[768,192]{0,1:T(8,128)}, f32[768,384]{0,1:T(8,128)}), (f32[768,192]{0,1:T(8,128)}, f32[768,384]{0,1:T(8,128)})) %all-reduce.11.cloned.1.call-update) | async-done | bytes 1769488 | tf_op jit(solution)/shard_map/psum | solution.py:537
  955.6 5.2 all-gather.10.cloned.1.call-done
  962.7 4.2 fusion.26
  (405 shorter events, 181.3 us)
Async XLA Ops:
  7.2 151.6 %all-gather.6.cloned.1.call-start = ((), (), s32[]{:S(2)}) async-start(), calls=%async_computation.3 | async-start | bytes 6488064 | tf_op jit(solution)/shard_map/all_gather | solution.py:285
  10.0 171.1 %all-gather.8.cloned.1.call-start = ((), (), s32[]{:S(2)}) async-start(), calls=%async_computation.4 | async-start | bytes 4866048 | tf_op jit(solution)/shard_map/all_gather | solution.py:285
  10.7 430.7 %reduce-scatter.6.cloned.1.call-start = ((), (), s32[]{:S(2)}) async-start(), calls=%async_computation.6 | async-start | bytes 11943936 | tf_op jit(solution)/shard_map/reduce_scatter | solution.py:490
  53.2 104.9 %collective-permute-start.2 = (bf16[192,1024]{1,0:T(8,128)(2,1)}, bf16[192,1024]{1,0:T(8,128)(2,1)S(1)}, u32[]{:S(2)}, u32[]{:S(2)}) collective-permute-start(bf16[192,1024]{1,0:T(8,128)(2,1)} %get-tuple-element.39), channel_id=1, source_target_pairs={{0,3},{1,0},{2,1},{3,2},{4,7},{5,4},{6,5},{7,6},{8,11},{9,8},{10,9... | collective-permute-start | bytes 1179656 | tf_op jit(solution)/shard_map/ppermute | solution.py:259
  80.9 75.4 %collective-permute-start.1 = (bf16[192,1024]{1,0:T(8,128)(2,1)}, bf16[192,1024]{1,0:T(8,128)(2,1)}, u32[]{:S(2)}, u32[]{:S(2)}) collective-permute-start(bf16[192,1024]{1,0:T(8,128)(2,1)} %get-tuple-element.38), channel_id=1, source_target_pairs={{0,2},{1,3},{2,0},{3,1},{4,6},{5,7},{6,4},{7,5},{8,10},{9,11},{10,... | collective-permute-start | bytes 1179656 | tf_op jit(solution)/shard_map/ppermute | solution.py:259
  102.5 52.0 %collective-permute-start = (bf16[192,1024]{1,0:T(8,128)(2,1)}, bf16[192,1024]{1,0:T(8,128)(2,1)}, u32[]{:S(2)}, u32[]{:S(2)}) collective-permute-start(bf16[192,1024]{1,0:T(8,128)(2,1)} %get-tuple-element.37), channel_id=1, source_target_pairs={{0,1},{1,2},{2,3},{3,0},{4,5},{5,6},{6,7},{7,4},{8,9},{9,10},{10,1... | collective-permute-start | bytes 1179656 | tf_op jit(solution)/shard_map/ppermute | solution.py:259
  280.0 303.9 %reduce-scatter.4.cloned.1.call-start = ((), (), s32[]{:S(2)}) async-start(), calls=%async_computation.5 | async-start | bytes 7864320 | tf_op jit(solution)/shard_map/reduce_scatter | solution.py:529
  288.1 9.8 %collective-permute-start.6 = (bf16[192,1024]{1,0:T(8,128)(2,1)S(1)}, bf16[192,1024]{1,0:T(8,128)(2,1)S(1)}, u32[]{:S(2)}, u32[]{:S(2)}) collective-permute-start(bf16[192,1024]{1,0:T(8,128)(2,1)S(1)} %get-tuple-element.106), channel_id=1, source_target_pairs={{0,1},{1,2},{2,3},{3,0},{4,5},{5,6},{6,7},{7,4},{8,9},{9,10},{10,1... | collective-permute-start | bytes 1179656 | tf_op jit(solution)/shard_map/ppermute | solution.py:259
  289.1 17.2 %collective-permute-start.7 = (bf16[192,1024]{1,0:T(8,128)(2,1)S(1)}, bf16[192,1024]{1,0:T(8,128)(2,1)}, u32[]{:S(2)}, u32[]{:S(2)}) collective-permute-start(bf16[192,1024]{1,0:T(8,128)(2,1)S(1)} %get-tuple-element.105), channel_id=1, source_target_pairs={{0,2},{1,3},{2,0},{3,1},{4,6},{5,7},{6,4},{7,5},{8,10},{9,11},{10,... | collective-permute-start | bytes 1179656 | tf_op jit(solution)/shard_map/ppermute | solution.py:259
  290.4 17.0 %collective-permute-start.8 = (bf16[192,1024]{1,0:T(8,128)(2,1)S(1)}, bf16[192,1024]{1,0:T(8,128)(2,1)}, u32[]{:S(2)}, u32[]{:S(2)}) collective-permute-start(bf16[192,1024]{1,0:T(8,128)(2,1)S(1)} %get-tuple-element.104), channel_id=1, source_target_pairs={{0,3},{1,0},{2,1},{3,2},{4,7},{5,4},{6,5},{7,6},{8,11},{9,8},{10,9... | collective-permute-start | bytes 1179656 | tf_op jit(solution)/shard_map/ppermute | solution.py:259
  309.5 121.2 %copy-start.20 = (bf16[768,384]{0,1:T(8,128)(2,1)S(1)}, bf16[768,384]{0,1:T(8,128)(2,1)}, u32[]{:S(2)}) copy-start(bf16[768,384]{0,1:T(8,128)(2,1)} %copy-done.19) | copy-start | bytes 1769476
  441.4 208.8 %reduce-scatter.8.cloned.1.call-start = ((), (), s32[]{:S(2)}) async-start(), calls=%async_computation.7 | async-start | bytes 1658880 | tf_op jit(solution)/shard_map/reduce_scatter | solution.py:496
  441.9 422.1 %all-reduce.9.cloned.1.call-start = ((), (), s32[]{:S(2)}) async-start(), calls=%async_computation.9 | async-start | bytes 917504 | tf_op jit(solution)/shard_map/psum | solution.py:500
  445.8 483.5 %all-reduce.11.cloned.1.call-start = ((), (), s32[]{:S(2)}) async-start(), calls=%async_computation.10 | async-start | bytes 3538944 | tf_op jit(solution)/shard_map/psum | solution.py:537
  453.5 130.5 %copy-start.6 = (f32[1024,768]{0,1:T(8,128)S(1)}, f32[1024,768]{0,1:T(8,128)}, u32[]{:S(2)}) copy-start(f32[1024,768]{0,1:T(8,128)} %copy-done.4) | copy-start | bytes 9437188
  458.6 502.1 %all-gather.10.cloned.1.call-start = ((), (), s32[]{:S(2)}) async-start(), calls=%async_computation.8 | async-start | bytes 2985984 | tf_op jit(solution)/shard_map/all_gather | solution.py:497
  458.7 191.5 %collective-permute-start.3 = (bf16[1024,768]{0,1:T(8,128)(2,1)}, bf16[1024,768]{0,1:T(8,128)(2,1)}, u32[]{:S(2)}, u32[]{:S(2)}) collective-permute-start(bf16[1024,768]{0,1:T(8,128)(2,1)} %add_convert_fusion.4), channel_id=1, source_target_pairs={{0,1},{1,2},{2,3},{3,0},{4,5},{5,6},{6,7},{7,4},{8,9},{9,10},{10,1... | collective-permute-start | bytes 4718600 | tf_op jit(solution)/shard_map/ppermute | solution.py:270
  587.1 103.2 %copy-start.63 = (f32[128]{0:T(128)S(1)}, f32[128]{0:T(128)}, u32[]{:S(2)}) copy-start(f32[128]{0:T(128)} %copy-done.62) | copy-start | bytes 1540
  587.1 103.2 %copy-start.71 = (f32[14]{0:T(128)S(1)}, f32[14]{0:T(128)}, u32[]{:S(2)}) copy-start(f32[14]{0:T(128)} %copy-done.70) | copy-start | bytes 172
  587.1 103.3 %copy-start.50 = (f32[768]{0:T(1024)S(1)}, f32[768]{0:T(1024)}, u32[]{:S(2)}) copy-start(f32[768]{0:T(1024)} %get-tuple-element.91) | copy-start | bytes 9220
  587.1 103.3 %copy-start.51 = (f32[768]{0:T(1024)S(1)}, f32[768]{0:T(1024)}, u32[]{:S(2)}) copy-start(f32[768]{0:T(1024)} %get-tuple-element.49) | copy-start | bytes 9220
  587.1 103.2 %copy-start.52 = (f32[768]{0:T(1024)S(1)}, f32[768]{0:T(1024)}, u32[]{:S(2)}) copy-start(f32[768]{0:T(1024)} %get-tuple-element.58) | copy-start | bytes 9220
  587.1 103.2 %copy-start.53 = (f32[768]{0:T(1024)S(1)}, f32[768]{0:T(1024)}, u32[]{:S(2)}) copy-start(f32[768]{0:T(1024)} %get-tuple-element.93) | copy-start | bytes 9220
  587.1 103.2 %copy-start.75 = (f32[768]{0:T(1024)S(1)}, f32[768]{0:T(1024)}, u32[]{:S(2)}) copy-start(f32[768]{0:T(1024)} %get-tuple-element.47) | copy-start | bytes 9220
  587.2 103.2 %copy-start.76 = (f32[768]{0:T(1024)S(1)}, f32[768]{0:T(1024)}, u32[]{:S(2)}) copy-start(f32[768]{0:T(1024)} %get-tuple-element.57) | copy-start | bytes 9220
  587.2 103.2 %copy-start.82 = (f32[14]{0:T(128)S(1)}, f32[14]{0:T(128)}, u32[]{:S(2)}) copy-start(f32[14]{0:T(128)} %get-tuple-element.89) | copy-start | bytes 172
  587.2 103.2 %copy-start.85 = (f32[128]{0:T(128)S(1)}, f32[128]{0:T(128)}, u32[]{:S(2)}) copy-start(f32[128]{0:T(128)} %get-tuple-element.147) | copy-start | bytes 1540
  587.2 63.1 %collective-permute-start.9 = (bf16[1024,768]{0,1:T(8,128)(2,1)}, bf16[1024,768]{0,1:T(8,128)(2,1)}, u32[]{:S(2)}, u32[]{:S(2)}) collective-permute-start(bf16[1024,768]{0,1:T(8,128)(2,1)} %add_convert_fusion.3), channel_id=1, source_target_pairs={{0,1},{1,2},{2,3},{3,0},{4,5},{5,6},{6,7},{7,4},{8,9},{9,10},{10,1... | collective-permute-start | bytes 4718600 | tf_op jit(solution)/shard_map/ppermute | solution.py:270
  650.2 40.0 %collective-permute-start.4 = (bf16[1024,768]{0,1:T(8,128)(2,1)}, bf16[1024,768]{0,1:T(8,128)(2,1)}, u32[]{:S(2)}, u32[]{:S(2)}) collective-permute-start(bf16[1024,768]{0,1:T(8,128)(2,1)} %collective-permute-done.3), channel_id=1, source_target_pairs={{0,1},{1,2},{2,3},{3,0},{4,5},{5,6},{6,7},{7,4},{8,9},{9,10},{10,1... | collective-permute-start | bytes 4718600 | tf_op jit(solution)/shard_map/ppermute | solution.py:270
  650.3 215.3 %collective-permute-start.10 = (bf16[1024,768]{0,1:T(8,128)(2,1)}, bf16[1024,768]{0,1:T(8,128)(2,1)}, u32[]{:S(2)}, u32[]{:S(2)}) collective-permute-start(bf16[1024,768]{0,1:T(8,128)(2,1)} %collective-permute-done.9), channel_id=1, source_target_pairs={{0,1},{1,2},{2,3},{3,0},{4,5},{5,6},{6,7},{7,4},{8,9},{9,10},{10,1... | collective-permute-start | bytes 4718600 | tf_op jit(solution)/shard_map/ppermute | solution.py:270
  690.2 247.4 %collective-permute-start.5 = (bf16[1024,768]{0,1:T(8,128)(2,1)}, bf16[1024,768]{0,1:T(8,128)(2,1)}, u32[]{:S(2)}, u32[]{:S(2)}) collective-permute-start(bf16[1024,768]{0,1:T(8,128)(2,1)} %collective-permute-done.4), channel_id=1, source_target_pairs={{0,1},{1,2},{2,3},{3,0},{4,5},{5,6},{6,7},{7,4},{8,9},{9,10},{10,1... | collective-permute-start | bytes 4718600 | tf_op jit(solution)/shard_map/ppermute | solution.py:270
  865.6 87.0 %collective-permute-start.11 = (bf16[1024,768]{0,1:T(8,128)(2,1)}, bf16[1024,768]{0,1:T(8,128)(2,1)}, u32[]{:S(2)}, u32[]{:S(2)}) collective-permute-start(bf16[1024,768]{0,1:T(8,128)(2,1)} %collective-permute-done.10), channel_id=1, source_target_pairs={{0,1},{1,2},{2,3},{3,0},{4,5},{5,6},{6,7},{7,4},{8,9},{9,10},{10,1... | collective-permute-start | bytes 4718600 | tf_op jit(solution)/shard_map/ppermute | solution.py:270
  (99 other events, 1110.0 us)
Sparse Core Ops, SparseCore 0:
  10.9 90.2 all-gather.5
  104.1 62.8 all-gather.7
  280.2 85.5 reduce-scatter.5
  441.5 142.4 reduce-scatter.3
  586.1 64.0 reduce-scatter.7
  656.5 207.4 all-reduce.8
  868.3 60.9 all-reduce.10
  931.2 29.4 all-gather.9

commit v2 on v1

v2 whole, which is shorter than its diff:
```python
import functools
import math

import jax
import jax.numpy as jnp
from jax import lax
from jax.experimental import pallas as pl
from jax.experimental.pallas import tpu as pltpu
from jax.sharding import PartitionSpec as P

HD = 64
POOL_HEADS = 2

epsilon = 1e-06
mask_fill = -1e30
highest = lax.Precision.HIGHEST
bf16 = jnp.bfloat16
f32 = jnp.float32
SCORE_SCALE = 1.0 / math.sqrt(HD)
SCORE_SCALE_2 = math.log2(math.e) * SCORE_SCALE
PLANE = 256
VMEM_LIMIT = 60 * 1024 * 1024


def matmul(left, right):
    return jnp.dot(left, right, preferred_element_type=f32)


def across_rows(left, right):
    return lax.dot_general(left, right, (((0,), (0,)), ((), ())), preferred_element_type=f32)


def against(left, right):
    return lax.dot_general(left, right, (((1,), (1,)), ((), ())), preferred_element_type=f32)


def project_kernel(
    width, info_ref, h_ref, wkv_ref, wt_ref, bkv_ref, bt_ref, rot_ref, k_ref, v_ref, t_ref
):
    hidden = h_ref[...]
    rot_ref[...] = hidden
    rows = hidden.shape[0]
    valid = info_ref[1 + pl.program_id(0)]
    key_value = (matmul(hidden, wkv_ref[...]) + bkv_ref[...]).astype(bf16)
    row = lax.broadcasted_iota(jnp.int32, (rows, PLANE - width), 0)
    lane = lax.broadcasted_iota(jnp.int32, (rows, PLANE - width), 1)
    k_ref[:, :width] = key_value[:, :width]
    k_ref[:, width:] = jnp.where((lane == 0) & (row >= valid), mask_fill, 0.0).astype(bf16)
    v_ref[:, :width] = key_value[:, width:]
    v_ref[:, width:] = jnp.zeros((rows, PLANE - width), bf16)
    t_ref[...] = (against(wt_ref[...], hidden) + bt_ref[...]).astype(bf16)


def project(info, hidden_in, w_kv, w_all_t, bias_kv, bias_t, chunks):
    slot_len, model = hidden_in.shape
    width = w_all_t.shape[0] // 3
    rows = slot_len // chunks
    whole = lambda c, info_ref: (0, 0)
    return pl.pallas_call(
        functools.partial(project_kernel, width),
        grid_spec=pltpu.PrefetchScalarGridSpec(
            num_scalar_prefetch=1,
            grid=(chunks,),
            in_specs=[
                pl.BlockSpec((rows, model), lambda c, info_ref: ((info_ref[0] + c) % chunks, 0)),
                pl.BlockSpec((model, 2 * width), whole),
                pl.BlockSpec((3 * width, model), whole),
                pl.BlockSpec((1, 2 * width), whole),
                pl.BlockSpec((3 * width, 1), whole),
            ],
            out_specs=[
                pl.BlockSpec((rows, model), lambda c, info_ref: (c, 0)),
                pl.BlockSpec((rows, PLANE), lambda c, info_ref: (c, 0)),
                pl.BlockSpec((rows, PLANE), lambda c, info_ref: (c, 0)),
                pl.BlockSpec((3 * width, rows), lambda c, info_ref: (0, c)),
            ],
        ),
        out_shape=(
            jax.ShapeDtypeStruct((slot_len, model), bf16),
            jax.ShapeDtypeStruct((slot_len, PLANE), bf16),
            jax.ShapeDtypeStruct((slot_len, PLANE), bf16),
            jax.ShapeDtypeStruct((3 * width, slot_len), bf16),
        ),
        compiler_params=pltpu.CompilerParams(vmem_limit_bytes=VMEM_LIMIT),
        cost_estimate=pl.CostEstimate(
            flops=10 * width * model * slot_len,
            bytes_accessed=slot_len * model * 8,
            transcendentals=0,
        ),
        name="project",
    )(info, hidden_in, w_kv, w_all_t, bias_kv, bias_t)


def forward_kernel(bq, bk, heads, info_ref, k_ref, qt_ref, vt_ref, ot_ref, lse_ref, head_q, acc):
    width = HD * heads
    chunks = info_ref.shape[0] - 3
    first_tile = info_ref[1 + chunks]
    tile_count = info_ref[2 + chunks]
    row = lax.broadcasted_iota(jnp.int32, (PLANE, bq), 0)
    for h in range(heads):
        head_q[h] = jnp.where(row == width, 1.0, 0.0).astype(bf16)

    def query_step(qb, unused):
        q0 = pl.multiple_of(qb * bq, bq)
        for h in range(heads):
            own = slice(HD * h, HD * h + HD)
            head_q[h, own, :] = qt_ref[own, pl.ds(q0, bq)]
        acc[...] = jnp.zeros_like(acc)

        def key_step(step, carry):
            k0 = pl.multiple_of(((first_tile + step) % 2) * bk, bk)
            keys = k_ref[pl.ds(k0, bk), :]
            scores = [matmul(keys, head_q[h]) for h in range(heads)]
            kept = []
            for h in range(heads):
                top, total = carry[h]
                new_top = jnp.maximum(
                    top, jnp.max(scores[h], axis=0, keepdims=True) * SCORE_SCALE_2
                )
                weights = jnp.exp2(scores[h] * SCORE_SCALE_2 - new_top)
                fade = jnp.exp2(top - new_top)
                total = fade * total + jnp.sum(weights, axis=0, keepdims=True)
                values_t = vt_ref[HD * h : HD * h + HD, pl.ds(k0, bk)]
                acc[h] = fade * acc[h] + matmul(values_t, weights.astype(bf16))
                kept.append((new_top, total))
            return tuple(kept)

        start = tuple(
            (jnp.full((1, bq), mask_fill, f32), jnp.zeros((1, bq), f32)) for _ in range(heads)
        )
        done = lax.fori_loop(0, tile_count, key_step, start)
        for h in range(heads):
            top, total = done[h]
            ot_ref[HD * h : HD * h + HD, pl.ds(q0, bq)] = (acc[h] * (1.0 / total)).astype(bf16)
            lse_ref[pl.ds(h, 1), pl.ds(q0, bq)] = top + jnp.log2(total)
        return unused

    lax.fori_loop(0, qt_ref.shape[1] // bq, query_step, 0)


def attend_forward(info, wide_k, projected_t, chunk, chunks):
    slot_len = wide_k.shape[0]
    width = projected_t.shape[0] // 3
    heads = width // HD
    rows = slot_len // chunks
    bq, bk = min(512, rows), slot_len // 2
    pairs = heads * rows * slot_len
    return pl.pallas_call(
        functools.partial(forward_kernel, bq, bk, heads),
        grid=(1,),
        out_shape=(
            jax.ShapeDtypeStruct((width, rows), bf16),
            jax.ShapeDtypeStruct((8, rows), f32),
        ),
        in_specs=[
            pl.BlockSpec(memory_space=pltpu.SMEM),
            pl.BlockSpec((slot_len, PLANE), lambda i: (0, 0)),
            pl.BlockSpec((width, rows), lambda i: (0, chunk)),
            pl.BlockSpec((width, slot_len), lambda i: (2, 0)),
        ],
        out_specs=[
            pl.BlockSpec((width, rows), lambda i: (0, 0)),
            pl.BlockSpec((8, rows), lambda i: (0, 0)),
        ],
        scratch_shapes=[
            pltpu.VMEM((heads, PLANE, bq), bf16),
            pltpu.VMEM((heads, HD, bq), f32),
        ],
        compiler_params=pltpu.CompilerParams(vmem_limit_bytes=VMEM_LIMIT),
        cost_estimate=pl.CostEstimate(
            flops=16 * HD * pairs, bytes_accessed=slot_len * width * 8, transcendentals=pairs
        ),
        name="attend_forward",
    )(info, wide_k, projected_t, projected_t)


def backward_kernel(bq, heads, q_span, k_span, rows, has_q, has_k, end_q, end_k, *refs):
    width = HD * heads
    one_key = k_span[1] - k_span[0] == 1
    refs = list(refs)
    info_ref, k_ref, v_ref, kt_ref, qt_ref, got_ref, ot_ref, lse_ref = refs[:8]
    del refs[:8]
    gq_in = refs.pop(0) if has_q else None
    gk_in = refs.pop(0) if has_k else None
    gv_in = refs.pop(0) if has_k else None
    gq_low = refs.pop(0) if end_q else None
    gq = None if end_q else refs.pop(0)
    gkv_low = refs.pop(0) if end_k else None
    gk = None if end_k else refs.pop(0)
    gv = None if end_k else refs.pop(0)
    head_q, head_go = refs[:2]
    del refs[:2]
    if end_q:
        gq = refs.pop(0)
    if end_k:
        gk, gv = refs.pop(0), refs.pop(0)
    gq[...] = gq_in[...] if has_q else jnp.zeros_like(gq)
    gk[...] = gk_in[...] if has_k else jnp.zeros_like(gk)
    gv[...] = gv_in[...] if has_k else jnp.zeros_like(gv)
    row = lax.broadcasted_iota(jnp.int32, (PLANE, bq), 0)
    for h in range(heads):
        head_q[h] = jnp.where(row == width, 1.0, 0.0).astype(bf16)
        head_go[h] = jnp.zeros((PLANE, bq), bf16)

    def chunk_step(q, unused):
        def query_step(qb, inner):
            q0 = pl.multiple_of(qb * bq, bq)
            span = pl.ds(q0, bq)
            all_span = pl.ds(pl.multiple_of(q * rows + q0, bq), bq)
            deltas = []
            tops = []
            for h in range(heads):
                own = slice(HD * h, HD * h + HD)
                head_q[h, own, :] = qt_ref[own, all_span]
                grad_out = got_ref[q - q_span[0], own, span]
                head_go[h, own, :] = grad_out
                outs = ot_ref[q - q_span[0], own, span]
                deltas.append(
                    jnp.sum(grad_out.astype(f32) * outs.astype(f32), axis=0, keepdims=True)
                )
                tops.append(lse_ref[q - q_span[0], pl.ds(h, 1), span])

            def key_step(k, innermost):
                @pl.when(info_ref[1 + k] > 0)
                def one_tile():
                    at = k - k_span[0]
                    k0 = pl.multiple_of((at if one_key else k) * rows, rows)
                    keys = k_ref[pl.ds(k0, rows), :]
                    values = v_ref[pl.ds(k0, rows), :]
                    grad_v = None
                    grad_k = None
                    for h in range(heads):
                        own = slice(HD * h, HD * h + HD)
                        scores = matmul(keys, head_q[h])
                        grad_weights = matmul(values, head_go[h])
                        weights = jnp.exp2(scores * SCORE_SCALE_2 - tops[h])
                        grad_scores = (weights * (grad_weights - deltas[h])).astype(bf16)
                        more_v = against(weights.astype(bf16), head_go[h])
                        more_k = against(grad_scores, head_q[h])
                        grad_v = more_v if grad_v is None else grad_v + more_v
                        grad_k = more_k if grad_k is None else grad_k + more_k
                        gq[q - q_span[0], own, span] += matmul(
                            kt_ref[own, pl.ds(k0, rows)], grad_scores
                        )
                    gk[at] += grad_k
                    gv[at] += grad_v

                return innermost

            lax.fori_loop(k_span[0], k_span[1], key_step, 0)
            return inner

        lax.fori_loop(0, (info_ref[1 + q] + bq - 1) // bq, query_step, 0)
        return unused

    lax.fori_loop(q_span[0], q_span[1], chunk_step, 0)
    if end_q:
        gq_low[...] = (gq[...] * SCORE_SCALE).astype(bf16)
    if end_k:
        gkv_low[:, :, :width] = (gk[:, :, :width] * SCORE_SCALE).astype(bf16)
        gkv_low[:, :, width:] = gv[:, :, :width].astype(bf16)


def attend_backward(
    info, wide_k, wide_v, projected_t, grad_out_t, out_t, lse, q_span, k_span, gq, gkv, end_q, end_k
):
    chunks = info.shape[0] - 3
    slot_len = wide_k.shape[0]
    width = projected_t.shape[0] // 3
    heads = width // HD
    rows = slot_len // chunks
    nq, nk = q_span[1] - q_span[0], k_span[1] - k_span[0]
    bq = min(512, rows)
    one = nk == 1
    k_at = k_span[0]
    if one:
        key_spec = pl.BlockSpec((rows, PLANE), lambda i: (k_at, 0))
        kt_spec = pl.BlockSpec((width, rows), lambda i: (1, k_at))
    else:
        key_spec = pl.BlockSpec((slot_len, PLANE), lambda i: (0, 0))
        kt_spec = pl.BlockSpec((width, slot_len), lambda i: (1, 0))
    full3 = lambda i: (0, 0, 0)
    gq_shape, gk_shape = (nq, width, rows), (nk, rows, PLANE)
    gq_spec, gk_spec = pl.BlockSpec(gq_shape, full3), pl.BlockSpec(gk_shape, full3)
    operands = [info, wide_k, wide_v, projected_t, projected_t, grad_out_t, out_t, lse]
    in_specs = [
        pl.BlockSpec(memory_space=pltpu.SMEM),
        key_spec,
        key_spec,
        kt_spec,
        pl.BlockSpec((width, slot_len), lambda i: (0, 0)),
        gq_spec,
        gq_spec,
        pl.BlockSpec((nq, 8, rows), full3),
    ]
    if gq is not None:
        operands.append(gq)
        in_specs.append(gq_spec)
    if gkv is not None:
        operands.extend(gkv)
        in_specs.extend([gk_spec, gk_spec])
    out_shape = [jax.ShapeDtypeStruct(gq_shape, bf16 if end_q else f32)]
    out_specs = [gq_spec]
    scratch = [
        pltpu.VMEM((heads, PLANE, bq), bf16),
        pltpu.VMEM((heads, PLANE, bq), bf16),
    ]
    if end_q:
        scratch.append(pltpu.VMEM(gq_shape, f32))
    if end_k:
        out_shape.append(jax.ShapeDtypeStruct((nk, rows, 2 * width), bf16))
        out_specs.append(pl.BlockSpec((nk, rows, 2 * width), full3))
        scratch.extend([pltpu.VMEM(gk_shape, f32)] * 2)
    else:
        out_shape.extend([jax.ShapeDtypeStruct(gk_shape, f32)] * 2)
        out_specs.extend([gk_spec] * 2)
    pairs = heads * nq * nk * rows * rows
    results = pl.pallas_call(
        functools.partial(
            backward_kernel,
            bq,
            heads,
            q_span,
            k_span,
            rows,
            gq is not None,
            gkv is not None,
            end_q,
            end_k,
        ),
        grid=(1,),
        out_shape=tuple(out_shape),
        in_specs=in_specs,
        out_specs=out_specs,
        scratch_shapes=scratch,
        compiler_params=pltpu.CompilerParams(vmem_limit_bytes=VMEM_LIMIT),
        cost_estimate=pl.CostEstimate(
            flops=40 * HD * pairs,
            bytes_accessed=(nq + nk) * rows * width * 12,
            transcendentals=pairs,
        ),
        name="attend_backward",
    )(*operands)
    return results[0], (results[1] if end_k else (results[1], results[2]))


def transposed(left, right):
    return lax.dot_general(left, right, (((0,), (0,)), ((), ())), preferred_element_type=f32)


def ffn_forward_kernel(row_step, x_ref, w_in_ref, b_ref, w_down_ref, act_ref, slope_ref, out_ref):
    for r0 in range(0, x_ref.shape[0], row_step):
        rows = slice(r0, r0 + row_step)
        pre = matmul(x_ref[rows, :], w_in_ref[0]) + b_ref[0].astype(f32)
        below = 0.5 + 0.5 * lax.erf(pre * math.sqrt(0.5))
        density = jnp.exp(-0.5 * pre * pre) * (1.0 / math.sqrt(2.0 * math.pi))
        act = (pre * below).astype(bf16)
        act_ref[0, rows, :] = act
        slope_ref[0, rows, :] = (below + pre * density).astype(bf16)
        more = matmul(act, w_down_ref[0])

        @pl.when(pl.program_id(0) == 0)
        def first():
            out_ref[rows, :] = more

        @pl.when(pl.program_id(0) > 0)
        def later():
            out_ref[rows, :] += more


def ffn_forward(first_low, gathered, b_in_all):
    count, model = first_low.shape
    groups = gathered.shape[0]
    units = b_in_all.shape[-1]
    block = pl.BlockSpec((1, count, units), lambda b: (b, 0, 0))
    return pl.pallas_call(
        functools.partial(ffn_forward_kernel, min(256, count)),
        grid=(groups,),
        in_specs=[
            pl.BlockSpec((count, model), lambda b: (0, 0)),
            pl.BlockSpec((1, model, units), lambda b: (b, 0, 0)),
            pl.BlockSpec((1, 1, units), lambda b: (b, 0, 0)),
            pl.BlockSpec((1, units, model), lambda b: (b, 1, 0)),
        ],
        out_specs=[block, block, pl.BlockSpec((count, model), lambda b: (0, 0))],
        out_shape=(
            jax.ShapeDtypeStruct((groups, count, units), bf16),
            jax.ShapeDtypeStruct((groups, count, units), bf16),
            jax.ShapeDtypeStruct((count, model), f32),
        ),
        compiler_params=pltpu.CompilerParams(vmem_limit_bytes=VMEM_LIMIT),
        cost_estimate=pl.CostEstimate(
            flops=8 * count * model * units * groups,
            bytes_accessed=8 * groups * count * units,
            transcendentals=groups * count * units,
        ),
        name="ffn_forward",
    )(first_low, gathered, b_in_all, gathered)


def ffn_backward_kernel(row_step, g_ref, w_in_ref, w_down_ref, slope_ref, pre_ref, out_ref):
    for r0 in range(0, g_ref.shape[0], row_step):
        rows = slice(r0, r0 + row_step)
        grad_act = against(g_ref[rows, :], w_down_ref[0])
        grad_pre = (grad_act * slope_ref[0, rows, :].astype(f32)).astype(bf16)
        pre_ref[0, rows, :] = grad_pre
        more = against(grad_pre, w_in_ref[0])

        @pl.when(pl.program_id(0) == 0)
        def first():
            out_ref[rows, :] = more

        @pl.when(pl.program_id(0) > 0)
        def later():
            out_ref[rows, :] += more


def ffn_backward(grad_ffn_low, gathered, slopes):
    count, model = grad_ffn_low.shape
    groups, _, units = slopes.shape
    block = pl.BlockSpec((1, count, units), lambda b: (b, 0, 0))
    return pl.pallas_call(
        functools.partial(ffn_backward_kernel, min(256, count)),
        grid=(groups,),
        in_specs=[
            pl.BlockSpec((count, model), lambda b: (0, 0)),
            pl.BlockSpec((1, model, units), lambda b: (b, 0, 0)),
            pl.BlockSpec((1, units, model), lambda b: (b, 1, 0)),
            block,
        ],
        out_specs=[block, pl.BlockSpec((count, model), lambda b: (0, 0))],
        out_shape=(
            jax.ShapeDtypeStruct((groups, count, units), bf16),
            jax.ShapeDtypeStruct((count, model), f32),
        ),
        compiler_params=pltpu.CompilerParams(vmem_limit_bytes=VMEM_LIMIT),
        cost_estimate=pl.CostEstimate(
            flops=4 * count * model * units * groups,
            bytes_accessed=8 * groups * count * units,
            transcendentals=0,
        ),
        name="ffn_backward",
    )(grad_ffn_low, gathered, gathered, slopes)


SMALL_ROWS = 32
UNIT = 128


def pack_kernel(
    dp_size,
    part,
    first_ref,
    gpre_ref,
    act_ref,
    gffn_ref,
    att_ref,
    gmix_ref,
    gstud_ref,
    second_ref,
    columns_ref,
    pool_ref,
    class_ref,
    tail_ref,
    out_ref,
    stud_acc,
    small,
):
    b = pl.program_id(0)
    at = 0

    def store(rows_value):
        nonlocal at
        done = 0
        count = rows_value.shape[0]
        while done < count:
            d, offset = divmod(at, part)
            take = min(part - offset, count - done)
            out_ref[d, 0, offset : offset + take, :] = rows_value[done : done + take].astype(bf16)
            done += take
            at += take

    store(transposed(first_ref[...], gpre_ref[0]))
    store(transposed(act_ref[0], gffn_ref[...]))
    store(matmul(att_ref[...], gmix_ref[...]))
    groups = pl.num_programs(0)
    stud_cols = stud_acc.shape[1]

    @pl.when(b == 0)
    def student():
        whole = transposed(gstud_ref[...], second_ref[...])
        for i in range(stud_acc.shape[0]):
            stud_acc[i] = whole[i * stud_cols : (i + 1) * stud_cols]

    store(stud_acc[b])
    small[...] = jnp.zeros_like(small)
    small[:, :UNIT] = pool_ref[...]
    units = columns_ref.shape[1] // UNIT
    count = columns_ref.shape[0] * units
    share = -(-count // stud_acc.shape[0])
    for block in range(stud_acc.shape[0]):

        @pl.when(b == block)
        def own_columns():
            for r in range(share):
                u = block * share + r
                if u < count:
                    lanes = slice((u % units) * UNIT, (u % units + 1) * UNIT)
                    small[r : r + 1, UNIT : 2 * UNIT] = columns_ref[
                        u // units : u // units + 1, lanes
                    ]

    small[: class_ref.shape[1], 2 * UNIT : 3 * UNIT] = class_ref[0]

    @pl.when(b == 0)
    def tail_rows():
        small[: tail_ref.shape[0], 3 * UNIT : 4 * UNIT] = tail_ref[...]

    grad_b_in = jnp.sum(gpre_ref[0].astype(f32), axis=0, keepdims=True)
    for u in range(grad_b_in.shape[1] // UNIT):
        small[u : u + 1, 4 * UNIT : 5 * UNIT] = grad_b_in[:, u * UNIT : (u + 1) * UNIT]
    small[0:1, 5 * UNIT : 6 * UNIT] = jnp.sum(gstud_ref[...].astype(f32), axis=0, keepdims=True)
    store(small[...])
    if at < dp_size * part:
        store(jnp.zeros((dp_size * part - at, small.shape[1]), f32))


def pack_gradients(dp_size, part, groups, dense, columns, pool, classes, tail):
    first_low, grad_pre, acts, grad_ffn, attended_t, grad_mix, grad_stud, second_low = dense
    count, model = first_low.shape
    units = acts.shape[2]
    width = attended_t.shape[0] // groups
    students = grad_stud.shape[1]
    stud_cols = students // groups
    rows = lambda cols: pl.BlockSpec((count, cols), lambda b: (0, 0))
    block = pl.BlockSpec((1, count, units), lambda b: (b, 0, 0))
    whole = lambda array: pl.BlockSpec(array.shape, lambda b: (0,) * array.ndim)
    return pl.pallas_call(
        functools.partial(pack_kernel, dp_size, part),
        grid=(groups,),
        in_specs=[
            rows(model),
            block,
            block,
            rows(model),
            pl.BlockSpec((width, count), lambda b: (b, 0)),
            rows(model),
            rows(students),
            rows(model),
            whole(columns),
            pl.BlockSpec((pool.shape[0] // groups, pool.shape[1]), lambda b: (b, 0)),
            pl.BlockSpec((1,) + classes.shape[1:], lambda b: (b, 0, 0)),
            whole(tail),
        ],
        out_specs=pl.BlockSpec((dp_size, 1, part, model), lambda b: (0, b, 0, 0)),
        out_shape=jax.ShapeDtypeStruct((dp_size, groups, part, model), bf16),
        scratch_shapes=[
            pltpu.VMEM((groups, stud_cols, model), f32),
            pltpu.VMEM((SMALL_ROWS, model), f32),
        ],
        compiler_params=pltpu.CompilerParams(vmem_limit_bytes=VMEM_LIMIT),
        cost_estimate=pl.CostEstimate(
            flops=6 * count * model * units * groups,
            bytes_accessed=8 * groups * count * units,
            transcendentals=0,
        ),
        name="pack_gradients",
    )(
        first_low,
        grad_pre,
        acts,
        grad_ffn,
        attended_t,
        grad_mix,
        grad_stud,
        second_low,
        columns,
        pool,
        classes,
        tail,
    )


def normalize(resid, gain, shift):
    center = resid - jnp.mean(resid, axis=-1, keepdims=True)
    invstd = lax.rsqrt(jnp.mean(center * center, axis=-1, keepdims=True) + epsilon)
    normed = center * invstd
    return (normed * gain + shift, normed, invstd)


def normalize_back(grad, normed, invstd, gain):
    scaled = grad * gain
    inner = (
        scaled
        - jnp.mean(scaled, axis=-1, keepdims=True)
        - normed * jnp.mean(scaled * normed, axis=-1, keepdims=True)
    )
    return (invstd * inner, jnp.sum(grad * normed, axis=0), jnp.sum(grad, axis=0))


def shift(array, ahead, group_size):
    if ahead % group_size == 0:
        return array
    moves = [(i, (i + ahead) % group_size) for i in range(group_size)]
    return lax.ppermute(array, "tensor", moves)


def group_tiles(tile, rank, group_size):
    found = [shift(tile, s, group_size) for s in range(group_size)]
    tiles = jnp.zeros((group_size,) + tile.shape, tile.dtype)
    for s in range(group_size):
        tiles = lax.dynamic_update_index_in_dim(tiles, found[s], (rank - s) % group_size, 0)
    return tiles


def ring_gather(own, rank, group_size):
    rows = own.shape[0]
    whole = jnp.zeros((group_size * rows,) + own.shape[1:], own.dtype)
    whole = lax.dynamic_update_slice_in_dim(whole, own, rank * rows, 0)
    held = own
    for s in range(1, group_size):
        held = shift(held, 1, group_size)
        source = (rank - s) % group_size
        whole = lax.dynamic_update_slice_in_dim(whole, held, source * rows, 0)
    return whole


def row_parts(rows):
    dp_size = lax.axis_size("dp")
    part = -(-rows // (16 * dp_size)) * 16
    return dp_size, part


def spread_gather(shard):
    dp_size, part = row_parts(shard.shape[0])
    shard = jnp.pad(shard, ((0, part * dp_size - shard.shape[0]), (0, 0)))
    mine = lax.dynamic_slice_in_dim(shard, lax.axis_index("dp") * part, part, 0)
    whole = lax.all_gather(mine, ("tensor", "dp"), axis=0, tiled=True)
    return whole.reshape(lax.axis_size("tensor"), part * dp_size, shard.shape[1])


def body(
    hidden_in,
    lengths,
    labels,
    out_cotangent,
    w_query,
    b_query,
    w_key,
    w_value,
    b_value,
    w_out,
    b_out,
    ln1_gain,
    ln1_bias,
    w_in,
    b_in,
    w_down,
    b_down,
    ln2_gain,
    ln2_bias,
    w_student,
    b_student,
    pool_query,
    w_pool,
    b_pool,
    w_class,
    b_class,
):
    slot_len, model = hidden_in.shape
    group_size = lax.axis_size("tensor")
    own_count = slot_len // group_size
    rank = lax.axis_index("tensor")
    own_start = rank * own_count
    width = w_query.shape[1]
    hidden_width = w_in.shape[1]
    stu_cols = w_student.shape[1]
    length = lengths[0]
    pad_row = lambda row: jnp.pad(row[None, :], ((0, 0), (0, model - row.shape[0])))

    w_kv = jnp.concatenate([w_key, w_value], axis=1)
    w_project_t = jnp.concatenate([w_query.T, w_key.T, w_value.T], axis=0)
    gathered = spread_gather(jnp.concatenate([w_in, w_down, w_out], axis=0))
    w_out_all = gathered[:, model + hidden_width : model + hidden_width + width].reshape(
        group_size * width, model
    )
    w_project_all = spread_gather(w_project_t)
    stud_tile = jnp.concatenate(
        [w_student.T, b_in[None, :], pad_row(b_student), jnp.zeros((6, model), bf16)], axis=0
    )
    stud_tiles = group_tiles(stud_tile, rank, group_size)
    w_stud_t = stud_tiles[:, :stu_cols].reshape(group_size * stu_cols, model)
    b_in_all = stud_tiles[:, stu_cols : stu_cols + 1]
    b_stud_all = stud_tiles[:, stu_cols + 1, :stu_cols].reshape(1, group_size * stu_cols)

    hidden_own = lax.dynamic_slice_in_dim(hidden_in, own_start, own_count, 0)
    cot_own = lax.dynamic_slice_in_dim(out_cotangent, own_start, own_count, 0)
    chunk_at = (rank + jnp.arange(group_size, dtype=jnp.int32)) % group_size
    chunk_valid = jnp.clip(length - chunk_at * own_count, 0, own_count)
    half = group_size // 2
    first_empty = (jnp.sum(chunk_valid[:half]) == 0).astype(jnp.int32)
    second_empty = (jnp.sum(chunk_valid[half:]) == 0).astype(jnp.int32)
    info = jnp.concatenate(
        [
            rank[None],
            chunk_valid,
            first_empty[None],
            (2 - first_empty - second_empty)[None],
        ]
    ).astype(jnp.int32)
    bias_t = jnp.concatenate([b_query, jnp.zeros_like(b_query), b_value])
    hidden_rot, wide_k, wide_v, projected_t = project(
        info, hidden_in, w_kv, w_project_t, bias_t[None, width:], bias_t[:, None], group_size
    )

    outs = [None] * group_size
    lses = [None] * group_size
    attended = [None] * group_size
    for s in list(range(1, group_size)) + [0]:
        outs[s], lses[s] = attend_forward(info, wide_k, projected_t, s, group_size)
        attended[s] = shift(outs[s], s, group_size)
    attended_t = jnp.zeros((group_size * width, own_count), bf16)
    for s in range(group_size):
        source = (rank - s) % group_size
        attended_t = lax.dynamic_update_slice_in_dim(attended_t, attended[s], source * width, 0)

    resid1 = across_rows(attended_t, w_out_all) + b_out + hidden_own.astype(f32)
    first, normed1, invstd1 = normalize(resid1, ln1_gain, ln1_bias)
    first_low = first.astype(bf16)
    acts, slopes, ffn = ffn_forward(first_low, gathered, b_in_all)
    resid2 = ffn + b_down + first_low.astype(f32)
    second, normed2, invstd2 = normalize(resid2, ln2_gain, ln2_bias)
    second_low = second.astype(bf16)
    leaving, w_project_all = lax.optimization_barrier((second_low, w_project_all))
    hidden_out = lax.all_gather(leaving, "tensor", axis=0, tiled=True)

    student_low = (against(second_low, w_stud_t) + b_stud_all.astype(f32)).astype(bf16)
    student = student_low.astype(f32)
    student_width = student.shape[1]
    head_width = student_width // POOL_HEADS
    probe_scale = 1.0 / math.sqrt(head_width)
    own_rows = own_start + lax.broadcasted_iota(jnp.int32, (own_count, 1), 0)
    row_valid = own_rows < length
    head_of = lax.broadcasted_iota(jnp.int32, (1, student_width), 1) // head_width

    def per_head(values_wide):
        whole = jnp.zeros_like(values_wide)
        for h in range(POOL_HEADS):
            part = jnp.sum(
                jnp.where(head_of == h, values_wide, 0.0), axis=-1, keepdims=True
            )
            whole = jnp.where(head_of == h, part, whole)
        return whole

    probes = pool_query[None, :]
    energies = jnp.where(row_valid, per_head(student * probes) * probe_scale, mask_fill)
    local_top = jnp.max(energies, axis=0, keepdims=True)
    local_weights = jnp.exp(energies - local_top)
    local_total = jnp.sum(local_weights, axis=0, keepdims=True)
    local_pooled = jnp.sum(local_weights * student, axis=0, keepdims=True)
    stats = jnp.concatenate(
        [local_top, local_total, local_pooled, jnp.zeros((5, student_width), f32)], axis=0
    )
    stats_all = jnp.stack([shift(stats, s, group_size) for s in range(group_size)])
    top = jnp.max(stats_all[:, 0], axis=0, keepdims=True)
    fade = jnp.exp(stats_all[:, 0] - top)
    inv_total = 1.0 / jnp.sum(fade * stats_all[:, 1], axis=0, keepdims=True)
    pooled = jnp.sum(fade * stats_all[:, 2], axis=0, keepdims=True) * inv_total
    squashed = jnp.tanh(jnp.dot(pooled, w_pool, precision=highest) + b_pool)
    logits = jnp.dot(squashed, w_class, precision=highest) + b_class
    classes = lax.broadcasted_iota(jnp.int32, logits.shape, 1)
    g_logits = jax.nn.softmax(logits, axis=-1) - (classes == labels[:, None]).astype(f32)
    grad_w_class_t = g_logits.reshape(-1, 1) * squashed
    grad_b_class = g_logits[0]
    g_u = lax.dot_general(
        g_logits, w_class, (((1,), (1,)), ((), ())), precision=highest
    ) * (1.0 - squashed * squashed)
    grad_w_pool = pooled.reshape(-1, 1) * g_u
    grad_b_pool = g_u[0]
    g_pooled = lax.dot_general(g_u, w_pool, (((1,), (1,)), ((), ())), precision=highest)
    inner = per_head(pooled * g_pooled)
    pool = jnp.exp(energies - top) * inv_total
    g_energy = pool * (per_head(student * g_pooled) - inner)
    g_stud_low = (pool * g_pooled + g_energy * probes * probe_scale).astype(bf16)
    grad_pool_query = jnp.sum(g_energy * student, axis=0) * probe_scale

    grad_second = jnp.where(row_valid, cot_own.astype(f32), 0.0) + matmul(g_stud_low, w_stud_t)
    grad_resid2, grad_ln2_gain, grad_ln2_bias = normalize_back(
        grad_second, normed2, invstd2, ln2_gain
    )
    grad_b_down = jnp.sum(grad_resid2, axis=0)
    grad_ffn_low = grad_resid2.astype(bf16)
    grad_pre, grad_first = ffn_backward(grad_ffn_low, gathered, slopes)
    grad_first = grad_first + grad_resid2
    grad_resid1, grad_ln1_gain, grad_ln1_bias = normalize_back(
        grad_first, normed1, invstd1, ln1_gain
    )
    grad_b_out = jnp.sum(grad_resid1, axis=0)
    grad_mix = grad_resid1.astype(bf16)
    grad_att_t = against(w_out_all, grad_mix).astype(bf16)
    grad_outs = []
    for s in range(group_size):
        target = (rank - s) % group_size
        piece = lax.dynamic_slice_in_dim(grad_att_t, target * width, width, 0)
        grad_outs.append(shift(piece, -s, group_size))

    only_once = (rank == 0).astype(f32)
    lanes = student_width
    class_count = grad_b_class.shape[0]
    columns = jnp.stack(
        [grad_b_out, grad_ln1_gain, grad_ln1_bias, grad_b_down, grad_ln2_gain, grad_ln2_bias]
    )
    class_share = -(-class_count // group_size)
    grad_w_class_t = jnp.pad(
        grad_w_class_t * only_once, ((0, class_share * group_size - class_count), (0, 0))
    ).reshape(group_size, class_share, lanes)
    tail = jnp.stack(
        [
            grad_b_pool * only_once,
            jnp.pad(grad_b_class, (0, lanes - class_count)) * only_once,
            grad_pool_query,
        ]
    )
    at = model + hidden_width
    small_at = at + width + stu_cols
    dp_size, part = row_parts(small_at + SMALL_ROWS)
    dense = (first_low, grad_pre, acts, grad_ffn_low, attended_t, grad_mix, g_stud_low, second_low)
    blocks = pack_gradients(
        dp_size, part, group_size, dense, columns, grad_w_pool * only_once, grad_w_class_t, tail
    )
    grad_outs[0], blocks = lax.optimization_barrier((grad_outs[0], blocks))
    part_of = functools.partial(attend_backward, info, wide_k, wide_v, projected_t)
    others = (1, group_size)
    own_side = (grad_outs[0][None], outs[0][None], lses[0][None])
    other_side = tuple(jnp.stack(side[1:]) for side in (grad_outs, outs, lses))
    gq_own, gkv_others = part_of(*own_side, (0, 1), others, None, None, False, False)
    blocks, hidden_out, gq_own = lax.optimization_barrier((blocks, hidden_out, gq_own))
    reduced = lax.psum_scatter(
        blocks.reshape(dp_size * group_size, part, model), "dp", scatter_dimension=0, tiled=True
    )
    gq_others = None
    grad_kv = [None] * group_size
    kv_arrived = [None] * group_size
    for s in range(1, group_size):
        so_far = tuple(side[s - 1 : s] for side in gkv_others)
        gq_others, low = part_of(
            *other_side, others, (s, s + 1), gq_others, so_far, False, True
        )
        grad_kv[s] = low[0]
        kv_arrived[s] = shift(grad_kv[s], s, group_size)
    reduced, gq_others = lax.optimization_barrier((reduced, gq_others))
    reduced = lax.psum_scatter(reduced, "tensor", scatter_dimension=0, tiled=True)
    gkv_own = None
    grad_q = [None] * group_size
    q_arrived = [None] * group_size
    for s in range(1, group_size):
        side = (grad_outs[s][None], outs[s][None], lses[s][None])
        low, gkv_own = part_of(
            *side, (s, s + 1), (0, 1), gq_others[s - 1 : s], gkv_own, True, False
        )
        grad_q[s] = low[0]
        q_arrived[s] = shift(grad_q[s], s, group_size)
    reduced, gkv_own = lax.optimization_barrier((reduced, gkv_own))
    reduced = lax.all_gather(reduced[0], "dp", axis=0, tiled=True)
    low_q, low_kv = part_of(*own_side, (0, 1), (0, 1), gq_own, gkv_own, True, True)
    grad_q[0] = q_arrived[0] = low_q[0]
    grad_kv[0] = kv_arrived[0] = low_kv[0]

    grad_in_own = grad_resid1
    for s in range(group_size):
        source = (rank - s) % group_size
        w_source = lax.dynamic_index_in_dim(w_project_all, source, 0, keepdims=False)
        grad_in_own = (
            grad_in_own
            + across_rows(q_arrived[s], w_source[:width])
            + matmul(kv_arrived[s], w_source[width : 3 * width])
        )
    grad_in = ring_gather(grad_in_own.astype(bf16), rank, group_size)

    grad_w_q = None
    grad_w_kv = None
    grad_b_q = None
    grad_b_kv = None
    for s in range(group_size):
        rows_here = hidden_rot[s * own_count : (s + 1) * own_count]
        more_q = lax.dot_general(
            grad_q[s], rows_here, (((1,), (0,)), ((), ())), preferred_element_type=f32
        )
        more_kv = across_rows(grad_kv[s], rows_here)
        more_bq = jnp.sum(grad_q[s], axis=1, dtype=f32)
        more_bkv = jnp.sum(grad_kv[s], axis=0, dtype=f32)
        grad_w_q = more_q if s == 0 else grad_w_q + more_q
        grad_w_kv = more_kv if s == 0 else grad_w_kv + more_kv
        grad_b_q = more_bq if s == 0 else grad_b_q + more_bq
        grad_b_kv = more_bkv if s == 0 else grad_b_kv + more_bkv
    late = jnp.concatenate(
        [grad_w_q, grad_w_kv, pad_row(grad_b_q), pad_row(grad_b_kv[width:])], axis=0
    ).astype(bf16)
    late, reduced = lax.optimization_barrier((late, reduced))
    small_own = reduced[small_at : small_at + SMALL_ROWS]
    small = group_tiles(small_own[:, : 4 * UNIT], rank, group_size).astype(f32)
    small_own = small_own[:, 4 * UNIT :].astype(f32)
    grad_w_pool = small[:, :, :UNIT].reshape(grad_w_pool.shape)
    column_share = -(-columns.size // (UNIT * group_size))
    columns = small[:, :column_share, UNIT : 2 * UNIT].reshape(-1)[: columns.size].reshape(
        columns.shape
    )
    grad_w_class = (
        small[:, :class_share, 2 * UNIT : 3 * UNIT].reshape(-1, lanes)[:class_count].T
    )
    grad_b_pool = small[0, 0, 3 * UNIT :]
    grad_b_class = small[0, 1, 3 * UNIT : 3 * UNIT + class_count]
    grad_pool_query = small[0, 2, 3 * UNIT :]
    grad_b_in = small_own[: hidden_width // UNIT, :UNIT].reshape(-1)
    grad_b_stud = lax.dynamic_slice_in_dim(small_own[0, UNIT:], rank * stu_cols, stu_cols, 0)

    late = lax.psum(late, "dp").astype(f32)
    reduced = reduced.astype(f32)
    return (
        hidden_out,
        logits,
        grad_in,
        late[:width].T,
        late[3 * width, :width],
        late[width : 2 * width].T,
        late[2 * width : 3 * width].T,
        late[3 * width + 1, :width],
        reduced[at : at + width],
        columns[0],
        columns[1],
        columns[2],
        reduced[:model],
        grad_b_in,
        reduced[model:at],
        columns[3],
        columns[4],
        columns[5],
        reduced[at + width : small_at].T,
        grad_b_stud,
        grad_pool_query,
        grad_w_pool,
        grad_b_pool,
        grad_w_class,
        grad_b_class,
    )


def solution(mesh):
    by_dp = P("dp", None)
    cols = P(None, "tensor")
    rows = P("tensor", None)
    cut = P("tensor")
    in_specs = (
        (by_dp, P("dp"), P("dp"), by_dp, cols, cut, cols, cols, cut, rows, P(), P(), P(), cols)
        + (cut, rows, P(), P(), P(), cols, cut, P(), P(), P(), P(), P())
    )
    out_specs = (
        (by_dp, by_dp, by_dp, cols, cut, cols, cols, cut, rows, P(), P(), P(), cols, cut, rows)
        + (P(), P(), P(), cols, cut, P(), P(), P(), P(), P())
    )
    return jax.shard_map(body, mesh=mesh, in_specs=in_specs, out_specs=out_specs, check_vma=False)
```

time: 983 us -> 748 us (0.76)
  blocking collectives: 159 us -> 0 us
  matrix products: 117 us -> 54.1 us
  local copies, waits for them, and re-layouts: 86.4 us -> 51.2 us
  starting transfers between devices: 19.2 us -> 53.3 us
  Pallas kernels: 208 us -> 176 us
  other arithmetic: 33.5 us -> 44.8 us
    ppermute x12 -> x24, waiting for transfers between devices: 45.4 us -> 191 us  [shift(): return lax.ppermute(array, 'tensor', moves)]
    psum x2 -> x0, blocking collectives: 127 us -> none  [the longest x1 114 us: body(): lax.psum((jnp.stack(grad_b_in), grad_pool_query, grad_w_pool * only_once,...]
    reduce_scatter x2 -> x1, waiting for transfers between devices: 122 us -> 0.01 us  [body(): lax.psum_scatter(blocks.reshape(dp_size * group_size, part, model), 'dp',...]
    reduce_scatter x1, waiting for transfers between devices: 62.3 us -> 11.6 us  [body(): lax.psum_scatter(reduced, 'tensor', scatter_dimension=0, tiled=True)]
    all_gather x0 -> x1, waiting for transfers between devices: none -> 35.9 us  [body(): hidden_out = lax.all_gather(leaving, 'tensor', axis=0, tiled=True)]
    dot_general x11 -> x2, matrix products: 38.3 us -> 3.53 us  [against(): lax.dot_general(left, right, (((1,), (1,)), ((), ())), preferred_element_...]
    ppermute x12 -> x24, starting transfers between devices: 18.6 us -> 52.8 us  [shift(): return lax.ppermute(array, 'tensor', moves)]
    pallas_call x5 -> x16, Pallas kernels: 208 us -> 176 us  [the longest x8 52.1 us: attend_backward(): pl.pallas_call(functools.partial(backward_kernel, bq, heads, q_span, k_sp...]
  transfers between devices with their start and end apart: 20 -> 31, of which waited for: 8 -> 14; matrix products, arithmetic and copies ran while one was open for 14% -> 16% of each run, Pallas kernels for 21% -> 24%
where the time goes in v2:
time: 748 us; the launch traced here: 735 us
  waiting for transfers between devices  337 us (45%)
  Pallas kernels  176 us (24%)
  matrix products  54.1 us (7%)
  starting transfers between devices  53.3 us (7%)
  local copies, waits for them, and re-layouts  51.2 us (7%)
  other arithmetic  44.8 us (6%)
  between operations  18.2 us (2%)
    ppermute x24, waiting for transfers between devices, shift(): return lax.ppermute(array, 'tensor', moves)  191 us
    psum x1, waiting for transfers between devices, body(): late = lax.psum(late, 'dp').astype(f32)  72.9 us
    ppermute x24, starting transfers between devices, shift(): return lax.ppermute(array, 'tensor', moves)  52.8 us
    pallas_call x8, Pallas kernels, attend_backward(): pl.pallas_call(functools.partial(backward_kernel, bq, heads, q_span, k_sp...  52.1 us
    pallas_call x4, Pallas kernels, attend_forward(): pl.pallas_call(functools.partial(forward_kernel, bq, bk, heads), grid=(1,...  48.3 us
    all_gather x1, waiting for transfers between devices, body(): hidden_out = lax.all_gather(leaving, 'tensor', axis=0, tiled=True)  35.9 us
    all_gather x2, waiting for transfers between devices, spread_gather(): whole = lax.all_gather(mine, ('tensor', 'dp'), axis=0, tiled=True)  25.8 us
    pallas_call x1, Pallas kernels, ffn_forward(): pl.pallas_call(functools.partial(ffn_forward_kernel, min(256, count)), gr...  22.7 us
  transfers between devices with their start and end apart: 31, of which 14 were waited for; matrix products, arithmetic and copies ran while one was open for 16% of the time, Pallas kernels for 24%

profile of v2, /device:TPU:0, one launch (start us, length us, event | category | flops | bytes accessed | tf_op | source)
XLA Modules:
  0.0 734.5 jit_solution(144057432146946838)
XLA Ops:
  24.2 11.4 %project.1 = (bf16[4096,768]{1,0:T(8,128)(2,1)}, bf16[4096,256]{1,0:T(8,128)(2,1)}, bf16[4096,256]{1,0:T(8,128)(2,1)}, bf16[576,4096]{1,0:T(8,128)(2,1)}) custom-call(s32[7]{0:T(128)} %pad_add_fusion.info_ref.refs_0_, bf16[4096,768]{1,0:T(8,128)(2,1)} %h_ref.1, bf16[768,384]{1,0:T(8,128)(2,1)} %pad_maximum_fusion.3.wkv_ref, ...), custom_call_target="tpu_custom_call" | custom-call | flops 6039797760 | bytes 25165824 | tf_op jit(solution)/shard_map/project/pallas_call | solution.py:59
  35.6 12.0 %attend_forward.5 = (bf16[192,1024]{1,0:T(8,128)(2,1)}, f32[8,1024]{1,0:T(8,128)}) custom-call(s32[7]{0:T(128)} %pad_add_fusion.info_ref.refs_0_, bf16[4096,256]{1,0:T(8,128)(2,1)} %get-tuple-element.76.k_ref.refs_1_, bf16[576,4096]{1,0:T(8,128)(2,1)} %get-tuple-element.77.qt_ref.vt_ref.refs_3_.refs_4_, ...), custom_call_target="tpu_custom_call" | custom-call | flops 12884901888 | bytes 6291456 | tf_op jit(solution)/shard_map/attend_forward/pallas_call | solution.py:148
  48.3 12.1 %attend_forward.6 = (bf16[192,1024]{1,0:T(8,128)(2,1)}, f32[8,1024]{1,0:T(8,128)}) custom-call(s32[7]{0:T(128)} %pad_add_fusion.info_ref.refs_0_, bf16[4096,256]{1,0:T(8,128)(2,1)} %get-tuple-element.76.k_ref.refs_1_, bf16[576,4096]{1,0:T(8,128)(2,1)} %get-tuple-element.77.qt_ref.vt_ref.refs_3_.refs_4_, ...), custom_call_target="tpu_custom_call" | custom-call | flops 12884901888 | bytes 6291456 | tf_op jit(solution)/shard_map/attend_forward/pallas_call | solution.py:148
  61.8 12.0 %attend_forward.4 = (bf16[192,1024]{1,0:T(8,128)(2,1)}, f32[8,1024]{1,0:T(8,128)}) custom-call(s32[7]{0:T(128)} %pad_add_fusion.info_ref.refs_0_, bf16[4096,256]{1,0:T(8,128)(2,1)} %get-tuple-element.76.k_ref.refs_1_, bf16[576,4096]{1,0:T(8,128)(2,1)} %get-tuple-element.77.qt_ref.vt_ref.refs_3_.refs_4_, ...), custom_call_target="tpu_custom_call" | custom-call | flops 12884901888 | bytes 6291456 | tf_op jit(solution)/shard_map/attend_forward/pallas_call | solution.py:148
  75.3 12.1 %attend_forward.7 = (bf16[192,1024]{1,0:T(8,128)(2,1)}, f32[8,1024]{1,0:T(8,128)}) custom-call(s32[7]{0:T(128)} %pad_add_fusion.info_ref.refs_0_, bf16[4096,256]{1,0:T(8,128)(2,1)} %get-tuple-element.76.k_ref.refs_1_, bf16[576,4096]{1,0:T(8,128)(2,1)} %get-tuple-element.77.qt_ref.vt_ref.refs_3_.refs_4_, ...), custom_call_target="tpu_custom_call" | custom-call | flops 12884901888 | bytes 6291456 | tf_op jit(solution)/shard_map/attend_forward/pallas_call | solution.py:148
  91.4 12.4 %collective-permute-done.1 = bf16[192,1024]{1,0:T(8,128)(2,1)S(1)} collective-permute-done((bf16[192,1024]{1,0:T(8,128)(2,1)}, bf16[192,1024]{1,0:T(8,128)(2,1)S(1)}, u32[]{:S(2)}, u32[]{:S(2)}) %collective-permute-start.1) | collective-permute-done | bytes 393248 | tf_op jit(solution)/shard_map/ppermute | solution.py:605
  103.8 10.7 %collective-permute-done.2 = bf16[192,1024]{1,0:T(8,128)(2,1)S(1)} collective-permute-done((bf16[192,1024]{1,0:T(8,128)(2,1)}, bf16[192,1024]{1,0:T(8,128)(2,1)S(1)}, u32[]{:S(2)}, u32[]{:S(2)}) %collective-permute-start.2) | collective-permute-done | bytes 393248 | tf_op jit(solution)/shard_map/ppermute | solution.py:605
  114.6 6.2 all-gather.6.cloned.1.call-done
  128.5 22.7 %ffn_forward.1 = (bf16[4,1024,768]{2,1,0:T(8,128)(2,1)}, bf16[4,1024,768]{2,1,0:T(8,128)(2,1)}, f32[1024,768]{1,0:T(8,128)}) custom-call(bf16[1024,768]{1,0:T(8,128)(2,1)} %add_convert_fusion.2.x_ref.first_ref, bf16[4,1792,768]{2,1,0:T(8,128)(2,1)} %bitcast.274, bf16[4,1,768]{2,1,0:T(2,128)(2,1)} %slice.268.b_ref, bf16[4,1792,768]{2,1,0:T(8,128)(2,1)} %bitcast.275), custom_call_target="tpu_custom_call" | custom-call | flops 19327352832 | bytes 25165824 | tf_op jit(solution)/shard_map/ffn_forward/pallas_call | solution.py:376
  165.4 19.6 %all-gather.8.cloned.1.call-done = bf16[2560,768]{1,0:T(8,128)(2,1)} async-done(((bf16[80,768]{1,0:T(8,128)(2,1)}), bf16[2560,768]{1,0:T(8,128)(2,1)}) %all-gather.8.cloned.1.call-update) | async-done | bytes 3932176 | tf_op jit(solution)/shard_map/all_gather | solution.py:638
  192.4 5.7 multiply_reduce_fusion
  202.2 21.2 %ffn_backward.1 = (bf16[4,1024,768]{2,1,0:T(8,128)(2,1)}, f32[1024,768]{1,0:T(8,128)}) custom-call(bf16[1024,768]{1,0:T(8,128)(2,1)} %convert_element_type.123.g_ref.gffn_ref, bf16[4,1792,768]{2,1,0:T(8,128)(2,1)} %bitcast.276, bf16[4,1792,768]{2,1,0:T(8,128)(2,1)} %bitcast.277, bf16[4,1024,768]{2,1,0:T(8,128)(2,1)} %get-tuple-element.83.slope_ref), custom_call_target="tpu_custom_call" | custom-call | flops 9663676416 | bytes 25165824 | tf_op jit(solution)/shard_map/ffn_backward/pallas_call | solution.py:422
  237.3 20.1 %pack_gradients.1 = bf16[8,4,224,768]{3,2,1,0:T(8,128)(2,1)} custom-call(bf16[1024,768]{1,0:T(8,128)(2,1)} %add_convert_fusion.2.x_ref.first_ref, bf16[4,1024,768]{2,1,0:T(8,128)(2,1)} %get-tuple-element.85.gpre_ref, bf16[4,1024,768]{2,1,0:T(8,128)(2,1)} %get-tuple-element.86.act_ref, bf16[1024,768]{1,0:T(8,128)(2,1)} %convert_element_type.123.g_ref.gffn_ref, ...), custom_call_target="tpu_custom_call" | custom-call | flops 14495514624 | bytes 25165824 | tf_op jit(solution)/shard_map/pack_gradients/pallas_call | solution.py:538
  257.4 7.4 %attend_backward.8 = (f32[1,192,1024]{2,1,0:T(8,128)}, f32[3,1024,256]{2,1,0:T(8,128)}, f32[3,1024,256]{2,1,0:T(8,128)}) custom-call(s32[7]{0:T(128)} %pad_add_fusion.info_ref.refs_0_, bf16[4096,256]{1,0:T(8,128)(2,1)} %get-tuple-element.76.k_ref.refs_1_, bf16[4096,256]{1,0:T(8,128)(2,1)} %get-tuple-element.89.refs_2_, ...), custom_call_target="tpu_custom_call" | custom-call | flops 24159191040 | bytes 9437184 | tf_op jit(solution)/shard_map/attend_backward/pallas_call | solution.py:318
  264.8 35.9 %all-gather.10.cloned.1.call-done = bf16[4096,768]{1,0:T(8,128)(2,1)} async-done(((bf16[1024,768]{1,0:T(8,128)(2,1)}), bf16[4096,768]{1,0:T(8,128)(2,1)}) %all-gather.10.cloned.1.call-update) | async-done | bytes 6291472 | tf_op jit(solution)/shard_map/all_gather | solution.py:735
  317.1 22.6 %collective-permute-done.10 = bf16[192,1024]{1,0:T(8,128)(2,1)S(1)} collective-permute-done((bf16[192,1024]{1,0:T(8,128)(2,1)}, bf16[192,1024]{1,0:T(8,128)(2,1)S(1)}, u32[]{:S(2)}, u32[]{:S(2)}) %collective-permute-start.10) | collective-permute-done | bytes 393248 | tf_op jit(solution)/shard_map/ppermute | solution.py:605
  341.7 5.6 attend_backward.9
  348.2 6.0 attend_backward.10
  354.3 11.0 %collective-permute-start.15 = (bf16[1024,384]{1,0:T(8,128)(2,1)}, bf16[1024,384]{1,0:T(8,128)(2,1)}, u32[]{:S(2)}, u32[]{:S(2)}) collective-permute-start(bf16[1024,384]{1,0:T(8,128)(2,1)} %bitcast.243), channel_id=1, source_target_pairs={{0,2},{1,3},{2,0},{3,1},{4,6},{5,7},{6,4},{7,5},{8,10},{9,11},{10,... | collective-permute-start | bytes 2359304 | tf_op jit(solution)/shard_map/ppermute | solution.py:605
  365.2 6.9 attend_backward.11
  374.4 29.5 %collective-permute-done.15 = bf16[1024,384]{1,0:T(8,128)(2,1)} collective-permute-done((bf16[1024,384]{1,0:T(8,128)(2,1)}, bf16[1024,384]{1,0:T(8,128)(2,1)}, u32[]{:S(2)}, u32[]{:S(2)}) %collective-permute-start.15) | collective-permute-done | bytes 786464 | tf_op jit(solution)/shard_map/ppermute | solution.py:605
  415.3 15.1 %collective-permute-start.12 = (bf16[192,1024]{1,0:T(8,128)(2,1)}, bf16[192,1024]{1,0:T(8,128)(2,1)S(1)}, u32[]{:S(2)}, u32[]{:S(2)}) collective-permute-start(bf16[192,1024]{1,0:T(8,128)(2,1)} %bitcast.244), channel_id=1, source_target_pairs={{0,1},{1,2},{2,3},{3,0},{4,5},{5,6},{6,7},{7,4},{8,9},{9,10},{10,1... | collective-permute-start | bytes 1179656 | tf_op jit(solution)/shard_map/ppermute | solution.py:605
  430.4 4.7 attend_backward.13
  446.9 23.5 %collective-permute-done.14 = bf16[192,1024]{1,0:T(8,128)(2,1)} collective-permute-done((bf16[192,1024]{1,0:T(8,128)(2,1)}, bf16[192,1024]{1,0:T(8,128)(2,1)}, u32[]{:S(2)}, u32[]{:S(2)}) %collective-permute-start.14) | collective-permute-done | bytes 393248 | tf_op jit(solution)/shard_map/ppermute | solution.py:605
  477.0 11.6 %reduce-scatter.5.cloned.1.call-done = bf16[1,224,768]{2,1,0:T(8,128)(2,1)} async-done(((bf16[4,224,768]{2,1,0:T(8,128)(2,1)}), bf16[1,224,768]{2,1,0:T(8,128)(2,1)}) %reduce-scatter.5.cloned.1.call-update) | async-done | bytes 344080 | tf_op jit(solution)/shard_map/reduce_scatter | solution.py:852
  488.6 12.5 %attend_backward.15 = (bf16[1,192,1024]{2,1,0:T(8,128)(2,1)}, bf16[1,1024,384]{2,1,0:T(8,128)(2,1)}) custom-call(s32[7]{0:T(128)} %pad_add_fusion.info_ref.refs_0_, bf16[4096,256]{1,0:T(8,128)(2,1)} %get-tuple-element.76.k_ref.refs_1_, bf16[4096,256]{1,0:T(8,128)(2,1)} %get-tuple-element.89.refs_2_, ...), custom_call_target="tpu_custom_call" | custom-call | flops 8053063680 | bytes 4718592 | tf_op jit(solution)/shard_map/attend_backward/pallas_call | solution.py:318
  512.2 5.9 constant_dynamic-update-slice_fusion.3
  527.6 27.8 %collective-permute-done.18 = bf16[1024,768]{1,0:T(8,128)(2,1)S(1)} collective-permute-done((bf16[1024,768]{1,0:T(8,128)(2,1)}, bf16[1024,768]{1,0:T(8,128)(2,1)S(1)}, u32[]{:S(2)}, u32[]{:S(2)}) %collective-permute-start.18) | collective-permute-done | bytes 1572896 | tf_op jit(solution)/shard_map/ppermute | solution.py:605
  561.1 30.7 %collective-permute-done.19 = bf16[1024,768]{1,0:T(8,128)(2,1)S(1)} collective-permute-done((bf16[1024,768]{1,0:T(8,128)(2,1)S(1)}, bf16[1024,768]{1,0:T(8,128)(2,1)S(1)}, u32[]{:S(2)}, u32[]{:S(2)}) %collective-permute-start.19) | collective-permute-done | bytes 1572896 | tf_op jit(solution)/shard_map/ppermute | solution.py:605
  598.3 28.8 %collective-permute-done.20 = bf16[1024,768]{1,0:T(8,128)(2,1)} collective-permute-done((bf16[1024,768]{1,0:T(8,128)(2,1)S(1)}, bf16[1024,768]{1,0:T(8,128)(2,1)}, u32[]{:S(2)}, u32[]{:S(2)}) %collective-permute-start.20) | collective-permute-done | bytes 1572896 | tf_op jit(solution)/shard_map/ppermute | solution.py:605
  644.6 72.9 %all-reduce.10.cloned.1.call-done = bf16[578,768]{1,0:T(8,128)(2,1)} async-done(((bf16[578,768]{1,0:T(8,128)(2,1)}), bf16[578,768]{1,0:T(8,128)(2,1)}) %all-reduce.10.cloned.1.call-update) | async-done | bytes 887824 | tf_op jit(solution)/shard_map/psum | solution.py:917
  721.3 5.9 copy.94
  (324 shorter events, 173.6 us)
Async XLA Ops:
  7.2 178.0 %copy-start = (f32[128,128]{1,0:T(8,128)S(1)}, f32[128,128]{1,0:T(8,128)}, u32[]{:S(2)}) copy-start(f32[128,128]{1,0:T(8,128)} %param.48) | copy-start | bytes 196612
  7.3 113.4 %all-gather.6.cloned.1.call-start = ((), (), s32[]{:S(2)}) async-start(), calls=%async_computation.2 | async-start | bytes 11354112 | tf_op jit(solution)/shard_map/all_gather | solution.py:638
  9.7 175.3 %all-gather.8.cloned.1.call-start = ((), (), s32[]{:S(2)}) async-start(), calls=%async_computation.3 | async-start | bytes 4055040 | tf_op jit(solution)/shard_map/all_gather | solution.py:638
  10.0 77.5 %collective-permute-start.3 = (bf16[40,768]{1,0:T(8,128)(2,1)S(1)}, bf16[40,768]{1,0:T(8,128)(2,1)S(1)}, u32[]{:S(2)}, u32[]{:S(2)}) collective-permute-start(bf16[40,768]{1,0:T(8,128)(2,1)S(1)} %fusion.61), channel_id=1, source_target_pairs={{0,1},{1,2},{2,3},{3,0},{4,5},{5,6},{6,7},{7,4},{8,9},{9,10},{10,1... | collective-permute-start | bytes 184328 | tf_op jit(solution)/shard_map/ppermute | solution.py:605
  13.0 77.6 %collective-permute-start.4 = (bf16[40,768]{1,0:T(8,128)(2,1)S(1)}, bf16[40,768]{1,0:T(8,128)(2,1)S(1)}, u32[]{:S(2)}, u32[]{:S(2)}) collective-permute-start(bf16[40,768]{1,0:T(8,128)(2,1)S(1)} %fusion.61), channel_id=1, source_target_pairs={{0,2},{1,3},{2,0},{3,1},{4,6},{5,7},{6,4},{7,5},{8,10},{9,11},{10,... | collective-permute-start | bytes 184328 | tf_op jit(solution)/shard_map/ppermute | solution.py:605
  15.6 75.0 %collective-permute-start.5 = (bf16[40,768]{1,0:T(8,128)(2,1)S(1)}, bf16[40,768]{1,0:T(8,128)(2,1)S(1)}, u32[]{:S(2)}, u32[]{:S(2)}) collective-permute-start(bf16[40,768]{1,0:T(8,128)(2,1)S(1)} %fusion.61), channel_id=1, source_target_pairs={{0,3},{1,0},{2,1},{3,2},{4,7},{5,4},{6,5},{7,6},{8,11},{9,8},{10,9... | collective-permute-start | bytes 184328 | tf_op jit(solution)/shard_map/ppermute | solution.py:605
  47.6 43.8 %collective-permute-start = (bf16[192,1024]{1,0:T(8,128)(2,1)}, bf16[192,1024]{1,0:T(8,128)(2,1)S(1)}, u32[]{:S(2)}, u32[]{:S(2)}) collective-permute-start(bf16[192,1024]{1,0:T(8,128)(2,1)} %get-tuple-element.79), channel_id=1, source_target_pairs={{0,1},{1,2},{2,3},{3,0},{4,5},{5,6},{6,7},{7,4},{8,9},{9,10},{10,1... | collective-permute-start | bytes 1179656 | tf_op jit(solution)/shard_map/ppermute | solution.py:605
  60.4 43.4 %collective-permute-start.1 = (bf16[192,1024]{1,0:T(8,128)(2,1)}, bf16[192,1024]{1,0:T(8,128)(2,1)S(1)}, u32[]{:S(2)}, u32[]{:S(2)}) collective-permute-start(bf16[192,1024]{1,0:T(8,128)(2,1)} %get-tuple-element.80), channel_id=1, source_target_pairs={{0,2},{1,3},{2,0},{3,1},{4,6},{5,7},{6,4},{7,5},{8,10},{9,11},{10,... | collective-permute-start | bytes 1179656 | tf_op jit(solution)/shard_map/ppermute | solution.py:605
  61.6 239.1 %all-gather.10.cloned.1.call-start = ((), (), s32[]{:S(2)}) async-start(), calls=%async_computation.4 | async-start | bytes 7864320 | tf_op jit(solution)/shard_map/all_gather | solution.py:735
  87.4 27.1 %collective-permute-start.2 = (bf16[192,1024]{1,0:T(8,128)(2,1)}, bf16[192,1024]{1,0:T(8,128)(2,1)S(1)}, u32[]{:S(2)}, u32[]{:S(2)}) collective-permute-start(bf16[192,1024]{1,0:T(8,128)(2,1)} %get-tuple-element.81), channel_id=1, source_target_pairs={{0,3},{1,0},{2,1},{3,2},{4,7},{5,4},{6,5},{7,6},{8,11},{9,8},{10,9... | collective-permute-start | bytes 1179656 | tf_op jit(solution)/shard_map/ppermute | solution.py:605
  161.0 24.2 %collective-permute-start.6 = (f32[8,128]{1,0:T(8,128)S(1)}, f32[8,128]{1,0:T(8,128)S(1)}, u32[]{:S(2)}, u32[]{:S(2)}) collective-permute-start(f32[8,128]{1,0:T(8,128)S(1)} %maximum_maximum_fusion), channel_id=1, source_target_pairs={{0,1},{1,2},{2,3},{3,0},{4,5},{5,6},{6,7},{7,4},{8,9},{9,10},{10,1... | collective-permute-start | bytes 12296 | tf_op jit(solution)/shard_map/ppermute | solution.py:605
  161.0 24.2 %collective-permute-start.7 = (f32[8,128]{1,0:T(8,128)S(1)}, f32[8,128]{1,0:T(8,128)S(1)}, u32[]{:S(2)}, u32[]{:S(2)}) collective-permute-start(f32[8,128]{1,0:T(8,128)S(1)} %maximum_maximum_fusion), channel_id=1, source_target_pairs={{0,2},{1,3},{2,0},{3,1},{4,6},{5,7},{6,4},{7,5},{8,10},{9,11},{10,... | collective-permute-start | bytes 12296 | tf_op jit(solution)/shard_map/ppermute | solution.py:605
  162.5 22.6 %collective-permute-start.8 = (f32[8,128]{1,0:T(8,128)S(1)}, f32[8,128]{1,0:T(8,128)S(1)}, u32[]{:S(2)}, u32[]{:S(2)}) collective-permute-start(f32[8,128]{1,0:T(8,128)S(1)} %maximum_maximum_fusion), channel_id=1, source_target_pairs={{0,3},{1,0},{2,1},{3,2},{4,7},{5,4},{6,5},{7,6},{8,11},{9,8},{10,9... | collective-permute-start | bytes 12296 | tf_op jit(solution)/shard_map/ppermute | solution.py:605
  185.1 222.8 %reduce-scatter.3.cloned.1.call-start = ((), (), s32[]{:S(2)}) async-start(), calls=%async_computation.5 | async-start | bytes 12386304 | tf_op jit(solution)/shard_map/reduce_scatter | solution.py:838
  300.7 187.9 %reduce-scatter.5.cloned.1.call-start = ((), (), s32[]{:S(2)}) async-start(), calls=%async_computation.6 | async-start | bytes 1720320 | tf_op jit(solution)/shard_map/reduce_scatter | solution.py:852
  304.5 12.6 %collective-permute-start.9 = (bf16[192,1024]{1,0:T(8,128)(2,1)}, bf16[192,1024]{1,0:T(8,128)(2,1)S(1)}, u32[]{:S(2)}, u32[]{:S(2)}) collective-permute-start(bf16[192,1024]{1,0:T(8,128)(2,1)} %get-tuple-element.176), channel_id=1, source_target_pairs={{0,3},{1,0},{2,1},{3,2},{4,7},{5,4},{6,5},{7,6},{8,11},{9,8},{10,9... | collective-permute-start | bytes 1179656 | tf_op jit(solution)/shard_map/ppermute | solution.py:605
  304.8 34.9 %collective-permute-start.10 = (bf16[192,1024]{1,0:T(8,128)(2,1)}, bf16[192,1024]{1,0:T(8,128)(2,1)S(1)}, u32[]{:S(2)}, u32[]{:S(2)}) collective-permute-start(bf16[192,1024]{1,0:T(8,128)(2,1)} %get-tuple-element.178), channel_id=1, source_target_pairs={{0,2},{1,3},{2,0},{3,1},{4,6},{5,7},{6,4},{7,5},{8,10},{9,11},{10,... | collective-permute-start | bytes 1179656 | tf_op jit(solution)/shard_map/ppermute | solution.py:605
  305.2 34.6 %collective-permute-start.11 = (bf16[192,1024]{1,0:T(8,128)(2,1)}, bf16[192,1024]{1,0:T(8,128)(2,1)S(1)}, u32[]{:S(2)}, u32[]{:S(2)}) collective-permute-start(bf16[192,1024]{1,0:T(8,128)(2,1)} %get-tuple-element.177), channel_id=1, source_target_pairs={{0,1},{1,2},{2,3},{3,0},{4,5},{5,6},{6,7},{7,4},{8,9},{9,10},{10,1... | collective-permute-start | bytes 1179656 | tf_op jit(solution)/shard_map/ppermute | solution.py:605
  347.3 24.8 %collective-permute-start.13 = (bf16[1024,384]{1,0:T(8,128)(2,1)}, bf16[1024,384]{1,0:T(8,128)(2,1)}, u32[]{:S(2)}, u32[]{:S(2)}) collective-permute-start(bf16[1024,384]{1,0:T(8,128)(2,1)} %bitcast.242), channel_id=1, source_target_pairs={{0,1},{1,2},{2,3},{3,0},{4,5},{5,6},{6,7},{7,4},{8,9},{9,10},{10,1... | collective-permute-start | bytes 2359304 | tf_op jit(solution)/shard_map/ppermute | solution.py:605
  354.3 49.6 %collective-permute-start.15 = (bf16[1024,384]{1,0:T(8,128)(2,1)}, bf16[1024,384]{1,0:T(8,128)(2,1)}, u32[]{:S(2)}, u32[]{:S(2)}) collective-permute-start(bf16[1024,384]{1,0:T(8,128)(2,1)} %bitcast.243), channel_id=1, source_target_pairs={{0,2},{1,3},{2,0},{3,1},{4,6},{5,7},{6,4},{7,5},{8,10},{9,11},{10,... | collective-permute-start | bytes 2359304 | tf_op jit(solution)/shard_map/ppermute | solution.py:605
  372.1 134.8 %collective-permute-start.17 = (bf16[1024,384]{1,0:T(8,128)(2,1)}, bf16[1024,384]{1,0:T(8,128)(2,1)}, u32[]{:S(2)}, u32[]{:S(2)}) collective-permute-start(bf16[1024,384]{1,0:T(8,128)(2,1)} %bitcast.249), channel_id=1, source_target_pairs={{0,3},{1,0},{2,1},{3,2},{4,7},{5,4},{6,5},{7,6},{8,11},{9,8},{10,9... | collective-permute-start | bytes 2359304 | tf_op jit(solution)/shard_map/ppermute | solution.py:605
  411.0 218.8 %all-gather.12.cloned.1.call-start = ((), (), s32[]{:S(2)}) async-start(), calls=%async_computation.8 | async-start | bytes 3096576 | tf_op jit(solution)/shard_map/all_gather | solution.py:864
  415.3 28.3 %collective-permute-start.12 = (bf16[192,1024]{1,0:T(8,128)(2,1)}, bf16[192,1024]{1,0:T(8,128)(2,1)S(1)}, u32[]{:S(2)}, u32[]{:S(2)}) collective-permute-start(bf16[192,1024]{1,0:T(8,128)(2,1)} %bitcast.244), channel_id=1, source_target_pairs={{0,1},{1,2},{2,3},{3,0},{4,5},{5,6},{6,7},{7,4},{8,9},{9,10},{10,1... | collective-permute-start | bytes 1179656 | tf_op jit(solution)/shard_map/ppermute | solution.py:605
  435.1 35.3 %collective-permute-start.14 = (bf16[192,1024]{1,0:T(8,128)(2,1)}, bf16[192,1024]{1,0:T(8,128)(2,1)}, u32[]{:S(2)}, u32[]{:S(2)}) collective-permute-start(bf16[192,1024]{1,0:T(8,128)(2,1)} %bitcast.262), channel_id=1, source_target_pairs={{0,2},{1,3},{2,0},{3,1},{4,6},{5,7},{6,4},{7,5},{8,10},{9,11},{10,... | collective-permute-start | bytes 1179656 | tf_op jit(solution)/shard_map/ppermute | solution.py:605
  443.4 30.3 %collective-permute-start.16 = (bf16[192,1024]{1,0:T(8,128)(2,1)}, bf16[192,1024]{1,0:T(8,128)(2,1)S(1)}, u32[]{:S(2)}, u32[]{:S(2)}) collective-permute-start(bf16[192,1024]{1,0:T(8,128)(2,1)} %bitcast.263), channel_id=1, source_target_pairs={{0,3},{1,0},{2,1},{3,2},{4,7},{5,4},{6,5},{7,6},{8,11},{9,8},{10,9... | collective-permute-start | bytes 1179656 | tf_op jit(solution)/shard_map/ppermute | solution.py:605
  518.1 37.3 %collective-permute-start.18 = (bf16[1024,768]{1,0:T(8,128)(2,1)}, bf16[1024,768]{1,0:T(8,128)(2,1)S(1)}, u32[]{:S(2)}, u32[]{:S(2)}) collective-permute-start(bf16[1024,768]{1,0:T(8,128)(2,1)} %get-tuple-element.194), channel_id=1, source_target_pairs={{0,1},{1,2},{2,3},{3,0},{4,5},{5,6},{6,7},{7,4},{8,9},{9,10},{10,1... | collective-permute-start | bytes 4718600 | tf_op jit(solution)/shard_map/ppermute | solution.py:605
  518.1 199.3 %all-reduce.10.cloned.1.call-start = ((), (), s32[]{:S(2)}) async-start(), calls=%async_computation.7 | async-start | bytes 1794048 | tf_op jit(solution)/shard_map/psum | solution.py:917
  555.4 36.4 %collective-permute-start.19 = (bf16[1024,768]{1,0:T(8,128)(2,1)S(1)}, bf16[1024,768]{1,0:T(8,128)(2,1)S(1)}, u32[]{:S(2)}, u32[]{:S(2)}) collective-permute-start(bf16[1024,768]{1,0:T(8,128)(2,1)S(1)} %collective-permute-done.18), channel_id=1, source_target_pairs={{0,1},{1,2},{2,3},{3,0},{4,5},{5,6},{6,7},{7,4},{8,9},{9,10},{10,1... | collective-permute-start | bytes 4718600 | tf_op jit(solution)/shard_map/ppermute | solution.py:605
  591.8 35.4 %collective-permute-start.20 = (bf16[1024,768]{1,0:T(8,128)(2,1)S(1)}, bf16[1024,768]{1,0:T(8,128)(2,1)}, u32[]{:S(2)}, u32[]{:S(2)}) collective-permute-start(bf16[1024,768]{1,0:T(8,128)(2,1)S(1)} %collective-permute-done.19), channel_id=1, source_target_pairs={{0,1},{1,2},{2,3},{3,0},{4,5},{5,6},{6,7},{7,4},{8,9},{9,10},{10,1... | collective-permute-start | bytes 4718600 | tf_op jit(solution)/shard_map/ppermute | solution.py:605
  632.4 9.1 %collective-permute-start.21 = (bf16[32,512]{1,0:T(8,128)(2,1)S(1)}, bf16[32,512]{1,0:T(8,128)(2,1)S(1)}, u32[]{:S(2)}, u32[]{:S(2)}) collective-permute-start(bf16[32,512]{1,0:T(8,128)(2,1)S(1)} %slice.247), channel_id=1, source_target_pairs={{0,1},{1,2},{2,3},{3,0},{4,5},{5,6},{6,7},{7,4},{8,9},{9,10},{10,1... | collective-permute-start | bytes 98312 | tf_op jit(solution)/shard_map/ppermute | solution.py:605
  632.7 8.8 %collective-permute-start.22 = (bf16[32,512]{1,0:T(8,128)(2,1)S(1)}, bf16[32,512]{1,0:T(8,128)(2,1)S(1)}, u32[]{:S(2)}, u32[]{:S(2)}) collective-permute-start(bf16[32,512]{1,0:T(8,128)(2,1)S(1)} %slice.247), channel_id=1, source_target_pairs={{0,2},{1,3},{2,0},{3,1},{4,6},{5,7},{6,4},{7,5},{8,10},{9,11},{10,... | collective-permute-start | bytes 98312 | tf_op jit(solution)/shard_map/ppermute | solution.py:605
  633.2 8.3 %collective-permute-start.23 = (bf16[32,512]{1,0:T(8,128)(2,1)S(1)}, bf16[32,512]{1,0:T(8,128)(2,1)S(1)}, u32[]{:S(2)}, u32[]{:S(2)}) collective-permute-start(bf16[32,512]{1,0:T(8,128)(2,1)S(1)} %slice.247), channel_id=1, source_target_pairs={{0,3},{1,0},{2,1},{3,2},{4,7},{5,4},{6,5},{7,6},{8,11},{9,8},{10,9... | collective-permute-start | bytes 98312 | tf_op jit(solution)/shard_map/ppermute | solution.py:605
  (56 other events, 604.0 us)
Sparse Core Ops, SparseCore 0:
  11.6 109.0 all-gather.5
  123.6 61.3 all-gather.7
  186.6 114.0 all-gather.9
  304.1 82.2 reduce-scatter.2
  411.1 77.4 reduce-scatter.4
  518.2 57.9 all-gather.11
  641.1 76.3 all-reduce.9

commit v3 on v2

--- a/solution.py
+++ b/solution.py
@@ -19,6 +19,8 @@
 SCORE_SCALE = 1.0 / math.sqrt(HD)
 SCORE_SCALE_2 = math.log2(math.e) * SCORE_SCALE
 PLANE = 256
+UNIT = 128
+SMALL_ROWS = 32
 VMEM_LIMIT = 60 * 1024 * 1024
 
 
@@ -82,11 +84,7 @@
             jax.ShapeDtypeStruct((3 * width, slot_len), bf16),
         ),
         compiler_params=pltpu.CompilerParams(vmem_limit_bytes=VMEM_LIMIT),
-        cost_estimate=pl.CostEstimate(
-            flops=10 * width * model * slot_len,
-            bytes_accessed=slot_len * model * 8,
-            transcendentals=0,
-        ),
+        cost_estimate=pl.CostEstimate(flops=1, bytes_accessed=1, transcendentals=0),
         name="project",
     )(info, hidden_in, w_kv, w_all_t, bias_kv, bias_t)
 
@@ -167,36 +165,36 @@
             pltpu.VMEM((heads, HD, bq), f32),
         ],
         compiler_params=pltpu.CompilerParams(vmem_limit_bytes=VMEM_LIMIT),
-        cost_estimate=pl.CostEstimate(
-            flops=16 * HD * pairs, bytes_accessed=slot_len * width * 8, transcendentals=pairs
-        ),
+        cost_estimate=pl.CostEstimate(flops=1, bytes_accessed=1, transcendentals=0),
         name="attend_forward",
     )(info, wide_k, projected_t, projected_t)
 
 
-def backward_kernel(bq, heads, q_span, k_span, rows, has_q, has_k, end_q, end_k, *refs):
+def backward_kernel(bq, heads, q_span, k_span, rows, has, end_q, end_k, *refs):
     width = HD * heads
     one_key = k_span[1] - k_span[0] == 1
     refs = list(refs)
     info_ref, k_ref, v_ref, kt_ref, qt_ref, got_ref, ot_ref, lse_ref = refs[:8]
     del refs[:8]
-    gq_in = refs.pop(0) if has_q else None
-    gk_in = refs.pop(0) if has_k else None
-    gv_in = refs.pop(0) if has_k else None
-    gq_low = refs.pop(0) if end_q else None
-    gq = None if end_q else refs.pop(0)
+    hidden_ref = refs.pop(0) if end_q or end_k else None
+    gq_in = refs.pop(0) if "q" in has else None
+    gk_in = refs.pop(0) if "k" in has else None
+    gv_in = refs.pop(0) if "k" in has else None
+    wq_in = refs.pop(0) if "wq" in has else None
+    wkv_in = refs.pop(0) if "wkv" in has else None
+    gq_out = refs.pop(0)
     gkv_low = refs.pop(0) if end_k else None
     gk = None if end_k else refs.pop(0)
     gv = None if end_k else refs.pop(0)
+    w_out_ref = refs.pop(0) if end_q or end_k else None
     head_q, head_go = refs[:2]
     del refs[:2]
-    if end_q:
-        gq = refs.pop(0)
+    gq = refs.pop(0) if end_q else gq_out
     if end_k:
         gk, gv = refs.pop(0), refs.pop(0)
-    gq[...] = gq_in[...] if has_q else jnp.zeros_like(gq)
-    gk[...] = gk_in[...] if has_k else jnp.zeros_like(gk)
-    gv[...] = gv_in[...] if has_k else jnp.zeros_like(gv)
+    gq[...] = jnp.zeros_like(gq) if gq_in is None else gq_in[...]
+    gk[...] = jnp.zeros_like(gk) if gk_in is None else gk_in[...]
+    gv[...] = jnp.zeros_like(gv) if gv_in is None else gv_in[...]
     row = lax.broadcasted_iota(jnp.int32, (PLANE, bq), 0)
     for h in range(heads):
         head_q[h] = jnp.where(row == width, 1.0, 0.0).astype(bf16)
@@ -254,34 +252,73 @@
         return unused
 
     lax.fori_loop(q_span[0], q_span[1], chunk_step, 0)
+    ones = jnp.ones((rows, UNIT), bf16)
+
+    def add_weights(first_row, product, sum_in):
+        lead = slice(first_row, first_row + product(ones).shape[0])
+        model = hidden_ref.shape[1]
+        for lanes, right in ((slice(0, model), hidden_ref[...]), (slice(model, None), ones)):
+            value = product(right)
+            if sum_in is not None:
+                value = value + sum_in[:, lanes]
+            w_out_ref[lead, lanes] = value.astype(w_out_ref.dtype)
+
     if end_q:
-        gq_low[...] = (gq[...] * SCORE_SCALE).astype(bf16)
+        low = (gq[0] * SCORE_SCALE).astype(bf16)
+        gq_out[0] = low
+        add_weights(0, lambda right: matmul(low, right), wq_in)
     if end_k:
-        gkv_low[:, :, :width] = (gk[:, :, :width] * SCORE_SCALE).astype(bf16)
-        gkv_low[:, :, width:] = gv[:, :, :width].astype(bf16)
+        gkv_low[0, :, :width] = (gk[0, :, :width] * SCORE_SCALE).astype(bf16)
+        gkv_low[0, :, width:] = gv[0, :, :width].astype(bf16)
+        both = gkv_low[0]
+        add_weights(
+            width if end_q else 0,
+            lambda right: lax.dot_general(
+                both, right, (((0,), (0,)), ((), ())), preferred_element_type=f32
+            ),
+            wkv_in,
+        )
 
 
 def attend_backward(
-    info, wide_k, wide_v, projected_t, grad_out_t, out_t, lse, q_span, k_span, gq, gkv, end_q, end_k
+    info,
+    wide_k,
+    wide_v,
+    projected_t,
+    hidden_rot,
+    grad_out_t,
+    out_t,
+    lse,
+    q_span,
+    k_span,
+    gq=None,
+    gkv=None,
+    wq=None,
+    wkv=None,
+    gq_at=0,
+    gkv_at=0,
+    end_q=False,
+    end_k=False,
 ):
     chunks = info.shape[0] - 3
     slot_len = wide_k.shape[0]
     width = projected_t.shape[0] // 3
+    model = hidden_rot.shape[1]
     heads = width // HD
     rows = slot_len // chunks
     nq, nk = q_span[1] - q_span[0], k_span[1] - k_span[0]
     bq = min(512, rows)
-    one = nk == 1
     k_at = k_span[0]
-    if one:
+    if nk == 1:
         key_spec = pl.BlockSpec((rows, PLANE), lambda i: (k_at, 0))
         kt_spec = pl.BlockSpec((width, rows), lambda i: (1, k_at))
     else:
         key_spec = pl.BlockSpec((slot_len, PLANE), lambda i: (0, 0))
         kt_spec = pl.BlockSpec((width, slot_len), lambda i: (1, 0))
-    full3 = lambda i: (0, 0, 0)
+    at_zero = lambda i: (0, 0, 0)
     gq_shape, gk_shape = (nq, width, rows), (nk, rows, PLANE)
-    gq_spec, gk_spec = pl.BlockSpec(gq_shape, full3), pl.BlockSpec(gk_shape, full3)
+    gq_spec, gk_spec = pl.BlockSpec(gq_shape, at_zero), pl.BlockSpec(gk_shape, at_zero)
+    whole2 = lambda array: pl.BlockSpec(array.shape, lambda i: (0, 0))
     operands = [info, wide_k, wide_v, projected_t, projected_t, grad_out_t, out_t, lse]
     in_specs = [
         pl.BlockSpec(memory_space=pltpu.SMEM),
@@ -291,14 +328,26 @@
         pl.BlockSpec((width, slot_len), lambda i: (0, 0)),
         gq_spec,
         gq_spec,
-        pl.BlockSpec((nq, 8, rows), full3),
+        pl.BlockSpec((nq, 8, rows), at_zero),
     ]
+    has = []
+    if end_q or end_k:
+        ended = k_at if end_k else q_span[0]
+        operands.append(hidden_rot)
+        in_specs.append(pl.BlockSpec((rows, model), lambda i: (ended, 0)))
     if gq is not None:
+        has.append("q")
         operands.append(gq)
-        in_specs.append(gq_spec)
+        in_specs.append(pl.BlockSpec(gq_shape, lambda i: (gq_at, 0, 0)))
     if gkv is not None:
+        has.append("k")
         operands.extend(gkv)
-        in_specs.extend([gk_spec, gk_spec])
+        in_specs.extend([pl.BlockSpec(gk_shape, lambda i: (gkv_at, 0, 0))] * 2)
+    for name, array in (("wq", wq), ("wkv", wkv)):
+        if array is not None:
+            has.append(name)
+            operands.append(array)
+            in_specs.append(whole2(array))
     out_shape = [jax.ShapeDtypeStruct(gq_shape, bf16 if end_q else f32)]
     out_specs = [gq_spec]
     scratch = [
@@ -309,24 +358,20 @@
         scratch.append(pltpu.VMEM(gq_shape, f32))
     if end_k:
         out_shape.append(jax.ShapeDtypeStruct((nk, rows, 2 * width), bf16))
-        out_specs.append(pl.BlockSpec((nk, rows, 2 * width), full3))
+        out_specs.append(pl.BlockSpec((nk, rows, 2 * width), at_zero))
         scratch.extend([pltpu.VMEM(gk_shape, f32)] * 2)
     else:
         out_shape.extend([jax.ShapeDtypeStruct(gk_shape, f32)] * 2)
         out_specs.extend([gk_spec] * 2)
+    if end_q or end_k:
+        w_rows = width * ((1 if end_q else 0) + (2 if end_k else 0))
+        w_shape = (w_rows, model + UNIT)
+        out_shape.append(jax.ShapeDtypeStruct(w_shape, bf16 if end_q and end_k else f32))
+        out_specs.append(pl.BlockSpec(w_shape, lambda i: (0, 0)))
     pairs = heads * nq * nk * rows * rows
-    results = pl.pallas_call(
+    return pl.pallas_call(
         functools.partial(
-            backward_kernel,
-            bq,
-            heads,
-            q_span,
-            k_span,
-            rows,
-            gq is not None,
-            gkv is not None,
-            end_q,
-            end_k,
+            backward_kernel, bq, heads, q_span, k_span, rows, tuple(has), end_q, end_k
         ),
         grid=(1,),
         out_shape=tuple(out_shape),
@@ -334,18 +379,46 @@
         out_specs=out_specs,
         scratch_shapes=scratch,
         compiler_params=pltpu.CompilerParams(vmem_limit_bytes=VMEM_LIMIT),
-        cost_estimate=pl.CostEstimate(
-            flops=40 * HD * pairs,
-            bytes_accessed=(nq + nk) * rows * width * 12,
-            transcendentals=pairs,
-        ),
+        cost_estimate=pl.CostEstimate(flops=1, bytes_accessed=1, transcendentals=0),
         name="attend_backward",
     )(*operands)
-    return results[0], (results[1] if end_k else (results[1], results[2]))
-
-
-def transposed(left, right):
-    return lax.dot_general(left, right, (((0,), (0,)), ((), ())), preferred_element_type=f32)
+
+
+def input_kernel(width, kv_from, q_from, rank_ref, sum_ref, w_ref, *refs):
+    out_ref = refs[-1]
+    groups = w_ref.shape[0]
+    total = sum_ref[...]
+    for at, behind in enumerate(kv_from + q_from):
+        source = lax.rem(rank_ref[0] + groups - behind, groups)
+        if at < len(kv_from):
+            total += matmul(refs[at][...], w_ref[source, width : 3 * width, :])
+        else:
+            total += across_rows(refs[at][...], w_ref[source, :width, :])
+    out_ref[...] = total.astype(out_ref.dtype)
+
+
+def add_input_gradients(info, so_far, w_project_all, kv_pieces, q_pieces, dtype):
+    width = next(iter(kv_pieces.values())).shape[1] // 2
+    count, model = so_far.shape
+    rows = min(256, count)
+    pieces = list(kv_pieces.values()) + list(q_pieces.values())
+    by_rows = pl.BlockSpec((rows, model), lambda r: (r, 0))
+    return pl.pallas_call(
+        functools.partial(input_kernel, width, tuple(kv_pieces), tuple(q_pieces)),
+        grid=(count // rows,),
+        in_specs=[
+            pl.BlockSpec(memory_space=pltpu.SMEM),
+            by_rows,
+            pl.BlockSpec(w_project_all.shape, lambda r: (0, 0, 0)),
+        ]
+        + [pl.BlockSpec((rows, 2 * width), lambda r: (r, 0))] * len(kv_pieces)
+        + [pl.BlockSpec((width, rows), lambda r: (0, r))] * len(q_pieces),
+        out_specs=by_rows,
+        out_shape=jax.ShapeDtypeStruct(so_far.shape, dtype),
+        compiler_params=pltpu.CompilerParams(vmem_limit_bytes=VMEM_LIMIT),
+        cost_estimate=pl.CostEstimate(flops=1, bytes_accessed=1, transcendentals=0),
+        name="add_input_gradients",
+    )(info, so_far, w_project_all, *pieces)
 
 
 def ffn_forward_kernel(row_step, x_ref, w_in_ref, b_ref, w_down_ref, act_ref, slope_ref, out_ref):
@@ -389,11 +462,7 @@
             jax.ShapeDtypeStruct((count, model), f32),
         ),
         compiler_params=pltpu.CompilerParams(vmem_limit_bytes=VMEM_LIMIT),
-        cost_estimate=pl.CostEstimate(
-            flops=8 * count * model * units * groups,
-            bytes_accessed=8 * groups * count * units,
-            transcendentals=groups * count * units,
-        ),
+        cost_estimate=pl.CostEstimate(flops=1, bytes_accessed=1, transcendentals=0),
         name="ffn_forward",
     )(first_low, gathered, b_in_all, gathered)
 
@@ -434,17 +503,9 @@
             jax.ShapeDtypeStruct((count, model), f32),
         ),
         compiler_params=pltpu.CompilerParams(vmem_limit_bytes=VMEM_LIMIT),
-        cost_estimate=pl.CostEstimate(
-            flops=4 * count * model * units * groups,
-            bytes_accessed=8 * groups * count * units,
-            transcendentals=0,
-        ),
+        cost_estimate=pl.CostEstimate(flops=1, bytes_accessed=1, transcendentals=0),
         name="ffn_backward",
     )(grad_ffn_low, gathered, gathered, slopes)
-
-
-SMALL_ROWS = 32
-UNIT = 128
 
 
 def pack_kernel(
@@ -480,15 +541,15 @@
             done += take
             at += take
 
-    store(transposed(first_ref[...], gpre_ref[0]))
-    store(transposed(act_ref[0], gffn_ref[...]))
+    store(across_rows(first_ref[...], gpre_ref[0]))
+    store(across_rows(act_ref[0], gffn_ref[...]))
     store(matmul(att_ref[...], gmix_ref[...]))
     groups = pl.num_programs(0)
     stud_cols = stud_acc.shape[1]
 
     @pl.when(b == 0)
     def student():
-        whole = transposed(gstud_ref[...], second_ref[...])
+        whole = across_rows(gstud_ref[...], second_ref[...])
         for i in range(stud_acc.shape[0]):
             stud_acc[i] = whole[i * stud_cols : (i + 1) * stud_cols]
 
@@ -559,11 +620,7 @@
             pltpu.VMEM((SMALL_ROWS, model), f32),
         ],
         compiler_params=pltpu.CompilerParams(vmem_limit_bytes=VMEM_LIMIT),
-        cost_estimate=pl.CostEstimate(
-            flops=6 * count * model * units * groups,
-            bytes_accessed=8 * groups * count * units,
-            transcendentals=0,
-        ),
+        cost_estimate=pl.CostEstimate(flops=1, bytes_accessed=1, transcendentals=0),
         name="pack_gradients",
     )(
         first_low,
@@ -613,16 +670,16 @@
     return tiles
 
 
-def ring_gather(own, rank, group_size):
-    rows = own.shape[0]
-    whole = jnp.zeros((group_size * rows,) + own.shape[1:], own.dtype)
-    whole = lax.dynamic_update_slice_in_dim(whole, own, rank * rows, 0)
-    held = own
-    for s in range(1, group_size):
-        held = shift(held, 1, group_size)
-        source = (rank - s) % group_size
-        whole = lax.dynamic_update_slice_in_dim(whole, held, source * rows, 0)
-    return whole
+def exchange_add(array, other, distance):
+    moves = [(i, i ^ distance) for i in range(lax.axis_size("dp"))]
+    came = lax.ppermute(array, "dp", moves)
+    came, other = lax.optimization_barrier((came, other))
+    return (array.astype(f32) + came.astype(f32)).astype(array.dtype), other
+
+
+def place_rows(whole, rows, rank, behind, group_size):
+    source = (rank - behind) % group_size
+    return lax.dynamic_update_slice_in_dim(whole, rows, source * rows.shape[0], 0)
 
 
 def row_parts(rows):
@@ -731,8 +788,7 @@
     resid2 = ffn + b_down + first_low.astype(f32)
     second, normed2, invstd2 = normalize(resid2, ln2_gain, ln2_bias)
     second_low = second.astype(bf16)
-    leaving, w_project_all = lax.optimization_barrier((second_low, w_project_all))
-    hidden_out = lax.all_gather(leaving, "tensor", axis=0, tiled=True)
+    held = shift(second_low, 1, group_size)
 
     student_low = (against(second_low, w_stud_t) + b_stud_all.astype(f32)).astype(bf16)
     student = student_low.astype(f32)
@@ -791,6 +847,11 @@
     grad_b_down = jnp.sum(grad_resid2, axis=0)
     grad_ffn_low = grad_resid2.astype(bf16)
     grad_pre, grad_first = ffn_backward(grad_ffn_low, gathered, slopes)
+    grad_first, held = lax.optimization_barrier((grad_first, held))
+    hidden_out = jnp.zeros((slot_len, model), bf16)
+    hidden_out = place_rows(hidden_out, second_low, rank, 0, group_size)
+    hidden_out = place_rows(hidden_out, held, rank, 1, group_size)
+    held = shift(held, 1, group_size)
     grad_first = grad_first + grad_resid2
     grad_resid1, grad_ln1_gain, grad_ln1_bias = normalize_back(
         grad_first, normed1, invstd1, ln1_gain
@@ -828,77 +889,110 @@
     blocks = pack_gradients(
         dp_size, part, group_size, dense, columns, grad_w_pool * only_once, grad_w_class_t, tail
     )
-    grad_outs[0], blocks = lax.optimization_barrier((grad_outs[0], blocks))
-    part_of = functools.partial(attend_backward, info, wide_k, wide_v, projected_t)
+    *grad_outs, blocks, w_project_all = lax.optimization_barrier(
+        (*grad_outs, blocks, w_project_all)
+    )
+    reduced = lax.psum_scatter(
+        blocks.reshape(dp_size * group_size, part, model), "dp", scatter_dimension=0, tiled=True
+    )
+
+    part_of = functools.partial(attend_backward, info, wide_k, wide_v, projected_t, hidden_rot)
     others = (1, group_size)
     own_side = (grad_outs[0][None], outs[0][None], lses[0][None])
+    gq_own, gk_others, gv_others = part_of(*own_side, (0, 1), others)
+    gq_own, held, grad_outs[1] = lax.optimization_barrier((gq_own, held, grad_outs[1]))
+    hidden_out = place_rows(hidden_out, held, rank, 2, group_size)
+    held = shift(held, 1, group_size)
     other_side = tuple(jnp.stack(side[1:]) for side in (grad_outs, outs, lses))
-    gq_own, gkv_others = part_of(*own_side, (0, 1), others, None, None, False, False)
-    blocks, hidden_out, gq_own = lax.optimization_barrier((blocks, hidden_out, gq_own))
-    reduced = lax.psum_scatter(
-        blocks.reshape(dp_size * group_size, part, model), "dp", scatter_dimension=0, tiled=True
-    )
     gq_others = None
-    grad_kv = [None] * group_size
-    kv_arrived = [None] * group_size
-    for s in range(1, group_size):
-        so_far = tuple(side[s - 1 : s] for side in gkv_others)
-        gq_others, low = part_of(
-            *other_side, others, (s, s + 1), gq_others, so_far, False, True
+    w_kv_sum = None
+    kv_arrived = {}
+    order = sorted(range(1, group_size), key=lambda s: -min(s, group_size - s))
+    for step, s in enumerate(order):
+        gq_others, low, w_kv_sum = part_of(
+            *other_side,
+            others,
+            (s, s + 1),
+            gq=gq_others,
+            gkv=(gk_others, gv_others),
+            wkv=w_kv_sum,
+            gkv_at=s - 1,
+            end_k=True,
         )
-        grad_kv[s] = low[0]
-        kv_arrived[s] = shift(grad_kv[s], s, group_size)
-    reduced, gq_others = lax.optimization_barrier((reduced, gq_others))
-    reduced = lax.psum_scatter(reduced, "tensor", scatter_dimension=0, tiled=True)
+        kv_arrived[s] = shift(low[0], s, group_size)
+        if step == 1:
+            earlier = order[0]
+            reduced, held, gq_others, kv_arrived[earlier] = lax.optimization_barrier(
+                (reduced, held, gq_others, kv_arrived[earlier])
+            )
+            reduced = lax.psum_scatter(reduced, "tensor", scatter_dimension=0, tiled=True)
+            hidden_out = place_rows(hidden_out, held, rank, 3, group_size)
     gkv_own = None
-    grad_q = [None] * group_size
-    q_arrived = [None] * group_size
-    for s in range(1, group_size):
-        side = (grad_outs[s][None], outs[s][None], lses[s][None])
-        low, gkv_own = part_of(
-            *side, (s, s + 1), (0, 1), gq_others[s - 1 : s], gkv_own, True, False
+    w_q_sum = None
+    q_arrived = {}
+    for step, s in enumerate(order):
+        low, *gkv_own, w_q_sum = part_of(
+            grad_outs[s][None],
+            outs[s][None],
+            lses[s][None],
+            (s, s + 1),
+            (0, 1),
+            gq=gq_others,
+            gkv=gkv_own,
+            wq=w_q_sum,
+            gq_at=s - 1,
+            end_q=True,
         )
-        grad_q[s] = low[0]
-        q_arrived[s] = shift(grad_q[s], s, group_size)
-    reduced, gkv_own = lax.optimization_barrier((reduced, gkv_own))
+        q_arrived[s] = shift(low[0], s, group_size)
+        if step < 2:
+            earlier = order[step + 1]
+            kv_arrived[earlier], w_q_sum = lax.optimization_barrier(
+                (kv_arrived[earlier], w_q_sum)
+            )
+    grad_resid1, w_q_sum = lax.optimization_barrier((grad_resid1, w_q_sum))
+    grad_in_own = add_input_gradients(
+        info, grad_resid1, w_project_all, kv_arrived, {}, f32
+    )
+    gq_own, reduced, grad_in_own, *arrivals = lax.optimization_barrier(
+        (gq_own, reduced, grad_in_own, *q_arrived.values())
+    )
+    q_arrived = dict(zip(q_arrived, arrivals))
     reduced = lax.all_gather(reduced[0], "dp", axis=0, tiled=True)
-    low_q, low_kv = part_of(*own_side, (0, 1), (0, 1), gq_own, gkv_own, True, True)
-    grad_q[0] = q_arrived[0] = low_q[0]
-    grad_kv[0] = kv_arrived[0] = low_kv[0]
-
-    grad_in_own = grad_resid1
-    for s in range(group_size):
-        source = (rank - s) % group_size
-        w_source = lax.dynamic_index_in_dim(w_project_all, source, 0, keepdims=False)
-        grad_in_own = (
-            grad_in_own
-            + across_rows(q_arrived[s], w_source[:width])
-            + matmul(kv_arrived[s], w_source[width : 3 * width])
-        )
-    grad_in = ring_gather(grad_in_own.astype(bf16), rank, group_size)
-
-    grad_w_q = None
-    grad_w_kv = None
-    grad_b_q = None
-    grad_b_kv = None
-    for s in range(group_size):
-        rows_here = hidden_rot[s * own_count : (s + 1) * own_count]
-        more_q = lax.dot_general(
-            grad_q[s], rows_here, (((1,), (0,)), ((), ())), preferred_element_type=f32
-        )
-        more_kv = across_rows(grad_kv[s], rows_here)
-        more_bq = jnp.sum(grad_q[s], axis=1, dtype=f32)
-        more_bkv = jnp.sum(grad_kv[s], axis=0, dtype=f32)
-        grad_w_q = more_q if s == 0 else grad_w_q + more_q
-        grad_w_kv = more_kv if s == 0 else grad_w_kv + more_kv
-        grad_b_q = more_bq if s == 0 else grad_b_q + more_bq
-        grad_b_kv = more_bkv if s == 0 else grad_b_kv + more_bkv
-    late = jnp.concatenate(
-        [grad_w_q, grad_w_kv, pad_row(grad_b_q), pad_row(grad_b_kv[width:])], axis=0
-    ).astype(bf16)
-    late, reduced = lax.optimization_barrier((late, reduced))
+    low_q, low_kv, late = part_of(
+        *own_side,
+        (0, 1),
+        (0, 1),
+        gq=gq_own,
+        gkv=gkv_own,
+        wq=w_q_sum,
+        wkv=w_kv_sum,
+        end_q=True,
+        end_k=True,
+    )
+    late, grad_in_own = exchange_add(late, grad_in_own, 1)
+    q_arrived[0] = low_q[0]
+    grad_in_own = add_input_gradients(
+        info, grad_in_own, w_project_all, {0: low_kv[0]}, q_arrived, bf16
+    )
+    grad_in, grad_in_own = lax.optimization_barrier((hidden_rot, grad_in_own))
+    held = shift(grad_in_own, 1, group_size)
+    grad_in = place_rows(grad_in, grad_in_own, rank, 0, group_size)
     small_own = reduced[small_at : small_at + SMALL_ROWS]
-    small = group_tiles(small_own[:, : 4 * UNIT], rank, group_size).astype(f32)
+    small = group_tiles(small_own[:, : 4 * UNIT], rank, group_size)
+    late, held = exchange_add(late, held, 2)
+    grad_in = place_rows(grad_in, held, rank, 1, group_size)
+    held = shift(held, 1, group_size)
+    distance = 4
+    while distance < dp_size:
+        late, held = exchange_add(late, held, distance)
+        distance *= 2
+    held, small = lax.optimization_barrier((held, small))
+    for s in range(2, group_size):
+        grad_in = place_rows(grad_in, held, rank, s, group_size)
+        if s < group_size - 1:
+            held = shift(held, 1, group_size)
+    late = late.astype(f32)
+    small = small.astype(f32)
     small_own = small_own[:, 4 * UNIT :].astype(f32)
     grad_w_pool = small[:, :, :UNIT].reshape(grad_w_pool.shape)
     column_share = -(-columns.size // (UNIT * group_size))
@@ -914,17 +1008,16 @@
     grad_b_in = small_own[: hidden_width // UNIT, :UNIT].reshape(-1)
     grad_b_stud = lax.dynamic_slice_in_dim(small_own[0, UNIT:], rank * stu_cols, stu_cols, 0)
 
-    late = lax.psum(late, "dp").astype(f32)
     reduced = reduced.astype(f32)
     return (
         hidden_out,
         logits,
         grad_in,
-        late[:width].T,
-        late[3 * width, :width],
-        late[width : 2 * width].T,
-        late[2 * width : 3 * width].T,
-        late[3 * width + 1, :width],
+        late[:width, :model].T,
+        late[:width, model],
+        late[width : 2 * width, :model].T,
+        late[2 * width :, :model].T,
+        late[2 * width :, model],
         reduced[at : at + width],
         columns[0],
         columns[1],

time: 748 us -> 634 us (0.85)
  waiting for transfers between devices: 337 us -> 109 us
  Pallas kernels: 176 us -> 356 us
  matrix products: 54.1 us -> 13.1 us
  starting transfers between devices: 53.3 us -> 43 us
    pallas_call x8, Pallas kernels: 52.1 us -> 181 us  [attend_backward(): pl.pallas_call(functools.partial(backward_kernel, bq, heads, q_span, k_sp...]
    ppermute x24 -> x27, waiting for transfers between devices: 191 us -> 61.7 us  [shift(): return lax.ppermute(array, 'tensor', moves)]
    psum x1 -> x0, waiting for transfers between devices: 72.9 us -> none  [body(): late = lax.psum(late, 'dp').astype(f32)]
    ppermute x0 -> x3, waiting for transfers between devices: none -> 46.9 us  [exchange_add(): came = lax.ppermute(array, 'dp', moves)]
    all_gather x1 -> x0, waiting for transfers between devices: 35.9 us -> none  [body(): hidden_out = lax.all_gather(leaving, 'tensor', axis=0, tiled=True)]
    pallas_call x4, Pallas kernels: 48.3 us -> 84 us  [attend_forward(): pl.pallas_call(functools.partial(forward_kernel, bq, bk, heads), grid=(1,...]
    all_gather x2, waiting for transfers between devices: 25.8 us -> 0.01 us  [spread_gather(): whole = lax.all_gather(mine, ('tensor', 'dp'), axis=0, tiled=True)]
    dot_general x9 -> x1, matrix products: 22 us -> 3.93 us  [across_rows(): lax.dot_general(left, right, (((0,), (0,)), ((), ())), preferred_element_...]
  transfers between devices with their start and end apart: 31 -> 35, of which waited for: 14 -> 12; matrix products, arithmetic and copies ran while one was open for 16% -> 14% of each run, Pallas kernels for 24% -> 55%
where the time goes in v3:
time: 634 us; the launch traced here: 624 us
  Pallas kernels  356 us (56%)
  waiting for transfers between devices  109 us (17%)
  local copies, waits for them, and re-layouts  46.8 us (7%)
  starting transfers between devices  43 us (7%)
  other arithmetic  39.1 us (6%)
  between operations  17.5 us (3%)
  matrix products  13.1 us (2%)
    pallas_call x8, Pallas kernels, attend_backward(): pl.pallas_call(functools.partial(backward_kernel, bq, heads, q_span, k_sp...  181 us
    pallas_call x4, Pallas kernels, attend_forward(): pl.pallas_call(functools.partial(forward_kernel, bq, bk, heads), grid=(1,...  84 us
    ppermute x27, waiting for transfers between devices, shift(): return lax.ppermute(array, 'tensor', moves)  61.7 us
    ppermute x3, waiting for transfers between devices, exchange_add(): came = lax.ppermute(array, 'dp', moves)  46.9 us
    ppermute x27, starting transfers between devices, shift(): return lax.ppermute(array, 'tensor', moves)  39.5 us
    pallas_call x1, Pallas kernels, ffn_forward(): pl.pallas_call(functools.partial(ffn_forward_kernel, min(256, count)), gr...  22.7 us
    pallas_call x1, Pallas kernels, ffn_backward(): pl.pallas_call(functools.partial(ffn_backward_kernel, min(256, count)), g...  21.2 us
    pallas_call x1, Pallas kernels, pack_gradients(): pl.pallas_call(functools.partial(pack_kernel, dp_size, part), grid=(group...  20.1 us
  transfers between devices with their start and end apart: 35, of which 12 were waited for; matrix products, arithmetic and copies ran while one was open for 14% of the time, Pallas kernels for 55%

profile of v3, /device:TPU:0, one launch (start us, length us, event | category | flops | bytes accessed | tf_op | source)
XLA Modules:
  0.0 624.0 jit_solution(18407250215549596408)
XLA Ops:
  10.0 3.0 collective-permute-start.3
  24.2 11.3 %project.1 = (bf16[4096,768]{1,0:T(8,128)(2,1)}, bf16[4096,256]{1,0:T(8,128)(2,1)}, bf16[4096,256]{1,0:T(8,128)(2,1)}, bf16[576,4096]{1,0:T(8,128)(2,1)}) custom-call(s32[7]{0:T(128)} %pad_add_fusion.info_ref.refs_0_.rank_ref, bf16[4096,768]{1,0:T(8,128)(2,1)} %h_ref.1, bf16[768,384]{1,0:T(8,128)(2,1)} %pad_maximum_fusion.3.wkv_ref, ...), custom_call_target="tpu_custom_call" | custom-call | flops 1 | bytes 1 | tf_op jit(solution)/shard_map/project/pallas_call | solution.py:61
  35.5 20.9 %attend_forward.5 = (bf16[192,1024]{1,0:T(8,128)(2,1)}, f32[8,1024]{1,0:T(8,128)}) custom-call(s32[7]{0:T(128)} %pad_add_fusion.info_ref.refs_0_.rank_ref, bf16[4096,256]{1,0:T(8,128)(2,1)} %get-tuple-element.106.k_ref.refs_1_, bf16[576,4096]{1,0:T(8,128)(2,1)} %get-tuple-element.107.qt_ref.vt_ref.refs_3_.refs_4_, ...), custom_call_target="tpu_custom_call" | custom-call | flops 1 | bytes 1 | tf_op jit(solution)/shard_map/attend_forward/pallas_call | solution.py:146
  57.1 21.0 %attend_forward.6 = (bf16[192,1024]{1,0:T(8,128)(2,1)}, f32[8,1024]{1,0:T(8,128)}) custom-call(s32[7]{0:T(128)} %pad_add_fusion.info_ref.refs_0_.rank_ref, bf16[4096,256]{1,0:T(8,128)(2,1)} %get-tuple-element.106.k_ref.refs_1_, bf16[576,4096]{1,0:T(8,128)(2,1)} %get-tuple-element.107.qt_ref.vt_ref.refs_3_.refs_4_, ...), custom_call_target="tpu_custom_call" | custom-call | flops 1 | bytes 1 | tf_op jit(solution)/shard_map/attend_forward/pallas_call | solution.py:146
  79.8 21.0 %attend_forward.4 = (bf16[192,1024]{1,0:T(8,128)(2,1)}, f32[8,1024]{1,0:T(8,128)}) custom-call(s32[7]{0:T(128)} %pad_add_fusion.info_ref.refs_0_.rank_ref, bf16[4096,256]{1,0:T(8,128)(2,1)} %get-tuple-element.106.k_ref.refs_1_, bf16[576,4096]{1,0:T(8,128)(2,1)} %get-tuple-element.107.qt_ref.vt_ref.refs_3_.refs_4_, ...), custom_call_target="tpu_custom_call" | custom-call | flops 1 | bytes 1 | tf_op jit(solution)/shard_map/attend_forward/pallas_call | solution.py:146
  100.9 21.0 %attend_forward.7 = (bf16[192,1024]{1,0:T(8,128)(2,1)}, f32[8,1024]{1,0:T(8,128)}) custom-call(s32[7]{0:T(128)} %pad_add_fusion.info_ref.refs_0_.rank_ref, bf16[4096,256]{1,0:T(8,128)(2,1)} %get-tuple-element.106.k_ref.refs_1_, bf16[576,4096]{1,0:T(8,128)(2,1)} %get-tuple-element.107.qt_ref.vt_ref.refs_3_.refs_4_, ...), custom_call_target="tpu_custom_call" | custom-call | flops 1 | bytes 1 | tf_op jit(solution)/shard_map/attend_forward/pallas_call | solution.py:146
  129.4 5.6 collective-permute-done.2
  137.1 3.9 fusion.41
  143.5 22.7 %ffn_forward.1 = (bf16[4,1024,768]{2,1,0:T(8,128)(2,1)}, bf16[4,1024,768]{2,1,0:T(8,128)(2,1)}, f32[1024,768]{1,0:T(8,128)}) custom-call(bf16[1024,768]{1,0:T(8,128)(2,1)} %add_convert_fusion.1.x_ref.first_ref, bf16[4,1792,768]{2,1,0:T(8,128)(2,1)} %bitcast.163, bf16[4,1,768]{2,1,0:T(2,128)(2,1)} %slice.147.b_ref, bf16[4,1792,768]{2,1,0:T(8,128)(2,1)} %bitcast.164), custom_call_target="tpu_custom_call" | custom-call | flops 1 | bytes 1 | tf_op jit(solution)/shard_map/ffn_forward/pallas_call | solution.py:449
  177.2 3.5 collective-permute-start.7
  191.6 5.2 multiply_reduce_fusion
  200.9 21.2 %ffn_backward.1 = (bf16[4,1024,768]{2,1,0:T(8,128)(2,1)}, f32[1024,768]{1,0:T(8,128)}) custom-call(bf16[1024,768]{1,0:T(8,128)(2,1)} %convert_element_type.119.g_ref.gffn_ref, bf16[4,1792,768]{2,1,0:T(8,128)(2,1)} %bitcast.165, bf16[4,1792,768]{2,1,0:T(8,128)(2,1)} %bitcast.166, bf16[4,1024,768]{2,1,0:T(8,128)(2,1)} %get-tuple-element.113.slope_ref), custom_call_target="tpu_custom_call" | custom-call | flops 1 | bytes 1 | tf_op jit(solution)/shard_map/ffn_backward/pallas_call | solution.py:491
  223.8 3.8 multiply_reduce_fusion.1
  239.2 20.1 %pack_gradients.1 = bf16[8,4,224,768]{3,2,1,0:T(8,128)(2,1)} custom-call(bf16[1024,768]{1,0:T(8,128)(2,1)} %add_convert_fusion.1.x_ref.first_ref, bf16[4,1024,768]{2,1,0:T(8,128)(2,1)} %get-tuple-element.118.gpre_ref, bf16[4,1024,768]{2,1,0:T(8,128)(2,1)} %get-tuple-element.119.act_ref, bf16[1024,768]{1,0:T(8,128)(2,1)} %convert_element_type.119.g_ref.gffn_ref, ...), custom_call_target="tpu_custom_call" | custom-call | flops 1 | bytes 1 | tf_op jit(solution)/shard_map/pack_gradients/pallas_call | solution.py:599
  259.3 4.5 collective-permute-done.11
  264.8 31.2 %attend_backward.8 = (f32[1,192,1024]{2,1,0:T(8,128)}, f32[3,1024,256]{2,1,0:T(8,128)}, f32[3,1024,256]{2,1,0:T(8,128)}) custom-call(s32[7]{0:T(128)} %pad_add_fusion.info_ref.refs_0_.rank_ref, bf16[4096,256]{1,0:T(8,128)(2,1)} %get-tuple-element.106.k_ref.refs_1_, bf16[4096,256]{1,0:T(8,128)(2,1)} %get-tuple-element.116.refs_2_, ...), custom_call_target="tpu_custom_call" | custom-call | flops 1 | bytes 1 | tf_op jit(solution)/shard_map/attend_backward/pallas_call | solution.py:372
  304.8 30.9 %attend_backward.9 = (f32[3,192,1024]{2,1,0:T(8,128)}, bf16[1,1024,384]{2,1,0:T(8,128)(2,1)}, f32[384,896]{1,0:T(8,128)}) custom-call(s32[7]{0:T(128)} %pad_add_fusion.info_ref.refs_0_.rank_ref, bf16[4096,256]{1,0:T(8,128)(2,1)} %get-tuple-element.106.k_ref.refs_1_, bf16[4096,256]{1,0:T(8,128)(2,1)} %get-tuple-element.116.refs_2_, ...), custom_call_target="tpu_custom_call" | custom-call | flops 1 | bytes 1 | tf_op jit(solution)/shard_map/attend_backward/pallas_call | solution.py:372
  337.8 31.8 %attend_backward.10 = (f32[3,192,1024]{2,1,0:T(8,128)}, bf16[1,1024,384]{2,1,0:T(8,128)(2,1)}, f32[384,896]{1,0:T(8,128)}) custom-call(s32[7]{0:T(128)} %pad_add_fusion.info_ref.refs_0_.rank_ref, bf16[4096,256]{1,0:T(8,128)(2,1)} %get-tuple-element.106.k_ref.refs_1_, bf16[4096,256]{1,0:T(8,128)(2,1)} %get-tuple-element.116.refs_2_, ...), custom_call_target="tpu_custom_call" | custom-call | flops 1 | bytes 1 | tf_op jit(solution)/shard_map/attend_backward/pallas_call | solution.py:372
  370.0 31.6 %attend_backward.11 = (f32[3,192,1024]{2,1,0:T(8,128)}, bf16[1,1024,384]{2,1,0:T(8,128)(2,1)}, f32[384,896]{1,0:T(8,128)}) custom-call(s32[7]{0:T(128)} %pad_add_fusion.info_ref.refs_0_.rank_ref, bf16[4096,256]{1,0:T(8,128)(2,1)} %get-tuple-element.106.k_ref.refs_1_, bf16[4096,256]{1,0:T(8,128)(2,1)} %get-tuple-element.116.refs_2_, ...), custom_call_target="tpu_custom_call" | custom-call | flops 1 | bytes 1 | tf_op jit(solution)/shard_map/attend_backward/pallas_call | solution.py:372
  401.6 3.8 collective-permute-start.17
  405.4 12.9 %attend_backward.12 = (bf16[1,192,1024]{2,1,0:T(8,128)(2,1)}, f32[1,1024,256]{2,1,0:T(8,128)}, f32[1,1024,256]{2,1,0:T(8,128)}, f32[192,896]{1,0:T(8,128)}) custom-call(s32[7]{0:T(128)} %pad_add_fusion.info_ref.refs_0_.rank_ref, bf16[4096,256]{1,0:T(8,128)(2,1)} %get-tuple-element.106.k_ref.refs_1_, bf16[4096,256]{1,0:T(8,128)(2,1)} %get-tuple-element.116.refs_2_, ...), custom_call_target="tpu_custom_call" | custom-call | flops 1 | bytes 1 | tf_op jit(solution)/shard_map/attend_backward/pallas_call | solution.py:372
  418.3 14.3 %attend_backward.13 = (bf16[1,192,1024]{2,1,0:T(8,128)(2,1)}, f32[1,1024,256]{2,1,0:T(8,128)}, f32[1,1024,256]{2,1,0:T(8,128)}, f32[192,896]{1,0:T(8,128)}) custom-call(s32[7]{0:T(128)} %pad_add_fusion.info_ref.refs_0_.rank_ref, bf16[4096,256]{1,0:T(8,128)(2,1)} %get-tuple-element.106.k_ref.refs_1_, bf16[4096,256]{1,0:T(8,128)(2,1)} %get-tuple-element.116.refs_2_, ...), custom_call_target="tpu_custom_call" | custom-call | flops 1 | bytes 1 | tf_op jit(solution)/shard_map/attend_backward/pallas_call | solution.py:372
  435.5 13.9 %attend_backward.14 = (bf16[1,192,1024]{2,1,0:T(8,128)(2,1)}, f32[1,1024,256]{2,1,0:T(8,128)}, f32[1,1024,256]{2,1,0:T(8,128)}, f32[192,896]{1,0:T(8,128)}) custom-call(s32[7]{0:T(128)} %pad_add_fusion.info_ref.refs_0_.rank_ref, bf16[4096,256]{1,0:T(8,128)(2,1)} %get-tuple-element.106.k_ref.refs_1_, bf16[4096,256]{1,0:T(8,128)(2,1)} %get-tuple-element.116.refs_2_, ...), custom_call_target="tpu_custom_call" | custom-call | flops 1 | bytes 1 | tf_op jit(solution)/shard_map/attend_backward/pallas_call | solution.py:372
  450.5 7.6 %add_input_gradients.2.sum_ref = f32[1024,768]{1,0:T(8,128)} custom-call(s32[7]{0:T(128)} %pad_add_fusion.info_ref.refs_0_.rank_ref, f32[1024,768]{1,0:T(8,128)} %copy-done.4, bf16[4,640,768]{2,1,0:T(8,128)(2,1)} %bitcast.168, bf16[1024,384]{1,0:T(8,128)(2,1)} %copy-done.27, bf16[1024,384]{1,0:T(8,128)(2,1)} %copy-done.28, bf16[1024,384]{1,0:T(8,128)(2,1)} %copy-done.29), custom_call_target="tpu_custom_call" | custom-call | flops 1 | bytes 1 | tf_op jit(solution)/shard_map/add_input_gradients/pallas_call | solution.py:406
  458.1 5.3 collective-permute-done.20.refs_3_
  463.4 14.9 %attend_backward.15 = (bf16[1,192,1024]{2,1,0:T(8,128)(2,1)}, bf16[1,1024,384]{2,1,0:T(8,128)(2,1)}, bf16[576,896]{1,0:T(8,128)(2,1)}) custom-call(s32[7]{0:T(128)} %pad_add_fusion.info_ref.refs_0_.rank_ref, bf16[4096,256]{1,0:T(8,128)(2,1)} %get-tuple-element.106.k_ref.refs_1_, bf16[4096,256]{1,0:T(8,128)(2,1)} %get-tuple-element.116.refs_2_, ...), custom_call_target="tpu_custom_call" | custom-call | flops 1 | bytes 1 | tf_op jit(solution)/shard_map/attend_backward/pallas_call | solution.py:372
  482.2 7.6 %add_input_gradients.3 = bf16[1024,768]{1,0:T(8,128)(2,1)} custom-call(s32[7]{0:T(128)} %pad_add_fusion.info_ref.refs_0_.rank_ref, f32[1024,768]{1,0:T(8,128)} %add_input_gradients.2.sum_ref, bf16[4,640,768]{2,1,0:T(8,128)(2,1)} %bitcast.169, bf16[1024,384]{1,0:T(8,128)(2,1)} %bitcast.193, bf16[192,1024]{1,0:T(8,128)(2,1)} %copy-done.31, ...), custom_call_target="tpu_custom_call" | custom-call | flops 1 | bytes 1 | tf_op jit(solution)/shard_map/add_input_gradients/pallas_call | solution.py:406
  493.4 31.9 %collective-permute-done.22 = bf16[576,896]{1,0:T(8,128)(2,1)S(1)} collective-permute-done((bf16[576,896]{1,0:T(8,128)(2,1)S(1)}, bf16[576,896]{1,0:T(8,128)(2,1)S(1)}, u32[]{:S(2)}, u32[]{:S(2)}) %collective-permute-start.22) | collective-permute-done | bytes 1032224 | tf_op jit(solution)/shard_map/ppermute | solution.py:675
  542.0 12.2 %collective-permute-done.24 = bf16[576,896]{1,0:T(8,128)(2,1)} collective-permute-done((bf16[576,896]{1,0:T(8,128)(2,1)S(1)}, bf16[576,896]{1,0:T(8,128)(2,1)}, u32[]{:S(2)}, u32[]{:S(2)}) %collective-permute-start.24) | collective-permute-done | bytes 1032224 | tf_op jit(solution)/shard_map/ppermute | solution.py:675
  554.2 11.9 %collective-permute-done.25 = bf16[1024,768]{1,0:T(8,128)(2,1)} collective-permute-done((bf16[1024,768]{1,0:T(8,128)(2,1)}, bf16[1024,768]{1,0:T(8,128)(2,1)}, u32[]{:S(2)}, u32[]{:S(2)}) %collective-permute-start.25) | collective-permute-done | bytes 1572896 | tf_op jit(solution)/shard_map/ppermute | solution.py:662
  570.5 3.5 collective-permute-start.28
  589.2 26.8 %collective-permute-done.29 = bf16[1024,768]{1,0:T(8,128)(2,1)S(1)} collective-permute-done((bf16[1024,768]{1,0:T(8,128)(2,1)}, bf16[1024,768]{1,0:T(8,128)(2,1)S(1)}, u32[]{:S(2)}, u32[]{:S(2)}) %collective-permute-start.29) | collective-permute-done | bytes 1572896 | tf_op jit(solution)/shard_map/ppermute | solution.py:662
  (295 shorter events, 125.7 us)
Async XLA Ops:
  7.3 128.4 %all-gather.5.cloned.1.call-start = ((), (), s32[]{:S(2)}) async-start(), calls=%async_computation.2 | async-start | bytes 11354112 | tf_op jit(solution)/shard_map/all_gather | solution.py:695
  9.7 249.6 %all-gather.7.cloned.1.call-start = ((), (), s32[]{:S(2)}) async-start(), calls=%async_computation.3 | async-start | bytes 4055040 | tf_op jit(solution)/shard_map/all_gather | solution.py:695
  10.0 114.2 %collective-permute-start.3 = (bf16[40,768]{1,0:T(8,128)(2,1)S(1)}, bf16[40,768]{1,0:T(8,128)(2,1)S(1)}, u32[]{:S(2)}, u32[]{:S(2)}) collective-permute-start(bf16[40,768]{1,0:T(8,128)(2,1)S(1)} %fusion.17), channel_id=1, source_target_pairs={{0,1},{1,2},{2,3},{3,0},{4,5},{5,6},{6,7},{7,4},{8,9},{9,10},{10,1... | collective-permute-start | bytes 184328 | tf_op jit(solution)/shard_map/ppermute | solution.py:662
  13.0 114.1 %collective-permute-start.4 = (bf16[40,768]{1,0:T(8,128)(2,1)S(1)}, bf16[40,768]{1,0:T(8,128)(2,1)S(1)}, u32[]{:S(2)}, u32[]{:S(2)}) collective-permute-start(bf16[40,768]{1,0:T(8,128)(2,1)S(1)} %fusion.17), channel_id=1, source_target_pairs={{0,2},{1,3},{2,0},{3,1},{4,6},{5,7},{6,4},{7,5},{8,10},{9,11},{10,... | collective-permute-start | bytes 184328 | tf_op jit(solution)/shard_map/ppermute | solution.py:662
  15.6 111.5 %collective-permute-start.5 = (bf16[40,768]{1,0:T(8,128)(2,1)S(1)}, bf16[40,768]{1,0:T(8,128)(2,1)S(1)}, u32[]{:S(2)}, u32[]{:S(2)}) collective-permute-start(bf16[40,768]{1,0:T(8,128)(2,1)S(1)} %fusion.17), channel_id=1, source_target_pairs={{0,3},{1,0},{2,1},{3,2},{4,7},{5,4},{6,5},{7,6},{8,11},{9,8},{10,9... | collective-permute-start | bytes 184328 | tf_op jit(solution)/shard_map/ppermute | solution.py:662
  56.5 71.3 %collective-permute-start = (bf16[192,1024]{1,0:T(8,128)(2,1)}, bf16[192,1024]{1,0:T(8,128)(2,1)S(1)}, u32[]{:S(2)}, u32[]{:S(2)}) collective-permute-start(bf16[192,1024]{1,0:T(8,128)(2,1)} %get-tuple-element.109), channel_id=1, source_target_pairs={{0,1},{1,2},{2,3},{3,0},{4,5},{5,6},{6,7},{7,4},{8,9},{9,10},{10,1... | collective-permute-start | bytes 1179656 | tf_op jit(solution)/shard_map/ppermute | solution.py:662
  78.1 50.5 %collective-permute-start.1 = (bf16[192,1024]{1,0:T(8,128)(2,1)}, bf16[192,1024]{1,0:T(8,128)(2,1)S(1)}, u32[]{:S(2)}, u32[]{:S(2)}) collective-permute-start(bf16[192,1024]{1,0:T(8,128)(2,1)} %get-tuple-element.110), channel_id=1, source_target_pairs={{0,2},{1,3},{2,0},{3,1},{4,6},{5,7},{6,4},{7,5},{8,10},{9,11},{10,... | collective-permute-start | bytes 1179656 | tf_op jit(solution)/shard_map/ppermute | solution.py:662
  79.3 290.3 %reduce-scatter.3.cloned.1.call-start = ((), (), s32[]{:S(2)}) async-start(), calls=%async_computation.4 | async-start | bytes 12386304 | tf_op jit(solution)/shard_map/reduce_scatter | solution.py:895
  124.2 10.7 %collective-permute-start.2 = (bf16[192,1024]{1,0:T(8,128)(2,1)}, bf16[192,1024]{1,0:T(8,128)(2,1)S(1)}, u32[]{:S(2)}, u32[]{:S(2)}) collective-permute-start(bf16[192,1024]{1,0:T(8,128)(2,1)} %get-tuple-element.111), channel_id=1, source_target_pairs={{0,3},{1,0},{2,1},{3,2},{4,7},{5,4},{6,5},{7,6},{8,11},{9,8},{10,9... | collective-permute-start | bytes 1179656 | tf_op jit(solution)/shard_map/ppermute | solution.py:662
  175.9 7.7 %collective-permute-start.6 = (f32[8,128]{1,0:T(8,128)S(1)}, f32[8,128]{1,0:T(8,128)S(1)}, u32[]{:S(2)}, u32[]{:S(2)}) collective-permute-start(f32[8,128]{1,0:T(8,128)S(1)} %maximum_maximum_fusion), channel_id=1, source_target_pairs={{0,1},{1,2},{2,3},{3,0},{4,5},{5,6},{6,7},{7,4},{8,9},{9,10},{10,1... | collective-permute-start | bytes 12296 | tf_op jit(solution)/shard_map/ppermute | solution.py:662
  181.4 42.4 %collective-permute-start.9 = (bf16[1024,768]{1,0:T(8,128)(2,1)}, bf16[1024,768]{1,0:T(8,128)(2,1)}, u32[]{:S(2)}, u32[]{:S(2)}) collective-permute-start(bf16[1024,768]{1,0:T(8,128)(2,1)} %copy-done.7), channel_id=1, source_target_pairs={{0,1},{1,2},{2,3},{3,0},{4,5},{5,6},{6,7},{7,4},{8,9},{9,10},{10,1... | collective-permute-start | bytes 4718600 | tf_op jit(solution)/shard_map/ppermute | solution.py:662
  233.2 26.1 %collective-permute-start.10 = (bf16[192,1024]{1,0:T(8,128)(2,1)S(1)}, bf16[192,1024]{1,0:T(8,128)(2,1)S(1)}, u32[]{:S(2)}, u32[]{:S(2)}) collective-permute-start(bf16[192,1024]{1,0:T(8,128)(2,1)S(1)} %get-tuple-element.233), channel_id=1, source_target_pairs={{0,3},{1,0},{2,1},{3,2},{4,7},{5,4},{6,5},{7,6},{8,11},{9,8},{10,9... | collective-permute-start | bytes 1179656 | tf_op jit(solution)/shard_map/ppermute | solution.py:662
  235.2 28.7 %collective-permute-start.11 = (bf16[192,1024]{1,0:T(8,128)(2,1)S(1)}, bf16[192,1024]{1,0:T(8,128)(2,1)S(1)}, u32[]{:S(2)}, u32[]{:S(2)}) collective-permute-start(bf16[192,1024]{1,0:T(8,128)(2,1)S(1)} %get-tuple-element.232), channel_id=1, source_target_pairs={{0,2},{1,3},{2,0},{3,1},{4,6},{5,7},{6,4},{7,5},{8,10},{9,11},{10,... | collective-permute-start | bytes 1179656 | tf_op jit(solution)/shard_map/ppermute | solution.py:662
  235.2 28.7 %collective-permute-start.12 = (bf16[192,1024]{1,0:T(8,128)(2,1)S(1)}, bf16[192,1024]{1,0:T(8,128)(2,1)S(1)}, u32[]{:S(2)}, u32[]{:S(2)}) collective-permute-start(bf16[192,1024]{1,0:T(8,128)(2,1)S(1)} %get-tuple-element.231), channel_id=1, source_target_pairs={{0,1},{1,2},{2,3},{3,0},{4,5},{5,6},{6,7},{7,4},{8,9},{9,10},{10,1... | collective-permute-start | bytes 1179656 | tf_op jit(solution)/shard_map/ppermute | solution.py:662
  264.6 198.8 %reduce-scatter.5.cloned.1.call-start = ((), (), s32[]{:S(2)}) async-start(), calls=%async_computation.5 | async-start | bytes 1720320 | tf_op jit(solution)/shard_map/reduce_scatter | solution.py:928
  264.6 33.6 %collective-permute-start.13 = (bf16[1024,768]{1,0:T(8,128)(2,1)}, bf16[1024,768]{1,0:T(8,128)(2,1)S(1)}, u32[]{:S(2)}, u32[]{:S(2)}) collective-permute-start(bf16[1024,768]{1,0:T(8,128)(2,1)} %collective-permute-done.9), channel_id=1, source_target_pairs={{0,1},{1,2},{2,3},{3,0},{4,5},{5,6},{6,7},{7,4},{8,9},{9,10},{10,1... | collective-permute-start | bytes 4718600 | tf_op jit(solution)/shard_map/ppermute | solution.py:662
  298.2 71.4 %collective-permute-start.14 = (bf16[1024,768]{1,0:T(8,128)(2,1)S(1)}, bf16[1024,768]{1,0:T(8,128)(2,1)}, u32[]{:S(2)}, u32[]{:S(2)}) collective-permute-start(bf16[1024,768]{1,0:T(8,128)(2,1)S(1)} %collective-permute-done.13), channel_id=1, source_target_pairs={{0,1},{1,2},{2,3},{3,0},{4,5},{5,6},{6,7},{7,4},{8,9},{9,10},{10,1... | collective-permute-start | bytes 4718600 | tf_op jit(solution)/shard_map/ppermute | solution.py:662
  335.7 33.9 %collective-permute-start.15 = (bf16[1024,384]{1,0:T(8,128)(2,1)}, bf16[1024,384]{1,0:T(8,128)(2,1)S(1)}, u32[]{:S(2)}, u32[]{:S(2)}) collective-permute-start(bf16[1024,384]{1,0:T(8,128)(2,1)} %bitcast.227), channel_id=1, source_target_pairs={{0,2},{1,3},{2,0},{3,1},{4,6},{5,7},{6,4},{7,5},{8,10},{9,11},{10,... | collective-permute-start | bytes 2359304 | tf_op jit(solution)/shard_map/ppermute | solution.py:662
  369.7 199.8 %all-gather.9.cloned.1.call-start = ((), (), s32[]{:S(2)}) async-start(), calls=%async_computation.6 | async-start | bytes 3096576 | tf_op jit(solution)/shard_map/all_gather | solution.py:960
  369.7 48.6 %collective-permute-start.16 = (bf16[1024,384]{1,0:T(8,128)(2,1)}, bf16[1024,384]{1,0:T(8,128)(2,1)S(1)}, u32[]{:S(2)}, u32[]{:S(2)}) collective-permute-start(bf16[1024,384]{1,0:T(8,128)(2,1)} %bitcast.225), channel_id=1, source_target_pairs={{0,1},{1,2},{2,3},{3,0},{4,5},{5,6},{6,7},{7,4},{8,9},{9,10},{10,1... | collective-permute-start | bytes 2359304 | tf_op jit(solution)/shard_map/ppermute | solution.py:662
  401.6 33.8 %collective-permute-start.17 = (bf16[1024,384]{1,0:T(8,128)(2,1)}, bf16[1024,384]{1,0:T(8,128)(2,1)S(1)}, u32[]{:S(2)}, u32[]{:S(2)}) collective-permute-start(bf16[1024,384]{1,0:T(8,128)(2,1)} %bitcast.226), channel_id=1, source_target_pairs={{0,3},{1,0},{2,1},{3,2},{4,7},{5,4},{6,5},{7,6},{8,11},{9,8},{10,9... | collective-permute-start | bytes 2359304 | tf_op jit(solution)/shard_map/ppermute | solution.py:662
  432.7 25.4 %collective-permute-start.19 = (bf16[192,1024]{1,0:T(8,128)(2,1)}, bf16[192,1024]{1,0:T(8,128)(2,1)S(1)}, u32[]{:S(2)}, u32[]{:S(2)}) collective-permute-start(bf16[192,1024]{1,0:T(8,128)(2,1)} %bitcast.229), channel_id=1, source_target_pairs={{0,1},{1,2},{2,3},{3,0},{4,5},{5,6},{6,7},{7,4},{8,9},{9,10},{10,1... | collective-permute-start | bytes 1179656 | tf_op jit(solution)/shard_map/ppermute | solution.py:662
  432.7 25.4 %collective-permute-start.18 = (bf16[192,1024]{1,0:T(8,128)(2,1)S(1)}, bf16[192,1024]{1,0:T(8,128)(2,1)S(1)}, u32[]{:S(2)}, u32[]{:S(2)}) collective-permute-start(bf16[192,1024]{1,0:T(8,128)(2,1)S(1)} %bitcast.228), channel_id=1, source_target_pairs={{0,2},{1,3},{2,0},{3,1},{4,6},{5,7},{6,4},{7,5},{8,10},{9,11},{10,... | collective-permute-start | bytes 1179656 | tf_op jit(solution)/shard_map/ppermute | solution.py:662
  449.3 14.1 %collective-permute-start.20 = (bf16[192,1024]{1,0:T(8,128)(2,1)}, bf16[192,1024]{1,0:T(8,128)(2,1)}, u32[]{:S(2)}, u32[]{:S(2)}) collective-permute-start(bf16[192,1024]{1,0:T(8,128)(2,1)} %bitcast.230), channel_id=1, source_target_pairs={{0,3},{1,0},{2,1},{3,2},{4,7},{5,4},{6,5},{7,6},{8,11},{9,8},{10,9... | collective-permute-start | bytes 1179656 | tf_op jit(solution)/shard_map/ppermute | solution.py:662
  489.8 38.5 %collective-permute-start.23 = (bf16[1024,768]{1,0:T(8,128)(2,1)}, bf16[1024,768]{1,0:T(8,128)(2,1)}, u32[]{:S(2)}, u32[]{:S(2)}) collective-permute-start(bf16[1024,768]{1,0:T(8,128)(2,1)} %add_input_gradients.3), channel_id=1, source_target_pairs={{0,1},{1,2},{2,3},{3,0},{4,5},{5,6},{6,7},{7,4},{8,9},{9,10},{10,1... | collective-permute-start | bytes 4718600 | tf_op jit(solution)/shard_map/ppermute | solution.py:662
  493.3 32.0 %collective-permute-start.22 = (bf16[576,896]{1,0:T(8,128)(2,1)S(1)}, bf16[576,896]{1,0:T(8,128)(2,1)S(1)}, u32[]{:S(2)}, u32[]{:S(2)}) collective-permute-start(bf16[576,896]{1,0:T(8,128)(2,1)S(1)} %add_convert_fusion.4), channel_id=1, source_target_pairs={{0,8},{4,12},{8,0},{12,4},{16,24},{20,28},{24,16},{28,20},{1,9},{5... | collective-permute-start | bytes 3096584 | tf_op jit(solution)/shard_map/ppermute | solution.py:675
  528.3 37.7 %collective-permute-start.25 = (bf16[1024,768]{1,0:T(8,128)(2,1)}, bf16[1024,768]{1,0:T(8,128)(2,1)}, u32[]{:S(2)}, u32[]{:S(2)}) collective-permute-start(bf16[1024,768]{1,0:T(8,128)(2,1)} %collective-permute-done.23), channel_id=1, source_target_pairs={{0,1},{1,2},{2,3},{3,0},{4,5},{5,6},{6,7},{7,4},{8,9},{9,10},{10,1... | collective-permute-start | bytes 4718600 | tf_op jit(solution)/shard_map/ppermute | solution.py:662
  528.8 25.3 %collective-permute-start.24 = (bf16[576,896]{1,0:T(8,128)(2,1)S(1)}, bf16[576,896]{1,0:T(8,128)(2,1)}, u32[]{:S(2)}, u32[]{:S(2)}) collective-permute-start(bf16[576,896]{1,0:T(8,128)(2,1)S(1)} %add_convert_fusion.3), channel_id=1, source_target_pairs={{0,16},{4,20},{8,24},{12,28},{16,0},{20,4},{24,8},{28,12},{1,17},{... | collective-permute-start | bytes 3096584 | tf_op jit(solution)/shard_map/ppermute | solution.py:675
  570.2 9.6 %collective-permute-start.26 = (bf16[32,512]{1,0:T(8,128)(2,1)S(1)}, bf16[32,512]{1,0:T(8,128)(2,1)S(1)}, u32[]{:S(2)}, u32[]{:S(2)}) collective-permute-start(bf16[32,512]{1,0:T(8,128)(2,1)S(1)} %slice.150), channel_id=1, source_target_pairs={{0,1},{1,2},{2,3},{3,0},{4,5},{5,6},{6,7},{7,4},{8,9},{9,10},{10,1... | collective-permute-start | bytes 98312 | tf_op jit(solution)/shard_map/ppermute | solution.py:662
  570.2 9.6 %collective-permute-start.27 = (bf16[32,512]{1,0:T(8,128)(2,1)S(1)}, bf16[32,512]{1,0:T(8,128)(2,1)S(1)}, u32[]{:S(2)}, u32[]{:S(2)}) collective-permute-start(bf16[32,512]{1,0:T(8,128)(2,1)S(1)} %slice.150), channel_id=1, source_target_pairs={{0,2},{1,3},{2,0},{3,1},{4,6},{5,7},{6,4},{7,5},{8,10},{9,11},{10,... | collective-permute-start | bytes 98312 | tf_op jit(solution)/shard_map/ppermute | solution.py:662
  570.5 9.3 %collective-permute-start.28 = (bf16[32,512]{1,0:T(8,128)(2,1)S(1)}, bf16[32,512]{1,0:T(8,128)(2,1)S(1)}, u32[]{:S(2)}, u32[]{:S(2)}) collective-permute-start(bf16[32,512]{1,0:T(8,128)(2,1)S(1)} %slice.150), channel_id=1, source_target_pairs={{0,3},{1,0},{2,1},{3,2},{4,7},{5,4},{6,5},{7,6},{8,11},{9,8},{10,9... | collective-permute-start | bytes 98312 | tf_op jit(solution)/shard_map/ppermute | solution.py:662
  579.8 36.2 %collective-permute-start.29 = (bf16[1024,768]{1,0:T(8,128)(2,1)}, bf16[1024,768]{1,0:T(8,128)(2,1)S(1)}, u32[]{:S(2)}, u32[]{:S(2)}) collective-permute-start(bf16[1024,768]{1,0:T(8,128)(2,1)} %collective-permute-done.25), channel_id=1, source_target_pairs={{0,1},{1,2},{2,3},{3,0},{4,5},{5,6},{6,7},{7,4},{8,9},{9,10},{10,1... | collective-permute-start | bytes 4718600 | tf_op jit(solution)/shard_map/ppermute | solution.py:662
  (56 other events, 910.7 us)
Sparse Core Ops, SparseCore 0:
  11.6 108.7 all-gather.4
  123.3 61.2 all-gather.6
  264.0 87.9 reduce-scatter.2
  369.8 54.5 reduce-scatter.4
  478.6 40.3 all-gather.8

commit v4 on v3

--- a/solution.py
+++ b/solution.py
@@ -18,6 +18,7 @@
 f32 = jnp.float32
 SCORE_SCALE = 1.0 / math.sqrt(HD)
 SCORE_SCALE_2 = math.log2(math.e) * SCORE_SCALE
+SAFE_SCORE = 50.0
 PLANE = 256
 UNIT = 128
 SMALL_ROWS = 32
@@ -37,7 +38,7 @@
 
 
 def project_kernel(
-    width, info_ref, h_ref, wkv_ref, wt_ref, bkv_ref, bt_ref, rot_ref, k_ref, v_ref, t_ref
+    width, info_ref, h_ref, wkv_ref, wt_ref, bkv_ref, bt_ref, rot_ref, k_ref, v_ref, t_ref, n_ref
 ):
     hidden = h_ref[...]
     rot_ref[...] = hidden
@@ -50,7 +51,17 @@
     k_ref[:, width:] = jnp.where((lane == 0) & (row >= valid), mask_fill, 0.0).astype(bf16)
     v_ref[:, :width] = key_value[:, width:]
     v_ref[:, width:] = jnp.zeros((rows, PLANE - width), bf16)
-    t_ref[...] = (against(wt_ref[...], hidden) + bt_ref[...]).astype(bf16)
+    part = lax.broadcasted_iota(jnp.int32, (3 * width, 1), 0)
+    scale = jnp.where(part < width, SCORE_SCALE_2, 1.0)
+    turned = ((against(wt_ref[...], hidden) + bt_ref[...]) * scale).astype(bf16)
+    t_ref[...] = turned
+    n_ref[...] = jnp.zeros_like(n_ref)
+    for h in range(2 * width // HD):
+        rows_h = turned[HD * h : HD * h + HD].astype(f32)
+        norms = jnp.sum(rows_h * rows_h, axis=0, keepdims=True)
+        n_ref[0, h : h + 1, :] = jnp.broadcast_to(
+            jnp.max(norms, axis=1, keepdims=True), (1, UNIT)
+        )
 
 
 def project(info, hidden_in, w_kv, w_all_t, bias_kv, bias_t, chunks):
@@ -75,6 +86,7 @@
                 pl.BlockSpec((rows, PLANE), lambda c, info_ref: (c, 0)),
                 pl.BlockSpec((rows, PLANE), lambda c, info_ref: (c, 0)),
                 pl.BlockSpec((3 * width, rows), lambda c, info_ref: (0, c)),
+                pl.BlockSpec((1, 8, UNIT), lambda c, info_ref: (c, 0, 0)),
             ],
         ),
         out_shape=(
@@ -82,6 +94,7 @@
             jax.ShapeDtypeStruct((slot_len, PLANE), bf16),
             jax.ShapeDtypeStruct((slot_len, PLANE), bf16),
             jax.ShapeDtypeStruct((3 * width, slot_len), bf16),
+            jax.ShapeDtypeStruct((chunks, 8, UNIT), f32),
         ),
         compiler_params=pltpu.CompilerParams(vmem_limit_bytes=VMEM_LIMIT),
         cost_estimate=pl.CostEstimate(flops=1, bytes_accessed=1, transcendentals=0),
@@ -89,7 +102,9 @@
     )(info, hidden_in, w_kv, w_all_t, bias_kv, bias_t)
 
 
-def forward_kernel(bq, bk, heads, info_ref, k_ref, qt_ref, vt_ref, ot_ref, lse_ref, head_q, acc):
+def forward_kernel(
+    bq, bk, heads, info_ref, n_ref, k_ref, qt_ref, vt_ref, ot_ref, lse_ref, head_q, acc
+):
     width = HD * heads
     chunks = info_ref.shape[0] - 3
     first_tile = info_ref[1 + chunks]
@@ -97,46 +112,71 @@
     row = lax.broadcasted_iota(jnp.int32, (PLANE, bq), 0)
     for h in range(heads):
         head_q[h] = jnp.where(row == width, 1.0, 0.0).astype(bf16)
-
-    def query_step(qb, unused):
-        q0 = pl.multiple_of(qb * bq, bq)
-        for h in range(heads):
-            own = slice(HD * h, HD * h + HD)
-            head_q[h, own, :] = qt_ref[own, pl.ds(q0, bq)]
-        acc[...] = jnp.zeros_like(acc)
-
-        def key_step(step, carry):
-            k0 = pl.multiple_of(((first_tile + step) % 2) * bk, bk)
-            keys = k_ref[pl.ds(k0, bk), :]
-            scores = [matmul(keys, head_q[h]) for h in range(heads)]
+    most = jnp.max(n_ref[...], axis=0)
+    small_scores = jnp.max(most[:heads] * most[heads : 2 * heads]) < SAFE_SCORE * SAFE_SCORE
+
+    def head_values(h, k0):
+        return vt_ref[HD * h : HD * h + HD, pl.ds(k0, bk)]
+
+    def key_tile(step):
+        k0 = pl.multiple_of(((first_tile + step) % 2) * bk, bk)
+        return k0, k_ref[pl.ds(k0, bk), :]
+
+    def run(key_step, start, finish):
+        def query_step(qb, unused):
+            q0 = pl.multiple_of(qb * bq, bq)
+            for h in range(heads):
+                own = slice(HD * h, HD * h + HD)
+                head_q[h, own, :] = qt_ref[own, pl.ds(q0, bq)]
+            acc[...] = jnp.zeros_like(acc)
+            done = lax.fori_loop(0, tile_count, key_step, start)
+            for h in range(heads):
+                total, lse = finish(done[h])
+                ot_ref[HD * h : HD * h + HD, pl.ds(q0, bq)] = (acc[h] * (1.0 / total)).astype(
+                    bf16
+                )
+                lse_ref[pl.ds(h, 1), pl.ds(q0, bq)] = lse
+            return unused
+
+        lax.fori_loop(0, qt_ref.shape[1] // bq, query_step, 0)
+
+    @pl.when(small_scores)
+    def unshifted():
+        def key_step(step, totals):
+            k0, keys = key_tile(step)
             kept = []
             for h in range(heads):
+                weights = jnp.exp2(matmul(keys, head_q[h]))
+                kept.append(totals[h] + jnp.sum(weights, axis=0, keepdims=True))
+                acc[h] += matmul(head_values(h, k0), weights.astype(bf16))
+            return tuple(kept)
+
+        start = tuple(jnp.zeros((1, bq), f32) for _ in range(heads))
+        run(key_step, start, lambda total: (total, jnp.log2(total)))
+
+    @pl.when(jnp.logical_not(small_scores))
+    def shifted():
+        def key_step(step, carry):
+            k0, keys = key_tile(step)
+            kept = []
+            for h in range(heads):
+                scores = matmul(keys, head_q[h])
                 top, total = carry[h]
-                new_top = jnp.maximum(
-                    top, jnp.max(scores[h], axis=0, keepdims=True) * SCORE_SCALE_2
-                )
-                weights = jnp.exp2(scores[h] * SCORE_SCALE_2 - new_top)
+                new_top = jnp.maximum(top, jnp.max(scores, axis=0, keepdims=True))
+                weights = jnp.exp2(scores - new_top)
                 fade = jnp.exp2(top - new_top)
                 total = fade * total + jnp.sum(weights, axis=0, keepdims=True)
-                values_t = vt_ref[HD * h : HD * h + HD, pl.ds(k0, bk)]
-                acc[h] = fade * acc[h] + matmul(values_t, weights.astype(bf16))
+                acc[h] = fade * acc[h] + matmul(head_values(h, k0), weights.astype(bf16))
                 kept.append((new_top, total))
             return tuple(kept)
 
         start = tuple(
             (jnp.full((1, bq), mask_fill, f32), jnp.zeros((1, bq), f32)) for _ in range(heads)
         )
-        done = lax.fori_loop(0, tile_count, key_step, start)
-        for h in range(heads):
-            top, total = done[h]
-            ot_ref[HD * h : HD * h + HD, pl.ds(q0, bq)] = (acc[h] * (1.0 / total)).astype(bf16)
-            lse_ref[pl.ds(h, 1), pl.ds(q0, bq)] = top + jnp.log2(total)
-        return unused
-
-    lax.fori_loop(0, qt_ref.shape[1] // bq, query_step, 0)
-
-
-def attend_forward(info, wide_k, projected_t, chunk, chunks):
+        run(key_step, start, lambda pair: (pair[1], pair[0] + jnp.log2(pair[1])))
+
+
+def attend_forward(info, norms, wide_k, projected_t, chunk, chunks):
     slot_len = wide_k.shape[0]
     width = projected_t.shape[0] // 3
     heads = width // HD
@@ -152,6 +192,7 @@
         ),
         in_specs=[
             pl.BlockSpec(memory_space=pltpu.SMEM),
+            pl.BlockSpec(norms.shape, lambda i: (0, 0, 0)),
             pl.BlockSpec((slot_len, PLANE), lambda i: (0, 0)),
             pl.BlockSpec((width, rows), lambda i: (0, chunk)),
             pl.BlockSpec((width, slot_len), lambda i: (2, 0)),
@@ -167,7 +208,7 @@
         compiler_params=pltpu.CompilerParams(vmem_limit_bytes=VMEM_LIMIT),
         cost_estimate=pl.CostEstimate(flops=1, bytes_accessed=1, transcendentals=0),
         name="attend_forward",
-    )(info, wide_k, projected_t, projected_t)
+    )(info, norms, wide_k, projected_t, projected_t)
 
 
 def backward_kernel(bq, heads, q_span, k_span, rows, has, end_q, end_k, *refs):
@@ -231,7 +272,7 @@
                         own = slice(HD * h, HD * h + HD)
                         scores = matmul(keys, head_q[h])
                         grad_weights = matmul(values, head_go[h])
-                        weights = jnp.exp2(scores * SCORE_SCALE_2 - tops[h])
+                        weights = jnp.exp2(scores - tops[h])
                         grad_scores = (weights * (grad_weights - deltas[h])).astype(bf16)
                         more_v = against(weights.astype(bf16), head_go[h])
                         more_k = against(grad_scores, head_q[h])
@@ -268,7 +309,7 @@
         gq_out[0] = low
         add_weights(0, lambda right: matmul(low, right), wq_in)
     if end_k:
-        gkv_low[0, :, :width] = (gk[0, :, :width] * SCORE_SCALE).astype(bf16)
+        gkv_low[0, :, :width] = (gk[0, :, :width] * math.log(2.0)).astype(bf16)
         gkv_low[0, :, width:] = gv[0, :, :width].astype(bf16)
         both = gkv_low[0]
         add_weights(
@@ -422,6 +463,10 @@
 
 
 def ffn_forward_kernel(row_step, x_ref, w_in_ref, b_ref, w_down_ref, act_ref, slope_ref, out_ref):
+    @pl.when(pl.program_id(0) == 0)
+    def start():
+        out_ref[...] = jnp.zeros_like(out_ref)
+
     for r0 in range(0, x_ref.shape[0], row_step):
         rows = slice(r0, r0 + row_step)
         pre = matmul(x_ref[rows, :], w_in_ref[0]) + b_ref[0].astype(f32)
@@ -431,14 +476,7 @@
         act_ref[0, rows, :] = act
         slope_ref[0, rows, :] = (below + pre * density).astype(bf16)
         more = matmul(act, w_down_ref[0])
-
-        @pl.when(pl.program_id(0) == 0)
-        def first():
-            out_ref[rows, :] = more
-
-        @pl.when(pl.program_id(0) > 0)
-        def later():
-            out_ref[rows, :] += more
+        out_ref[rows, :] += more
 
 
 def ffn_forward(first_low, gathered, b_in_all):
@@ -468,20 +506,17 @@
 
 
 def ffn_backward_kernel(row_step, g_ref, w_in_ref, w_down_ref, slope_ref, pre_ref, out_ref):
+    @pl.when(pl.program_id(0) == 0)
+    def start():
+        out_ref[...] = jnp.zeros_like(out_ref)
+
     for r0 in range(0, g_ref.shape[0], row_step):
         rows = slice(r0, r0 + row_step)
         grad_act = against(g_ref[rows, :], w_down_ref[0])
         grad_pre = (grad_act * slope_ref[0, rows, :].astype(f32)).astype(bf16)
         pre_ref[0, rows, :] = grad_pre
         more = against(grad_pre, w_in_ref[0])
-
-        @pl.when(pl.program_id(0) == 0)
-        def first():
-            out_ref[rows, :] = more
-
-        @pl.when(pl.program_id(0) > 0)
-        def later():
-            out_ref[rows, :] += more
+        out_ref[rows, :] += more
 
 
 def ffn_backward(grad_ffn_low, gathered, slopes):
@@ -662,8 +697,12 @@
     return lax.ppermute(array, "tensor", moves)
 
 
-def group_tiles(tile, rank, group_size):
-    found = [shift(tile, s, group_size) for s in range(group_size)]
+def send_tiles(tile, group_size):
+    return [shift(tile, s, group_size) for s in range(group_size)]
+
+
+def order_tiles(found, rank):
+    tile, group_size = found[0], len(found)
     tiles = jnp.zeros((group_size,) + tile.shape, tile.dtype)
     for s in range(group_size):
         tiles = lax.dynamic_update_index_in_dim(tiles, found[s], (rank - s) % group_size, 0)
@@ -688,10 +727,15 @@
     return dp_size, part
 
 
-def spread_gather(shard):
+def spread_parts(shard):
     dp_size, part = row_parts(shard.shape[0])
     shard = jnp.pad(shard, ((0, part * dp_size - shard.shape[0]), (0, 0)))
-    mine = lax.dynamic_slice_in_dim(shard, lax.axis_index("dp") * part, part, 0)
+    return lax.dynamic_slice_in_dim(shard, lax.axis_index("dp") * part, part, 0)
+
+
+def spread_gather(shard):
+    mine = spread_parts(shard)
+    part, dp_size = mine.shape[0], lax.axis_size("dp")
     whole = lax.all_gather(mine, ("tensor", "dp"), axis=0, tiled=True)
     return whole.reshape(lax.axis_size("tensor"), part * dp_size, shard.shape[1])
 
@@ -741,15 +785,17 @@
     w_out_all = gathered[:, model + hidden_width : model + hidden_width + width].reshape(
         group_size * width, model
     )
-    w_project_all = spread_gather(w_project_t)
-    stud_tile = jnp.concatenate(
-        [w_student.T, b_in[None, :], pad_row(b_student), jnp.zeros((6, model), bf16)], axis=0
-    )
-    stud_tiles = group_tiles(stud_tile, rank, group_size)
-    w_stud_t = stud_tiles[:, :stu_cols].reshape(group_size * stu_cols, model)
-    b_in_all = stud_tiles[:, stu_cols : stu_cols + 1]
-    b_stud_all = stud_tiles[:, stu_cols + 1, :stu_cols].reshape(1, group_size * stu_cols)
-
+    tile = jnp.concatenate(
+        [
+            spread_parts(w_project_t),
+            w_student.T,
+            b_in[None, :],
+            pad_row(b_student),
+            jnp.zeros((14, model), bf16),
+        ],
+        axis=0,
+    )
+    found = send_tiles(tile, group_size)
     hidden_own = lax.dynamic_slice_in_dim(hidden_in, own_start, own_count, 0)
     cot_own = lax.dynamic_slice_in_dim(out_cotangent, own_start, own_count, 0)
     chunk_at = (rank + jnp.arange(group_size, dtype=jnp.int32)) % group_size
@@ -766,16 +812,31 @@
         ]
     ).astype(jnp.int32)
     bias_t = jnp.concatenate([b_query, jnp.zeros_like(b_query), b_value])
-    hidden_rot, wide_k, wide_v, projected_t = project(
+    hidden_rot, wide_k, wide_v, projected_t, norms = project(
         info, hidden_in, w_kv, w_project_t, bias_t[None, width:], bias_t[:, None], group_size
     )
 
+    order = sorted(range(1, group_size), key=lambda s: -min(s, group_size - s))
     outs = [None] * group_size
     lses = [None] * group_size
     attended = [None] * group_size
-    for s in list(range(1, group_size)) + [0]:
-        outs[s], lses[s] = attend_forward(info, wide_k, projected_t, s, group_size)
+    for step, s in enumerate(order + [0]):
+        outs[s], lses[s] = attend_forward(info, norms, wide_k, projected_t, s, group_size)
         attended[s] = shift(outs[s], s, group_size)
+        if step == 0:
+            *found, projected_t = lax.optimization_barrier((*found, projected_t))
+            tiles = order_tiles(found, rank)
+            part = tile.shape[0] - stu_cols - 16
+            w_project_all = lax.all_gather(tiles[:, :part], "dp", axis=1, tiled=True)
+            stud_tiles = tiles[:, part:]
+        if step == 2:
+            attended[order[0]], attended[order[1]], projected_t = lax.optimization_barrier(
+                (attended[order[0]], attended[order[1]], projected_t)
+            )
+    w_stud_t = stud_tiles[:, :stu_cols].reshape(group_size * stu_cols, model)
+    b_in_all = stud_tiles[:, stu_cols : stu_cols + 1]
+    b_stud_all = stud_tiles[:, stu_cols + 1, :stu_cols].reshape(1, group_size * stu_cols)
+
     attended_t = jnp.zeros((group_size * width, own_count), bf16)
     for s in range(group_size):
         source = (rank - s) % group_size
@@ -907,7 +968,6 @@
     gq_others = None
     w_kv_sum = None
     kv_arrived = {}
-    order = sorted(range(1, group_size), key=lambda s: -min(s, group_size - s))
     for step, s in enumerate(order):
         gq_others, low, w_kv_sum = part_of(
             *other_side,
@@ -974,25 +1034,25 @@
     grad_in_own = add_input_gradients(
         info, grad_in_own, w_project_all, {0: low_kv[0]}, q_arrived, bf16
     )
-    grad_in, grad_in_own = lax.optimization_barrier((hidden_rot, grad_in_own))
-    held = shift(grad_in_own, 1, group_size)
-    grad_in = place_rows(grad_in, grad_in_own, rank, 0, group_size)
     small_own = reduced[small_at : small_at + SMALL_ROWS]
-    small = group_tiles(small_own[:, : 4 * UNIT], rank, group_size)
-    late, held = exchange_add(late, held, 2)
-    grad_in = place_rows(grad_in, held, rank, 1, group_size)
-    held = shift(held, 1, group_size)
+    passed = [grad_in_own]
+    passed.append(shift(passed[-1], 1, group_size))
+    late, passed[-1] = exchange_add(late, passed[-1], 2)
+    passed[-1], small_own, hidden_out = lax.optimization_barrier(
+        (passed[-1], small_own, hidden_out)
+    )
+    found = send_tiles(small_own[:, : 4 * UNIT], group_size)
+    passed.append(shift(passed[-1], 1, group_size))
     distance = 4
     while distance < dp_size:
-        late, held = exchange_add(late, held, distance)
+        late, passed[-1] = exchange_add(late, passed[-1], distance)
         distance *= 2
-    held, small = lax.optimization_barrier((held, small))
-    for s in range(2, group_size):
-        grad_in = place_rows(grad_in, held, rank, s, group_size)
-        if s < group_size - 1:
-            held = shift(held, 1, group_size)
+    grad_in, found, *passed = lax.optimization_barrier((hidden_rot, found, *passed))
+    passed.append(shift(passed[-1], 1, group_size))
+    for s in range(group_size):
+        grad_in = place_rows(grad_in, passed[s], rank, s, group_size)
     late = late.astype(f32)
-    small = small.astype(f32)
+    small = order_tiles(found, rank).astype(f32)
     small_own = small_own[:, 4 * UNIT :].astype(f32)
     grad_w_pool = small[:, :, :UNIT].reshape(grad_w_pool.shape)
     column_share = -(-columns.size // (UNIT * group_size))

time: 634 us -> 643 us (1.014)
  the two profiles are of different devices: /device:TPU:0 before, /device:TPU:6 now
where the time goes in v4:
time: 643 us; the launch traced here: 632 us
  Pallas kernels  284 us (44%)
  waiting for transfers between devices  159 us (25%)
  starting transfers between devices  72.9 us (11%)
  local copies, waits for them, and re-layouts  46.7 us (7%)
  other arithmetic  37 us (6%)
  between operations  19.5 us (3%)
  matrix products  13 us (2%)
    ppermute x27, waiting for transfers between devices, shift(): return lax.ppermute(array, 'tensor', moves)  124 us
    pallas_call x8, Pallas kernels, attend_backward(): pl.pallas_call(functools.partial(backward_kernel, bq, heads, q_span, k_sp...  113 us
    pallas_call x4, Pallas kernels, attend_forward(): pl.pallas_call(functools.partial(forward_kernel, bq, bk, heads), grid=(1,...  89.5 us
    ppermute x27, starting transfers between devices, shift(): return lax.ppermute(array, 'tensor', moves)  63.4 us
    ppermute x3, waiting for transfers between devices, exchange_add(): came = lax.ppermute(array, 'dp', moves)  34.8 us
    pallas_call x1, Pallas kernels, pack_gradients(): pl.pallas_call(functools.partial(pack_kernel, dp_size, part), grid=(group...  20.1 us
    pallas_call x1, Pallas kernels, ffn_forward(): pl.pallas_call(functools.partial(ffn_forward_kernel, min(256, count)), gr...  18 us
    pallas_call x1, Pallas kernels, ffn_backward(): pl.pallas_call(functools.partial(ffn_backward_kernel, min(256, count)), g...  16.3 us
  transfers between devices with their start and end apart: 35, of which 17 were waited for; matrix products, arithmetic and copies ran while one was open for 12% of the time, Pallas kernels for 45%

profile of v4, /device:TPU:6, one launch (start us, length us, event | category | flops | bytes accessed | tf_op | source)
XLA Modules:
  0.0 631.9 jit_solution(2305841638939598308)
XLA Ops:
  22.8 11.7 %project.1 = (bf16[4096,768]{1,0:T(8,128)(2,1)}, bf16[4096,256]{1,0:T(8,128)(2,1)}, bf16[4096,256]{1,0:T(8,128)(2,1)}, bf16[576,4096]{1,0:T(8,128)(2,1)}, f32[4,8,128]{2,1,0:T(8,128)}) custom-call(s32[7]{0:T(128)} %pad_add_fusion.info_ref.refs_0_.rank_ref, bf16[4096,768]{1,0:T(8,128)(2,1)} %h_ref.1, bf16[768,384]{1,0:T(8,128)(2,1)} %pad_maximum_fusion.3.wkv_ref, ...), custom_call_target="tpu_custom_call" | custom-call | flops 1 | bytes 1 | tf_op jit(solution)/shard_map/project/pallas_call | solution.py:72
  34.5 22.1 %attend_forward.4 = (bf16[192,1024]{1,0:T(8,128)(2,1)}, f32[8,1024]{1,0:T(8,128)}) custom-call(s32[7]{0:T(128)} %pad_add_fusion.info_ref.refs_0_.rank_ref, f32[4,8,128]{2,1,0:T(8,128)} %get-tuple-element.124.n_ref, bf16[4096,256]{1,0:T(8,128)(2,1)} %get-tuple-element.122.k_ref.refs_1_, bf16[576,4096]{1,0:T(8,128)(2,1)} %get-tuple-element.129.qt_ref.vt_ref.refs_3_.refs_4_, ...), custom_call_target="tpu_custom_call" | custom-call | flops 1 | bytes 1 | tf_op jit(solution)/shard_map/attend_forward/pallas_call | solution.py:186
  57.2 22.6 %attend_forward.5 = (bf16[192,1024]{1,0:T(8,128)(2,1)}, f32[8,1024]{1,0:T(8,128)}) custom-call(s32[7]{0:T(128)} %pad_add_fusion.info_ref.refs_0_.rank_ref, f32[4,8,128]{2,1,0:T(8,128)} %get-tuple-element.124.n_ref, bf16[4096,256]{1,0:T(8,128)(2,1)} %get-tuple-element.122.k_ref.refs_1_, bf16[576,4096]{1,0:T(8,128)(2,1)} %get-tuple-element.129.qt_ref.vt_ref.refs_3_.refs_4_, ...), custom_call_target="tpu_custom_call" | custom-call | flops 1 | bytes 1 | tf_op jit(solution)/shard_map/attend_forward/pallas_call | solution.py:186
  79.8 22.3 %attend_forward.7 = (bf16[192,1024]{1,0:T(8,128)(2,1)}, f32[8,1024]{1,0:T(8,128)}) custom-call(s32[7]{0:T(128)} %pad_add_fusion.info_ref.refs_0_.rank_ref, f32[4,8,128]{2,1,0:T(8,128)} %get-tuple-element.124.n_ref, bf16[4096,256]{1,0:T(8,128)(2,1)} %get-tuple-element.122.k_ref.refs_1_, bf16[576,4096]{1,0:T(8,128)(2,1)} %get-tuple-element.129.qt_ref.vt_ref.refs_3_.refs_4_, ...), custom_call_target="tpu_custom_call" | custom-call | flops 1 | bytes 1 | tf_op jit(solution)/shard_map/attend_forward/pallas_call | solution.py:186
  107.7 16.5 %collective-permute-done.4 = bf16[192,1024]{1,0:T(8,128)(2,1)S(1)} collective-permute-done((bf16[192,1024]{1,0:T(8,128)(2,1)S(1)}, bf16[192,1024]{1,0:T(8,128)(2,1)S(1)}, u32[]{:S(2)}, u32[]{:S(2)}) %collective-permute-start.4) | collective-permute-done | bytes 393248 | tf_op jit(solution)/shard_map/ppermute | solution.py:697
  124.2 22.5 %attend_forward.6 = (bf16[192,1024]{1,0:T(8,128)(2,1)}, f32[8,1024]{1,0:T(8,128)}) custom-call(s32[7]{0:T(128)} %pad_add_fusion.info_ref.refs_0_.rank_ref, f32[4,8,128]{2,1,0:T(8,128)} %get-tuple-element.124.n_ref, bf16[4096,256]{1,0:T(8,128)(2,1)} %get-tuple-element.122.k_ref.refs_1_, bf16[576,4096]{1,0:T(8,128)(2,1)} %get-tuple-element.129.qt_ref.vt_ref.refs_3_.refs_4_, ...), custom_call_target="tpu_custom_call" | custom-call | flops 1 | bytes 1 | tf_op jit(solution)/shard_map/attend_forward/pallas_call | solution.py:186
  159.9 18.0 %ffn_forward.1 = (bf16[4,1024,768]{2,1,0:T(8,128)(2,1)}, bf16[4,1024,768]{2,1,0:T(8,128)(2,1)}, f32[1024,768]{1,0:T(8,128)}) custom-call(bf16[1024,768]{1,0:T(8,128)(2,1)} %add_convert_fusion.1.x_ref.first_ref, bf16[4,1792,768]{2,1,0:T(8,128)(2,1)} %bitcast.170, bf16[4,1,768]{2,1,0:T(2,128)(2,1)} %slice.161.b_ref, bf16[4,1792,768]{2,1,0:T(8,128)(2,1)} %bitcast.171), custom_call_target="tpu_custom_call" | custom-call | flops 1 | bytes 1 | tf_op jit(solution)/shard_map/ffn_forward/pallas_call | solution.py:487
  213.1 16.3 %ffn_backward.1 = (bf16[4,1024,768]{2,1,0:T(8,128)(2,1)}, f32[1024,768]{1,0:T(8,128)}) custom-call(bf16[1024,768]{1,0:T(8,128)(2,1)} %convert_element_type.119.g_ref.gffn_ref, bf16[4,1792,768]{2,1,0:T(8,128)(2,1)} %bitcast.172, bf16[4,1792,768]{2,1,0:T(8,128)(2,1)} %bitcast.173, bf16[4,1024,768]{2,1,0:T(8,128)(2,1)} %get-tuple-element.139.slope_ref), custom_call_target="tpu_custom_call" | custom-call | flops 1 | bytes 1 | tf_op jit(solution)/shard_map/ffn_backward/pallas_call | solution.py:526
  248.0 20.1 %pack_gradients.1 = bf16[8,4,224,768]{3,2,1,0:T(8,128)(2,1)} custom-call(bf16[1024,768]{1,0:T(8,128)(2,1)} %add_convert_fusion.1.x_ref.first_ref, bf16[4,1024,768]{2,1,0:T(8,128)(2,1)} %get-tuple-element.142.gpre_ref, bf16[4,1024,768]{2,1,0:T(8,128)(2,1)} %get-tuple-element.143.act_ref, bf16[1024,768]{1,0:T(8,128)(2,1)} %convert_element_type.119.g_ref.gffn_ref, ...), custom_call_target="tpu_custom_call" | custom-call | flops 1 | bytes 1 | tf_op jit(solution)/shard_map/pack_gradients/pallas_call | solution.py:634
  268.1 7.7 %collective-permute-done.11 = bf16[192,1024]{1,0:T(8,128)(2,1)S(1)} collective-permute-done((bf16[192,1024]{1,0:T(8,128)(2,1)S(1)}, bf16[192,1024]{1,0:T(8,128)(2,1)S(1)}, u32[]{:S(2)}, u32[]{:S(2)}) %collective-permute-start.11) | collective-permute-done | bytes 393248 | tf_op jit(solution)/shard_map/ppermute | solution.py:697
  276.8 23.1 %attend_backward.8 = (f32[1,192,1024]{2,1,0:T(8,128)}, f32[3,1024,256]{2,1,0:T(8,128)}, f32[3,1024,256]{2,1,0:T(8,128)}) custom-call(s32[7]{0:T(128)} %pad_add_fusion.info_ref.refs_0_.rank_ref, bf16[4096,256]{1,0:T(8,128)(2,1)} %get-tuple-element.122.k_ref.refs_1_, bf16[4096,256]{1,0:T(8,128)(2,1)} %get-tuple-element.123.refs_2_, ...), custom_call_target="tpu_custom_call" | custom-call | flops 1 | bytes 1 | tf_op jit(solution)/shard_map/attend_backward/pallas_call | solution.py:413
  299.9 12.5 %collective-permute-done.13 = bf16[1024,768]{1,0:T(8,128)(2,1)S(1)} collective-permute-done((bf16[1024,768]{1,0:T(8,128)(2,1)}, bf16[1024,768]{1,0:T(8,128)(2,1)S(1)}, u32[]{:S(2)}, u32[]{:S(2)}) %collective-permute-start.13) | collective-permute-done | bytes 1572896 | tf_op jit(solution)/shard_map/ppermute | solution.py:697
  316.4 18.6 %attend_backward.9 = (f32[3,192,1024]{2,1,0:T(8,128)}, bf16[1,1024,384]{2,1,0:T(8,128)(2,1)}, f32[384,896]{1,0:T(8,128)}) custom-call(s32[7]{0:T(128)} %pad_add_fusion.info_ref.refs_0_.rank_ref, bf16[4096,256]{1,0:T(8,128)(2,1)} %get-tuple-element.122.k_ref.refs_1_, bf16[4096,256]{1,0:T(8,128)(2,1)} %get-tuple-element.123.refs_2_, ...), custom_call_target="tpu_custom_call" | custom-call | flops 1 | bytes 1 | tf_op jit(solution)/shard_map/attend_backward/pallas_call | solution.py:413
  335.0 6.0 collective-permute-start.15
  341.1 20.2 %attend_backward.10 = (f32[3,192,1024]{2,1,0:T(8,128)}, bf16[1,1024,384]{2,1,0:T(8,128)(2,1)}, f32[384,896]{1,0:T(8,128)}) custom-call(s32[7]{0:T(128)} %pad_add_fusion.info_ref.refs_0_.rank_ref, bf16[4096,256]{1,0:T(8,128)(2,1)} %get-tuple-element.122.k_ref.refs_1_, bf16[4096,256]{1,0:T(8,128)(2,1)} %get-tuple-element.123.refs_2_, ...), custom_call_target="tpu_custom_call" | custom-call | flops 1 | bytes 1 | tf_op jit(solution)/shard_map/attend_backward/pallas_call | solution.py:413
  361.2 17.6 %collective-permute-done.15.refs_0_ = bf16[1024,384]{1,0:T(8,128)(2,1)S(1)} collective-permute-done((bf16[1024,384]{1,0:T(8,128)(2,1)}, bf16[1024,384]{1,0:T(8,128)(2,1)S(1)}, u32[]{:S(2)}, u32[]{:S(2)}) %collective-permute-start.15) | collective-permute-done | bytes 786464 | tf_op jit(solution)/shard_map/ppermute | solution.py:697
  380.7 7.7 %attend_backward.11 = (f32[3,192,1024]{2,1,0:T(8,128)}, bf16[1,1024,384]{2,1,0:T(8,128)(2,1)}, f32[384,896]{1,0:T(8,128)}) custom-call(s32[7]{0:T(128)} %pad_add_fusion.info_ref.refs_0_.rank_ref, bf16[4096,256]{1,0:T(8,128)(2,1)} %get-tuple-element.122.k_ref.refs_1_, bf16[4096,256]{1,0:T(8,128)(2,1)} %get-tuple-element.123.refs_2_, ...), custom_call_target="tpu_custom_call" | custom-call | flops 1 | bytes 1 | tf_op jit(solution)/shard_map/attend_backward/pallas_call | solution.py:413
  388.4 22.6 %collective-permute-start.17 = (bf16[1024,384]{1,0:T(8,128)(2,1)}, bf16[1024,384]{1,0:T(8,128)(2,1)S(1)}, u32[]{:S(2)}, u32[]{:S(2)}) collective-permute-start(bf16[1024,384]{1,0:T(8,128)(2,1)} %bitcast.226), channel_id=1, source_target_pairs={{0,3},{1,0},{2,1},{3,2},{4,7},{5,4},{6,5},{7,6},{8,11},{9,8},{10,9... | collective-permute-start | bytes 2359304 | tf_op jit(solution)/shard_map/ppermute | solution.py:697
  411.1 8.8 %attend_backward.12 = (bf16[1,192,1024]{2,1,0:T(8,128)(2,1)}, f32[1,1024,256]{2,1,0:T(8,128)}, f32[1,1024,256]{2,1,0:T(8,128)}, f32[192,896]{1,0:T(8,128)}) custom-call(s32[7]{0:T(128)} %pad_add_fusion.info_ref.refs_0_.rank_ref, bf16[4096,256]{1,0:T(8,128)(2,1)} %get-tuple-element.122.k_ref.refs_1_, bf16[4096,256]{1,0:T(8,128)(2,1)} %get-tuple-element.123.refs_2_, ...), custom_call_target="tpu_custom_call" | custom-call | flops 1 | bytes 1 | tf_op jit(solution)/shard_map/attend_backward/pallas_call | solution.py:413
  419.9 14.2 %attend_backward.13 = (bf16[1,192,1024]{2,1,0:T(8,128)(2,1)}, f32[1,1024,256]{2,1,0:T(8,128)}, f32[1,1024,256]{2,1,0:T(8,128)}, f32[192,896]{1,0:T(8,128)}) custom-call(s32[7]{0:T(128)} %pad_add_fusion.info_ref.refs_0_.rank_ref, bf16[4096,256]{1,0:T(8,128)(2,1)} %get-tuple-element.122.k_ref.refs_1_, bf16[4096,256]{1,0:T(8,128)(2,1)} %get-tuple-element.123.refs_2_, ...), custom_call_target="tpu_custom_call" | custom-call | flops 1 | bytes 1 | tf_op jit(solution)/shard_map/attend_backward/pallas_call | solution.py:413
  434.3 5.4 collective-permute-done.17.refs_2_
  439.7 5.8 attend_backward.14
  446.1 7.6 %add_input_gradients.2.sum_ref = f32[1024,768]{1,0:T(8,128)} custom-call(s32[7]{0:T(128)} %pad_add_fusion.info_ref.refs_0_.rank_ref, f32[1024,768]{1,0:T(8,128)} %copy-done.4, bf16[4,640,768]{2,1,0:T(8,128)(2,1)} %all-gather.7.cloned.1.call-done.w_ref, bf16[1024,384]{1,0:T(8,128)(2,1)} %copy-done.27, bf16[1024,384]{1,0:T(8,128)(2,1)} %copy-done.28, ...), custom_call_target="tpu_custom_call" | custom-call | flops 1 | bytes 1 | tf_op jit(solution)/shard_map/add_input_gradients/pallas_call | solution.py:447
  453.7 11.8 %collective-permute-done.18.refs_1_ = bf16[192,1024]{1,0:T(8,128)(2,1)S(1)} collective-permute-done((bf16[192,1024]{1,0:T(8,128)(2,1)}, bf16[192,1024]{1,0:T(8,128)(2,1)S(1)}, u32[]{:S(2)}, u32[]{:S(2)}) %collective-permute-start.18) | collective-permute-done | bytes 393248 | tf_op jit(solution)/shard_map/ppermute | solution.py:697
  468.9 15.0 %attend_backward.15 = (bf16[1,192,1024]{2,1,0:T(8,128)(2,1)}, bf16[1,1024,384]{2,1,0:T(8,128)(2,1)}, bf16[576,896]{1,0:T(8,128)(2,1)}) custom-call(s32[7]{0:T(128)} %pad_add_fusion.info_ref.refs_0_.rank_ref, bf16[4096,256]{1,0:T(8,128)(2,1)} %get-tuple-element.122.k_ref.refs_1_, bf16[4096,256]{1,0:T(8,128)(2,1)} %get-tuple-element.123.refs_2_, ...), custom_call_target="tpu_custom_call" | custom-call | flops 1 | bytes 1 | tf_op jit(solution)/shard_map/attend_backward/pallas_call | solution.py:413
  483.9 9.3 %collective-permute-start.21 = (bf16[576,896]{1,0:T(8,128)(2,1)}, bf16[576,896]{1,0:T(8,128)(2,1)}, u32[]{:S(2)}, u32[]{:S(2)}) collective-permute-start(bf16[576,896]{1,0:T(8,128)(2,1)} %get-tuple-element.193), channel_id=1, source_target_pairs={{0,4},{4,0},{8,12},{12,8},{16,20},{20,16},{24,28},{28,24},{1,5},{5... | collective-permute-start | bytes 3096584 | tf_op jit(solution)/shard_map/ppermute | solution.py:714
  495.8 7.4 %add_input_gradients.3 = bf16[1024,768]{1,0:T(8,128)(2,1)} custom-call(s32[7]{0:T(128)} %pad_add_fusion.info_ref.refs_0_.rank_ref, f32[1024,768]{1,0:T(8,128)} %add_input_gradients.2.sum_ref, bf16[4,640,768]{2,1,0:T(8,128)(2,1)} %all-gather.7.cloned.1.call-done.w_ref, bf16[1024,384]{1,0:T(8,128)(2,1)} %bitcast.195, bf16[192,1024]{1,0:T(8,128)(2,1)} %copy-done.31, ...), custom_call_target="tpu_custom_call" | custom-call | flops 1 | bytes 1 | tf_op jit(solution)/shard_map/add_input_gradients/pallas_call | solution.py:447
  515.0 18.3 %collective-permute-done.22 = bf16[576,896]{1,0:T(8,128)(2,1)} collective-permute-done((bf16[576,896]{1,0:T(8,128)(2,1)S(1)}, bf16[576,896]{1,0:T(8,128)(2,1)}, u32[]{:S(2)}, u32[]{:S(2)}) %collective-permute-start.22) | collective-permute-done | bytes 1032224 | tf_op jit(solution)/shard_map/ppermute | solution.py:714
  533.3 8.7 %collective-permute-done.23 = bf16[1024,768]{1,0:T(8,128)(2,1)} collective-permute-done((bf16[1024,768]{1,0:T(8,128)(2,1)}, bf16[1024,768]{1,0:T(8,128)(2,1)}, u32[]{:S(2)}, u32[]{:S(2)}) %collective-permute-start.23) | collective-permute-done | bytes 1572896 | tf_op jit(solution)/shard_map/ppermute | solution.py:697
  556.1 14.0 %collective-permute-done.27 = bf16[576,896]{1,0:T(8,128)(2,1)S(1)} collective-permute-done((bf16[576,896]{1,0:T(8,128)(2,1)S(1)}, bf16[576,896]{1,0:T(8,128)(2,1)S(1)}, u32[]{:S(2)}, u32[]{:S(2)}) %collective-permute-start.27) | collective-permute-done | bytes 1032224 | tf_op jit(solution)/shard_map/ppermute | solution.py:714
  570.0 12.1 %collective-permute-done.28 = bf16[1024,768]{1,0:T(8,128)(2,1)} collective-permute-done((bf16[1024,768]{1,0:T(8,128)(2,1)}, bf16[1024,768]{1,0:T(8,128)(2,1)}, u32[]{:S(2)}, u32[]{:S(2)}) %collective-permute-start.28) | collective-permute-done | bytes 1572896 | tf_op jit(solution)/shard_map/ppermute | solution.py:697
  597.3 25.6 %collective-permute-done.29 = bf16[1024,768]{1,0:T(8,128)(2,1)S(1)} collective-permute-done((bf16[1024,768]{1,0:T(8,128)(2,1)}, bf16[1024,768]{1,0:T(8,128)(2,1)S(1)}, u32[]{:S(2)}, u32[]{:S(2)}) %collective-permute-start.29) | collective-permute-done | bytes 1572896 | tf_op jit(solution)/shard_map/ppermute | solution.py:697
  (297 shorter events, 140.3 us)
Async XLA Ops:
  8.1 144.0 %all-gather.5.cloned.1.call-start = ((), (), s32[]{:S(2)}) async-start(), calls=%async_computation.2 | async-start | bytes 11354112 | tf_op jit(solution)/shard_map/all_gather | solution.py:739
  10.5 257.6 %all-gather.7.cloned.1.call-start = ((), (), s32[]{:S(2)}) async-start(), calls=%async_computation.3 | async-start | bytes 4423680 | tf_op jit(solution)/shard_map/all_gather | solution.py:830
  11.0 46.3 %collective-permute-start.1 = (bf16[128,768]{1,0:T(8,128)(2,1)S(1)}, bf16[128,768]{1,0:T(8,128)(2,1)S(1)}, u32[]{:S(2)}, u32[]{:S(2)}) collective-permute-start(bf16[128,768]{1,0:T(8,128)(2,1)S(1)} %concatenate.29), channel_id=1, source_target_pairs={{0,1},{1,2},{2,3},{3,0},{4,5},{5,6},{6,7},{7,4},{8,9},{9,10},{10,1... | collective-permute-start | bytes 589832 | tf_op jit(solution)/shard_map/ppermute | solution.py:697
  12.6 44.6 %collective-permute-start.2 = (bf16[128,768]{1,0:T(8,128)(2,1)S(1)}, bf16[128,768]{1,0:T(8,128)(2,1)S(1)}, u32[]{:S(2)}, u32[]{:S(2)}) collective-permute-start(bf16[128,768]{1,0:T(8,128)(2,1)S(1)} %concatenate.29), channel_id=1, source_target_pairs={{0,2},{1,3},{2,0},{3,1},{4,6},{5,7},{6,4},{7,5},{8,10},{9,11},{10,... | collective-permute-start | bytes 589832 | tf_op jit(solution)/shard_map/ppermute | solution.py:697
  15.2 42.1 %collective-permute-start.3 = (bf16[128,768]{1,0:T(8,128)(2,1)S(1)}, bf16[128,768]{1,0:T(8,128)(2,1)S(1)}, u32[]{:S(2)}, u32[]{:S(2)}) collective-permute-start(bf16[128,768]{1,0:T(8,128)(2,1)S(1)} %concatenate.29), channel_id=1, source_target_pairs={{0,3},{1,0},{2,1},{3,2},{4,7},{5,4},{6,5},{7,6},{8,11},{9,8},{10,9... | collective-permute-start | bytes 589832 | tf_op jit(solution)/shard_map/ppermute | solution.py:697
  56.6 51.1 %collective-permute-start = (bf16[192,1024]{1,0:T(8,128)(2,1)}, bf16[192,1024]{1,0:T(8,128)(2,1)S(1)}, u32[]{:S(2)}, u32[]{:S(2)}) collective-permute-start(bf16[192,1024]{1,0:T(8,128)(2,1)} %get-tuple-element.126), channel_id=1, source_target_pairs={{0,2},{1,3},{2,0},{3,1},{4,6},{5,7},{6,4},{7,5},{8,10},{9,11},{10,... | collective-permute-start | bytes 1179656 | tf_op jit(solution)/shard_map/ppermute | solution.py:697
  102.2 22.1 %collective-permute-start.4 = (bf16[192,1024]{1,0:T(8,128)(2,1)S(1)}, bf16[192,1024]{1,0:T(8,128)(2,1)S(1)}, u32[]{:S(2)}, u32[]{:S(2)}) collective-permute-start(bf16[192,1024]{1,0:T(8,128)(2,1)S(1)} %copy-done.16), channel_id=1, source_target_pairs={{0,1},{1,2},{2,3},{3,0},{4,5},{5,6},{6,7},{7,4},{8,9},{9,10},{10,1... | collective-permute-start | bytes 1179656 | tf_op jit(solution)/shard_map/ppermute | solution.py:697
  102.5 48.9 %collective-permute-start.5 = (bf16[192,1024]{1,0:T(8,128)(2,1)}, bf16[192,1024]{1,0:T(8,128)(2,1)S(1)}, u32[]{:S(2)}, u32[]{:S(2)}) collective-permute-start(bf16[192,1024]{1,0:T(8,128)(2,1)} %get-tuple-element.133), channel_id=1, source_target_pairs={{0,3},{1,0},{2,1},{3,2},{4,7},{5,4},{6,5},{7,6},{8,11},{9,8},{10,9... | collective-permute-start | bytes 1179656 | tf_op jit(solution)/shard_map/ppermute | solution.py:697
  159.9 219.0 %reduce-scatter.3.cloned.1.call-start = ((), (), s32[]{:S(2)}) async-start(), calls=%async_computation.4 | async-start | bytes 12386304 | tf_op jit(solution)/shard_map/reduce_scatter | solution.py:956
  196.0 36.6 %collective-permute-start.9 = (bf16[1024,768]{1,0:T(8,128)(2,1)}, bf16[1024,768]{1,0:T(8,128)(2,1)}, u32[]{:S(2)}, u32[]{:S(2)}) collective-permute-start(bf16[1024,768]{1,0:T(8,128)(2,1)} %copy-done.7), channel_id=1, source_target_pairs={{0,1},{1,2},{2,3},{3,0},{4,5},{5,6},{6,7},{7,4},{8,9},{9,10},{10,1... | collective-permute-start | bytes 4718600 | tf_op jit(solution)/shard_map/ppermute | solution.py:697
  242.0 26.1 %collective-permute-start.10 = (bf16[192,1024]{1,0:T(8,128)(2,1)S(1)}, bf16[192,1024]{1,0:T(8,128)(2,1)S(1)}, u32[]{:S(2)}, u32[]{:S(2)}) collective-permute-start(bf16[192,1024]{1,0:T(8,128)(2,1)S(1)} %get-tuple-element.265), channel_id=1, source_target_pairs={{0,3},{1,0},{2,1},{3,2},{4,7},{5,4},{6,5},{7,6},{8,11},{9,8},{10,9... | collective-permute-start | bytes 1179656 | tf_op jit(solution)/shard_map/ppermute | solution.py:697
  244.8 30.9 %collective-permute-start.11 = (bf16[192,1024]{1,0:T(8,128)(2,1)S(1)}, bf16[192,1024]{1,0:T(8,128)(2,1)S(1)}, u32[]{:S(2)}, u32[]{:S(2)}) collective-permute-start(bf16[192,1024]{1,0:T(8,128)(2,1)S(1)} %get-tuple-element.264), channel_id=1, source_target_pairs={{0,2},{1,3},{2,0},{3,1},{4,6},{5,7},{6,4},{7,5},{8,10},{9,11},{10,... | collective-permute-start | bytes 1179656 | tf_op jit(solution)/shard_map/ppermute | solution.py:697
  244.8 30.9 %collective-permute-start.12 = (bf16[192,1024]{1,0:T(8,128)(2,1)S(1)}, bf16[192,1024]{1,0:T(8,128)(2,1)S(1)}, u32[]{:S(2)}, u32[]{:S(2)}) collective-permute-start(bf16[192,1024]{1,0:T(8,128)(2,1)S(1)} %get-tuple-element.263), channel_id=1, source_target_pairs={{0,1},{1,2},{2,3},{3,0},{4,5},{5,6},{6,7},{7,4},{8,9},{9,10},{10,1... | collective-permute-start | bytes 1179656 | tf_op jit(solution)/shard_map/ppermute | solution.py:697
  276.5 192.4 %reduce-scatter.5.cloned.1.call-start = ((), (), s32[]{:S(2)}) async-start(), calls=%async_computation.5 | async-start | bytes 1720320 | tf_op jit(solution)/shard_map/reduce_scatter | solution.py:988
  276.5 35.9 %collective-permute-start.13 = (bf16[1024,768]{1,0:T(8,128)(2,1)}, bf16[1024,768]{1,0:T(8,128)(2,1)S(1)}, u32[]{:S(2)}, u32[]{:S(2)}) collective-permute-start(bf16[1024,768]{1,0:T(8,128)(2,1)} %collective-permute-done.9), channel_id=1, source_target_pairs={{0,1},{1,2},{2,3},{3,0},{4,5},{5,6},{6,7},{7,4},{8,9},{9,10},{10,1... | collective-permute-start | bytes 4718600 | tf_op jit(solution)/shard_map/ppermute | solution.py:697
  312.4 66.5 %collective-permute-start.14 = (bf16[1024,768]{1,0:T(8,128)(2,1)S(1)}, bf16[1024,768]{1,0:T(8,128)(2,1)}, u32[]{:S(2)}, u32[]{:S(2)}) collective-permute-start(bf16[1024,768]{1,0:T(8,128)(2,1)S(1)} %collective-permute-done.13), channel_id=1, source_target_pairs={{0,1},{1,2},{2,3},{3,0},{4,5},{5,6},{6,7},{7,4},{8,9},{9,10},{10,1... | collective-permute-start | bytes 4718600 | tf_op jit(solution)/shard_map/ppermute | solution.py:697
  335.0 43.9 %collective-permute-start.15 = (bf16[1024,384]{1,0:T(8,128)(2,1)}, bf16[1024,384]{1,0:T(8,128)(2,1)S(1)}, u32[]{:S(2)}, u32[]{:S(2)}) collective-permute-start(bf16[1024,384]{1,0:T(8,128)(2,1)} %bitcast.227), channel_id=1, source_target_pairs={{0,2},{1,3},{2,0},{3,1},{4,6},{5,7},{6,4},{7,5},{8,10},{9,11},{10,... | collective-permute-start | bytes 2359304 | tf_op jit(solution)/shard_map/ppermute | solution.py:697
  378.9 163.1 %all-gather.9.cloned.1.call-start = ((), (), s32[]{:S(2)}) async-start(), calls=%async_computation.6 | async-start | bytes 3096576 | tf_op jit(solution)/shard_map/all_gather | solution.py:1020
  379.0 40.9 %collective-permute-start.16 = (bf16[1024,384]{1,0:T(8,128)(2,1)}, bf16[1024,384]{1,0:T(8,128)(2,1)S(1)}, u32[]{:S(2)}, u32[]{:S(2)}) collective-permute-start(bf16[1024,384]{1,0:T(8,128)(2,1)} %bitcast.225), channel_id=1, source_target_pairs={{0,1},{1,2},{2,3},{3,0},{4,5},{5,6},{6,7},{7,4},{8,9},{9,10},{10,1... | collective-permute-start | bytes 2359304 | tf_op jit(solution)/shard_map/ppermute | solution.py:697
  388.4 51.2 %collective-permute-start.17 = (bf16[1024,384]{1,0:T(8,128)(2,1)}, bf16[1024,384]{1,0:T(8,128)(2,1)S(1)}, u32[]{:S(2)}, u32[]{:S(2)}) collective-permute-start(bf16[1024,384]{1,0:T(8,128)(2,1)} %bitcast.226), channel_id=1, source_target_pairs={{0,3},{1,0},{2,1},{3,2},{4,7},{5,4},{6,5},{7,6},{8,11},{9,8},{10,9... | collective-permute-start | bytes 2359304 | tf_op jit(solution)/shard_map/ppermute | solution.py:697
  434.1 19.6 %collective-permute-start.19 = (bf16[192,1024]{1,0:T(8,128)(2,1)}, bf16[192,1024]{1,0:T(8,128)(2,1)S(1)}, u32[]{:S(2)}, u32[]{:S(2)}) collective-permute-start(bf16[192,1024]{1,0:T(8,128)(2,1)} %bitcast.229), channel_id=1, source_target_pairs={{0,1},{1,2},{2,3},{3,0},{4,5},{5,6},{6,7},{7,4},{8,9},{9,10},{10,1... | collective-permute-start | bytes 1179656 | tf_op jit(solution)/shard_map/ppermute | solution.py:697
  434.2 31.4 %collective-permute-start.18 = (bf16[192,1024]{1,0:T(8,128)(2,1)}, bf16[192,1024]{1,0:T(8,128)(2,1)S(1)}, u32[]{:S(2)}, u32[]{:S(2)}) collective-permute-start(bf16[192,1024]{1,0:T(8,128)(2,1)} %bitcast.228), channel_id=1, source_target_pairs={{0,2},{1,3},{2,0},{3,1},{4,6},{5,7},{6,4},{7,5},{8,10},{9,11},{10,... | collective-permute-start | bytes 1179656 | tf_op jit(solution)/shard_map/ppermute | solution.py:697
  445.5 23.4 %collective-permute-start.20 = (bf16[192,1024]{1,0:T(8,128)(2,1)}, bf16[192,1024]{1,0:T(8,128)(2,1)S(1)}, u32[]{:S(2)}, u32[]{:S(2)}) collective-permute-start(bf16[192,1024]{1,0:T(8,128)(2,1)} %bitcast.230), channel_id=1, source_target_pairs={{0,3},{1,0},{2,1},{3,2},{4,7},{5,4},{6,5},{7,6},{8,11},{9,8},{10,9... | collective-permute-start | bytes 1179656 | tf_op jit(solution)/shard_map/ppermute | solution.py:697
  483.9 11.9 %collective-permute-start.21 = (bf16[576,896]{1,0:T(8,128)(2,1)}, bf16[576,896]{1,0:T(8,128)(2,1)}, u32[]{:S(2)}, u32[]{:S(2)}) collective-permute-start(bf16[576,896]{1,0:T(8,128)(2,1)} %get-tuple-element.193), channel_id=1, source_target_pairs={{0,4},{4,0},{8,12},{12,8},{16,20},{20,16},{24,28},{28,24},{1,5},{5... | collective-permute-start | bytes 3096584 | tf_op jit(solution)/shard_map/ppermute | solution.py:714
  503.2 38.8 %collective-permute-start.23 = (bf16[1024,768]{1,0:T(8,128)(2,1)}, bf16[1024,768]{1,0:T(8,128)(2,1)}, u32[]{:S(2)}, u32[]{:S(2)}) collective-permute-start(bf16[1024,768]{1,0:T(8,128)(2,1)} %add_input_gradients.3), channel_id=1, source_target_pairs={{0,1},{1,2},{2,3},{3,0},{4,5},{5,6},{6,7},{7,4},{8,9},{9,10},{10,1... | collective-permute-start | bytes 4718600 | tf_op jit(solution)/shard_map/ppermute | solution.py:697
  508.4 24.9 %collective-permute-start.22 = (bf16[576,896]{1,0:T(8,128)(2,1)S(1)}, bf16[576,896]{1,0:T(8,128)(2,1)}, u32[]{:S(2)}, u32[]{:S(2)}) collective-permute-start(bf16[576,896]{1,0:T(8,128)(2,1)S(1)} %add_convert_fusion.4), channel_id=1, source_target_pairs={{0,8},{4,12},{8,0},{12,4},{16,24},{20,28},{24,16},{28,20},{1,9},{5... | collective-permute-start | bytes 3096584 | tf_op jit(solution)/shard_map/ppermute | solution.py:714
  543.0 39.2 %collective-permute-start.28 = (bf16[1024,768]{1,0:T(8,128)(2,1)}, bf16[1024,768]{1,0:T(8,128)(2,1)}, u32[]{:S(2)}, u32[]{:S(2)}) collective-permute-start(bf16[1024,768]{1,0:T(8,128)(2,1)} %collective-permute-done.23), channel_id=1, source_target_pairs={{0,1},{1,2},{2,3},{3,0},{4,5},{5,6},{6,7},{7,4},{8,9},{9,10},{10,1... | collective-permute-start | bytes 4718600 | tf_op jit(solution)/shard_map/ppermute | solution.py:697
  546.0 24.0 %collective-permute-start.27 = (bf16[576,896]{1,0:T(8,128)(2,1)S(1)}, bf16[576,896]{1,0:T(8,128)(2,1)S(1)}, u32[]{:S(2)}, u32[]{:S(2)}) collective-permute-start(bf16[576,896]{1,0:T(8,128)(2,1)S(1)} %add_convert_fusion.3), channel_id=1, source_target_pairs={{0,16},{4,20},{8,24},{12,28},{16,0},{20,4},{24,8},{28,12},{1,17},{... | collective-permute-start | bytes 3096584 | tf_op jit(solution)/shard_map/ppermute | solution.py:714
  546.1 36.3 %collective-permute-start.24 = (bf16[32,512]{1,0:T(8,128)(2,1)S(1)}, bf16[32,512]{1,0:T(8,128)(2,1)S(1)}, u32[]{:S(2)}, u32[]{:S(2)}) collective-permute-start(bf16[32,512]{1,0:T(8,128)(2,1)S(1)} %slice.129), channel_id=1, source_target_pairs={{0,1},{1,2},{2,3},{3,0},{4,5},{5,6},{6,7},{7,4},{8,9},{9,10},{10,1... | collective-permute-start | bytes 98312 | tf_op jit(solution)/shard_map/ppermute | solution.py:697
  547.8 35.3 %collective-permute-start.25 = (bf16[32,512]{1,0:T(8,128)(2,1)S(1)}, bf16[32,512]{1,0:T(8,128)(2,1)S(1)}, u32[]{:S(2)}, u32[]{:S(2)}) collective-permute-start(bf16[32,512]{1,0:T(8,128)(2,1)S(1)} %slice.129), channel_id=1, source_target_pairs={{0,2},{1,3},{2,0},{3,1},{4,6},{5,7},{6,4},{7,5},{8,10},{9,11},{10,... | collective-permute-start | bytes 98312 | tf_op jit(solution)/shard_map/ppermute | solution.py:697
  549.0 34.1 %collective-permute-start.26 = (bf16[32,512]{1,0:T(8,128)(2,1)S(1)}, bf16[32,512]{1,0:T(8,128)(2,1)S(1)}, u32[]{:S(2)}, u32[]{:S(2)}) collective-permute-start(bf16[32,512]{1,0:T(8,128)(2,1)S(1)} %slice.129), channel_id=1, source_target_pairs={{0,3},{1,0},{2,1},{3,2},{4,7},{5,4},{6,5},{7,6},{8,11},{9,8},{10,9... | collective-permute-start | bytes 98312 | tf_op jit(solution)/shard_map/ppermute | solution.py:697
  584.6 38.3 %collective-permute-start.29 = (bf16[1024,768]{1,0:T(8,128)(2,1)}, bf16[1024,768]{1,0:T(8,128)(2,1)S(1)}, u32[]{:S(2)}, u32[]{:S(2)}) collective-permute-start(bf16[1024,768]{1,0:T(8,128)(2,1)} %collective-permute-done.28), channel_id=1, source_target_pairs={{0,1},{1,2},{2,3},{3,0},{4,5},{5,6},{6,7},{7,4},{8,9},{9,10},{10,1... | collective-permute-start | bytes 4718600 | tf_op jit(solution)/shard_map/ppermute | solution.py:697
  (56 other events, 875.2 us)
Sparse Core Ops, SparseCore 0:
  12.4 120.3 all-gather.4
  379.0 54.0 reduce-scatter.4
Sparse Core Ops, SparseCore 1:
  159.9 36.8 all-gather.6
  275.9 82.8 reduce-scatter.2
  469.0 39.7 all-gather.8

commit v5 on v4

--- a/solution.py
+++ b/solution.py
@@ -122,14 +122,14 @@
         k0 = pl.multiple_of(((first_tile + step) % 2) * bk, bk)
         return k0, k_ref[pl.ds(k0, bk), :]
 
-    def run(key_step, start, finish):
+    def run(key_step, start, finish, steps):
         def query_step(qb, unused):
             q0 = pl.multiple_of(qb * bq, bq)
             for h in range(heads):
                 own = slice(HD * h, HD * h + HD)
                 head_q[h, own, :] = qt_ref[own, pl.ds(q0, bq)]
             acc[...] = jnp.zeros_like(acc)
-            done = lax.fori_loop(0, tile_count, key_step, start)
+            done = lax.fori_loop(0, steps, key_step, start)
             for h in range(heads):
                 total, lse = finish(done[h])
                 ot_ref[HD * h : HD * h + HD, pl.ds(q0, bq)] = (acc[h] * (1.0 / total)).astype(
@@ -152,12 +152,17 @@
             return tuple(kept)
 
         start = tuple(jnp.zeros((1, bq), f32) for _ in range(heads))
-        run(key_step, start, lambda total: (total, jnp.log2(total)))
+        run(key_step, start, lambda total: (total, jnp.log2(total)), tile_count)
 
     @pl.when(jnp.logical_not(small_scores))
     def shifted():
+        small = min(512, bk)
+        cuts = bk // small
+
         def key_step(step, carry):
-            k0, keys = key_tile(step)
+            tile = (first_tile + step // cuts) % 2
+            k0 = pl.multiple_of(tile * bk + (step % cuts) * small, small)
+            keys = k_ref[pl.ds(k0, small), :]
             kept = []
             for h in range(heads):
                 scores = matmul(keys, head_q[h])
@@ -166,14 +171,16 @@
                 weights = jnp.exp2(scores - new_top)
                 fade = jnp.exp2(top - new_top)
                 total = fade * total + jnp.sum(weights, axis=0, keepdims=True)
-                acc[h] = fade * acc[h] + matmul(head_values(h, k0), weights.astype(bf16))
+                values_t = vt_ref[HD * h : HD * h + HD, pl.ds(k0, small)]
+                acc[h] = fade * acc[h] + matmul(values_t, weights.astype(bf16))
                 kept.append((new_top, total))
             return tuple(kept)
 
         start = tuple(
             (jnp.full((1, bq), mask_fill, f32), jnp.zeros((1, bq), f32)) for _ in range(heads)
         )
-        run(key_step, start, lambda pair: (pair[1], pair[0] + jnp.log2(pair[1])))
+        finish = lambda pair: (pair[1], pair[0] + jnp.log2(pair[1]))
+        run(key_step, start, finish, tile_count * cuts)
 
 
 def attend_forward(info, norms, wide_k, projected_t, chunk, chunks):
@@ -214,6 +221,7 @@
 def backward_kernel(bq, heads, q_span, k_span, rows, has, end_q, end_k, *refs):
     width = HD * heads
     one_key = k_span[1] - k_span[0] == 1
+    one_query = q_span[1] - q_span[0] == 1
     refs = list(refs)
     info_ref, k_ref, v_ref, kt_ref, qt_ref, got_ref, ot_ref, lse_ref = refs[:8]
     del refs[:8]
@@ -245,7 +253,8 @@
         def query_step(qb, inner):
             q0 = pl.multiple_of(qb * bq, bq)
             span = pl.ds(q0, bq)
-            all_span = pl.ds(pl.multiple_of(q * rows + q0, bq), bq)
+            first_row = q0 if one_query else q * rows + q0
+            all_span = pl.ds(pl.multiple_of(first_row, bq), bq)
             deltas = []
             tops = []
             for h in range(heads):
@@ -356,6 +365,11 @@
     else:
         key_spec = pl.BlockSpec((slot_len, PLANE), lambda i: (0, 0))
         kt_spec = pl.BlockSpec((width, slot_len), lambda i: (1, 0))
+    q_at = q_span[0]
+    if nq == 1:
+        qt_spec = pl.BlockSpec((width, rows), lambda i: (0, q_at))
+    else:
+        qt_spec = pl.BlockSpec((width, slot_len), lambda i: (0, 0))
     at_zero = lambda i: (0, 0, 0)
     gq_shape, gk_shape = (nq, width, rows), (nk, rows, PLANE)
     gq_spec, gk_spec = pl.BlockSpec(gq_shape, at_zero), pl.BlockSpec(gk_shape, at_zero)
@@ -366,7 +380,7 @@
         key_spec,
         key_spec,
         kt_spec,
-        pl.BlockSpec((width, slot_len), lambda i: (0, 0)),
+        qt_spec,
         gq_spec,
         gq_spec,
         pl.BlockSpec((nq, 8, rows), at_zero),
@@ -733,13 +747,6 @@
     return lax.dynamic_slice_in_dim(shard, lax.axis_index("dp") * part, part, 0)
 
 
-def spread_gather(shard):
-    mine = spread_parts(shard)
-    part, dp_size = mine.shape[0], lax.axis_size("dp")
-    whole = lax.all_gather(mine, ("tensor", "dp"), axis=0, tiled=True)
-    return whole.reshape(lax.axis_size("tensor"), part * dp_size, shard.shape[1])
-
-
 def body(
     hidden_in,
     lengths,
@@ -781,10 +788,7 @@
 
     w_kv = jnp.concatenate([w_key, w_value], axis=1)
     w_project_t = jnp.concatenate([w_query.T, w_key.T, w_value.T], axis=0)
-    gathered = spread_gather(jnp.concatenate([w_in, w_down, w_out], axis=0))
-    w_out_all = gathered[:, model + hidden_width : model + hidden_width + width].reshape(
-        group_size * width, model
-    )
+    main = send_tiles(spread_parts(jnp.concatenate([w_in, w_down, w_out], axis=0)), group_size)
     tile = jnp.concatenate(
         [
             spread_parts(w_project_t),
@@ -824,6 +828,9 @@
         outs[s], lses[s] = attend_forward(info, norms, wide_k, projected_t, s, group_size)
         attended[s] = shift(outs[s], s, group_size)
         if step == 0:
+            *main, projected_t = lax.optimization_barrier((*main, projected_t))
+            gathered = lax.all_gather(order_tiles(main, rank), "dp", axis=1, tiled=True)
+        if step == 1:
             *found, projected_t = lax.optimization_barrier((*found, projected_t))
             tiles = order_tiles(found, rank)
             part = tile.shape[0] - stu_cols - 16
@@ -833,6 +840,9 @@
             attended[order[0]], attended[order[1]], projected_t = lax.optimization_barrier(
                 (attended[order[0]], attended[order[1]], projected_t)
             )
+    w_out_all = gathered[:, model + hidden_width : model + hidden_width + width].reshape(
+        group_size * width, model
+    )
     w_stud_t = stud_tiles[:, :stu_cols].reshape(group_size * stu_cols, model)
     b_in_all = stud_tiles[:, stu_cols : stu_cols + 1]
     b_stud_all = stud_tiles[:, stu_cols + 1, :stu_cols].reshape(1, group_size * stu_cols)

time: 643 us -> 664 us (1.033)
  the two profiles are of different devices: /device:TPU:6 before, /device:TPU:0 now
where the time goes in v5:
time: 664 us; the launch traced here: 653 us
  Pallas kernels  320 us (48%)
  waiting for transfers between devices  163 us (25%)
  starting transfers between devices  53.4 us (8%)
  local copies, waits for them, and re-layouts  49.5 us (7%)
  other arithmetic  37.1 us (6%)
  between operations  17.7 us (3%)
  matrix products  13 us (2%)
    pallas_call x8, Pallas kernels, attend_backward(): pl.pallas_call(functools.partial(backward_kernel, bq, heads, q_span, k_sp...  179 us
    ppermute x30, waiting for transfers between devices, shift(): return lax.ppermute(array, 'tensor', moves)  95.5 us
    pallas_call x4, Pallas kernels, attend_forward(): pl.pallas_call(functools.partial(forward_kernel, bq, bk, heads), grid=(1,...  59.3 us
    ppermute x30, starting transfers between devices, shift(): return lax.ppermute(array, 'tensor', moves)  49.6 us
    reduce_scatter x1, waiting for transfers between devices, body(): lax.psum_scatter(blocks.reshape(dp_size * group_size, part, model), 'dp',...  34 us
    ppermute x3, waiting for transfers between devices, exchange_add(): came = lax.ppermute(array, 'dp', moves)  33.3 us
    pallas_call x1, Pallas kernels, pack_gradients(): pl.pallas_call(functools.partial(pack_kernel, dp_size, part), grid=(group...  20.2 us
    pallas_call x1, Pallas kernels, ffn_forward(): pl.pallas_call(functools.partial(ffn_forward_kernel, min(256, count)), gr...  18 us
  transfers between devices with their start and end apart: 38, of which 16 were waited for; matrix products, arithmetic and copies ran while one was open for 12% of the time, Pallas kernels for 49%

profile of v5, /device:TPU:0, one launch (start us, length us, event | category | flops | bytes accessed | tf_op | source)
XLA Modules:
  0.0 653.4 jit_solution(15271547852397857715)
XLA Ops:
  23.1 11.8 %project.1 = (bf16[4096,768]{1,0:T(8,128)(2,1)}, bf16[4096,256]{1,0:T(8,128)(2,1)}, bf16[4096,256]{1,0:T(8,128)(2,1)}, bf16[576,4096]{1,0:T(8,128)(2,1)}, f32[4,8,128]{2,1,0:T(8,128)}) custom-call(s32[7]{0:T(128)} %pad_add_fusion.info_ref.refs_0_.rank_ref, bf16[4096,768]{1,0:T(8,128)(2,1)} %h_ref.1, bf16[768,384]{1,0:T(8,128)(2,1)} %pad_maximum_fusion.3.wkv_ref, ...), custom_call_target="tpu_custom_call" | custom-call | flops 1 | bytes 1 | tf_op jit(solution)/shard_map/project/pallas_call | solution.py:72
  40.1 7.9 %collective-permute-start.5 = (bf16[128,768]{1,0:T(8,128)(2,1)S(1)}, bf16[128,768]{1,0:T(8,128)(2,1)S(1)}, u32[]{:S(2)}, u32[]{:S(2)}) collective-permute-start(bf16[128,768]{1,0:T(8,128)(2,1)S(1)} %concatenate.30), channel_id=1, source_target_pairs={{0,1},{1,2},{2,3},{3,0},{4,5},{5,6},{6,7},{7,4},{8,9},{9,10},{10,1... | collective-permute-start | bytes 589832 | tf_op jit(solution)/shard_map/ppermute | solution.py:711
  50.5 14.7 %attend_forward.4 = (bf16[192,1024]{1,0:T(8,128)(2,1)}, f32[8,1024]{1,0:T(8,128)}) custom-call(s32[7]{0:T(128)} %pad_add_fusion.info_ref.refs_0_.rank_ref, f32[4,8,128]{2,1,0:T(8,128)} %get-tuple-element.129.n_ref, bf16[4096,256]{1,0:T(8,128)(2,1)} %get-tuple-element.127.k_ref.refs_1_, bf16[576,4096]{1,0:T(8,128)(2,1)} %get-tuple-element.135.qt_ref.vt_ref.refs_3_.refs_4_, ...), custom_call_target="tpu_custom_call" | custom-call | flops 1 | bytes 1 | tf_op jit(solution)/shard_map/attend_forward/pallas_call | solution.py:193
  66.0 15.1 %attend_forward.5 = (bf16[192,1024]{1,0:T(8,128)(2,1)}, f32[8,1024]{1,0:T(8,128)}) custom-call(s32[7]{0:T(128)} %pad_add_fusion.info_ref.refs_0_.rank_ref, f32[4,8,128]{2,1,0:T(8,128)} %get-tuple-element.129.n_ref, bf16[4096,256]{1,0:T(8,128)(2,1)} %get-tuple-element.127.k_ref.refs_1_, bf16[576,4096]{1,0:T(8,128)(2,1)} %get-tuple-element.135.qt_ref.vt_ref.refs_3_.refs_4_, ...), custom_call_target="tpu_custom_call" | custom-call | flops 1 | bytes 1 | tf_op jit(solution)/shard_map/attend_forward/pallas_call | solution.py:193
  83.0 14.7 %attend_forward.7 = (bf16[192,1024]{1,0:T(8,128)(2,1)}, f32[8,1024]{1,0:T(8,128)}) custom-call(s32[7]{0:T(128)} %pad_add_fusion.info_ref.refs_0_.rank_ref, f32[4,8,128]{2,1,0:T(8,128)} %get-tuple-element.129.n_ref, bf16[4096,256]{1,0:T(8,128)(2,1)} %get-tuple-element.127.k_ref.refs_1_, bf16[576,4096]{1,0:T(8,128)(2,1)} %get-tuple-element.135.qt_ref.vt_ref.refs_3_.refs_4_, ...), custom_call_target="tpu_custom_call" | custom-call | flops 1 | bytes 1 | tf_op jit(solution)/shard_map/attend_forward/pallas_call | solution.py:193
  101.4 14.8 %attend_forward.6 = (bf16[192,1024]{1,0:T(8,128)(2,1)}, f32[8,1024]{1,0:T(8,128)}) custom-call(s32[7]{0:T(128)} %pad_add_fusion.info_ref.refs_0_.rank_ref, f32[4,8,128]{2,1,0:T(8,128)} %get-tuple-element.129.n_ref, bf16[4096,256]{1,0:T(8,128)(2,1)} %get-tuple-element.127.k_ref.refs_1_, bf16[576,4096]{1,0:T(8,128)(2,1)} %get-tuple-element.135.qt_ref.vt_ref.refs_3_.refs_4_, ...), custom_call_target="tpu_custom_call" | custom-call | flops 1 | bytes 1 | tf_op jit(solution)/shard_map/attend_forward/pallas_call | solution.py:193
  123.0 3.9 fusion.36
  129.5 18.0 %ffn_forward.1 = (bf16[4,1024,768]{2,1,0:T(8,128)(2,1)}, bf16[4,1024,768]{2,1,0:T(8,128)(2,1)}, f32[1024,768]{1,0:T(8,128)}) custom-call(bf16[1024,768]{1,0:T(8,128)(2,1)} %add_convert_fusion.1.x_ref.first_ref, bf16[4,1792,768]{2,1,0:T(8,128)(2,1)} %all-gather.5.cloned.1.call-done.w_in_ref.w_down_ref, bf16[4,1,768]{2,1,0:T(2,128)(2,1)} %slice.161.b_ref, ...), custom_call_target="tpu_custom_call" | custom-call | flops 1 | bytes 1 | tf_op jit(solution)/shard_map/ffn_forward/pallas_call | solution.py:501
  170.4 5.2 multiply_reduce_fusion
  179.6 16.2 %ffn_backward.1 = (bf16[4,1024,768]{2,1,0:T(8,128)(2,1)}, f32[1024,768]{1,0:T(8,128)}) custom-call(bf16[1024,768]{1,0:T(8,128)(2,1)} %convert_element_type.119.g_ref.gffn_ref, bf16[4,1792,768]{2,1,0:T(8,128)(2,1)} %all-gather.5.cloned.1.call-done.w_in_ref.w_down_ref, bf16[4,1792,768]{2,1,0:T(8,128)(2,1)} %all-gather.5.cloned.1.call-done.w_in_ref.w_down_ref, ...), custom_call_target="tpu_custom_call" | custom-call | flops 1 | bytes 1 | tf_op jit(solution)/shard_map/ffn_backward/pallas_call | solution.py:540
  197.6 3.8 multiply_reduce_fusion.1
  213.5 20.2 %pack_gradients.1 = bf16[8,4,224,768]{3,2,1,0:T(8,128)(2,1)} custom-call(bf16[1024,768]{1,0:T(8,128)(2,1)} %add_convert_fusion.1.x_ref.first_ref, bf16[4,1024,768]{2,1,0:T(8,128)(2,1)} %get-tuple-element.152.gpre_ref, bf16[4,1024,768]{2,1,0:T(8,128)(2,1)} %get-tuple-element.153.act_ref, bf16[1024,768]{1,0:T(8,128)(2,1)} %convert_element_type.119.g_ref.gffn_ref, ...), custom_call_target="tpu_custom_call" | custom-call | flops 1 | bytes 1 | tf_op jit(solution)/shard_map/pack_gradients/pallas_call | solution.py:648
  233.7 12.3 %collective-permute-done.14 = bf16[192,1024]{1,0:T(8,128)(2,1)S(1)} collective-permute-done((bf16[192,1024]{1,0:T(8,128)(2,1)S(1)}, bf16[192,1024]{1,0:T(8,128)(2,1)S(1)}, u32[]{:S(2)}, u32[]{:S(2)}) %collective-permute-start.14) | collective-permute-done | bytes 393248 | tf_op jit(solution)/shard_map/ppermute | solution.py:711
  247.0 30.8 %attend_backward.8 = (f32[1,192,1024]{2,1,0:T(8,128)}, f32[3,1024,256]{2,1,0:T(8,128)}, f32[3,1024,256]{2,1,0:T(8,128)}) custom-call(s32[7]{0:T(128)} %pad_add_fusion.info_ref.refs_0_.rank_ref, bf16[4096,256]{1,0:T(8,128)(2,1)} %get-tuple-element.127.k_ref.refs_1_, bf16[4096,256]{1,0:T(8,128)(2,1)} %get-tuple-element.128.refs_2_, ...), custom_call_target="tpu_custom_call" | custom-call | flops 1 | bytes 1 | tf_op jit(solution)/shard_map/attend_backward/pallas_call | solution.py:427
  281.8 30.5 %attend_backward.9 = (f32[3,192,1024]{2,1,0:T(8,128)}, bf16[1,1024,384]{2,1,0:T(8,128)(2,1)}, f32[384,896]{1,0:T(8,128)}) custom-call(s32[7]{0:T(128)} %pad_add_fusion.info_ref.refs_0_.rank_ref, bf16[4096,256]{1,0:T(8,128)(2,1)} %get-tuple-element.127.k_ref.refs_1_, bf16[4096,256]{1,0:T(8,128)(2,1)} %get-tuple-element.128.refs_2_, ...), custom_call_target="tpu_custom_call" | custom-call | flops 1 | bytes 1 | tf_op jit(solution)/shard_map/attend_backward/pallas_call | solution.py:427
  312.3 4.3 collective-permute-start.18
  316.6 31.6 %attend_backward.10 = (f32[3,192,1024]{2,1,0:T(8,128)}, bf16[1,1024,384]{2,1,0:T(8,128)(2,1)}, f32[384,896]{1,0:T(8,128)}) custom-call(s32[7]{0:T(128)} %pad_add_fusion.info_ref.refs_0_.rank_ref, bf16[4096,256]{1,0:T(8,128)(2,1)} %get-tuple-element.127.k_ref.refs_1_, bf16[4096,256]{1,0:T(8,128)(2,1)} %get-tuple-element.128.refs_2_, ...), custom_call_target="tpu_custom_call" | custom-call | flops 1 | bytes 1 | tf_op jit(solution)/shard_map/attend_backward/pallas_call | solution.py:427
  348.2 20.2 %collective-permute-done.18.refs_0_ = bf16[1024,384]{1,0:T(8,128)(2,1)S(1)} collective-permute-done((bf16[1024,384]{1,0:T(8,128)(2,1)}, bf16[1024,384]{1,0:T(8,128)(2,1)S(1)}, u32[]{:S(2)}, u32[]{:S(2)}) %collective-permute-start.18) | collective-permute-done | bytes 786464 | tf_op jit(solution)/shard_map/ppermute | solution.py:711
  368.4 34.0 %reduce-scatter.3.cloned.1.call-done = bf16[4,224,768]{2,1,0:T(8,128)(2,1)} async-done(((bf16[32,224,768]{2,1,0:T(8,128)(2,1)}), bf16[4,224,768]{2,1,0:T(8,128)(2,1)}) %reduce-scatter.3.cloned.1.call-update) | async-done | bytes 1376272 | tf_op jit(solution)/shard_map/reduce_scatter | solution.py:966
  404.2 31.7 %attend_backward.11 = (f32[3,192,1024]{2,1,0:T(8,128)}, bf16[1,1024,384]{2,1,0:T(8,128)(2,1)}, f32[384,896]{1,0:T(8,128)}) custom-call(s32[7]{0:T(128)} %pad_add_fusion.info_ref.refs_0_.rank_ref, bf16[4096,256]{1,0:T(8,128)(2,1)} %get-tuple-element.127.k_ref.refs_1_, bf16[4096,256]{1,0:T(8,128)(2,1)} %get-tuple-element.128.refs_2_, ...), custom_call_target="tpu_custom_call" | custom-call | flops 1 | bytes 1 | tf_op jit(solution)/shard_map/attend_backward/pallas_call | solution.py:427
  438.2 12.5 %attend_backward.12 = (bf16[1,192,1024]{2,1,0:T(8,128)(2,1)}, f32[1,1024,256]{2,1,0:T(8,128)}, f32[1,1024,256]{2,1,0:T(8,128)}, f32[192,896]{1,0:T(8,128)}) custom-call(s32[7]{0:T(128)} %pad_add_fusion.info_ref.refs_0_.rank_ref, bf16[4096,256]{1,0:T(8,128)(2,1)} %get-tuple-element.127.k_ref.refs_1_, bf16[4096,256]{1,0:T(8,128)(2,1)} %get-tuple-element.128.refs_2_, ...), custom_call_target="tpu_custom_call" | custom-call | flops 1 | bytes 1 | tf_op jit(solution)/shard_map/attend_backward/pallas_call | solution.py:427
  450.7 13.9 %attend_backward.13 = (bf16[1,192,1024]{2,1,0:T(8,128)(2,1)}, f32[1,1024,256]{2,1,0:T(8,128)}, f32[1,1024,256]{2,1,0:T(8,128)}, f32[192,896]{1,0:T(8,128)}) custom-call(s32[7]{0:T(128)} %pad_add_fusion.info_ref.refs_0_.rank_ref, bf16[4096,256]{1,0:T(8,128)(2,1)} %get-tuple-element.127.k_ref.refs_1_, bf16[4096,256]{1,0:T(8,128)(2,1)} %get-tuple-element.128.refs_2_, ...), custom_call_target="tpu_custom_call" | custom-call | flops 1 | bytes 1 | tf_op jit(solution)/shard_map/attend_backward/pallas_call | solution.py:427
  468.2 13.5 %attend_backward.14 = (bf16[1,192,1024]{2,1,0:T(8,128)(2,1)}, f32[1,1024,256]{2,1,0:T(8,128)}, f32[1,1024,256]{2,1,0:T(8,128)}, f32[192,896]{1,0:T(8,128)}) custom-call(s32[7]{0:T(128)} %pad_add_fusion.info_ref.refs_0_.rank_ref, bf16[4096,256]{1,0:T(8,128)(2,1)} %get-tuple-element.127.k_ref.refs_1_, bf16[4096,256]{1,0:T(8,128)(2,1)} %get-tuple-element.128.refs_2_, ...), custom_call_target="tpu_custom_call" | custom-call | flops 1 | bytes 1 | tf_op jit(solution)/shard_map/attend_backward/pallas_call | solution.py:427
  482.1 7.6 %add_input_gradients.2.sum_ref = f32[1024,768]{1,0:T(8,128)} custom-call(s32[7]{0:T(128)} %pad_add_fusion.info_ref.refs_0_.rank_ref, f32[1024,768]{1,0:T(8,128)} %copy-done.4, bf16[4,640,768]{2,1,0:T(8,128)(2,1)} %all-gather.7.cloned.1.call-done.w_ref, bf16[1024,384]{1,0:T(8,128)(2,1)} %copy-done.27, bf16[1024,384]{1,0:T(8,128)(2,1)} %copy-done.28, ...), custom_call_target="tpu_custom_call" | custom-call | flops 1 | bytes 1 | tf_op jit(solution)/shard_map/add_input_gradients/pallas_call | solution.py:461
  490.1 10.9 %collective-permute-done.23.refs_3_ = bf16[192,1024]{1,0:T(8,128)(2,1)S(1)} collective-permute-done((bf16[192,1024]{1,0:T(8,128)(2,1)}, bf16[192,1024]{1,0:T(8,128)(2,1)S(1)}, u32[]{:S(2)}, u32[]{:S(2)}) %collective-permute-start.23) | collective-permute-done | bytes 393248 | tf_op jit(solution)/shard_map/ppermute | solution.py:711
  501.0 14.7 %attend_backward.15 = (bf16[1,192,1024]{2,1,0:T(8,128)(2,1)}, bf16[1,1024,384]{2,1,0:T(8,128)(2,1)}, bf16[576,896]{1,0:T(8,128)(2,1)}) custom-call(s32[7]{0:T(128)} %pad_add_fusion.info_ref.refs_0_.rank_ref, bf16[4096,256]{1,0:T(8,128)(2,1)} %get-tuple-element.127.k_ref.refs_1_, bf16[4096,256]{1,0:T(8,128)(2,1)} %get-tuple-element.128.refs_2_, ...), custom_call_target="tpu_custom_call" | custom-call | flops 1 | bytes 1 | tf_op jit(solution)/shard_map/attend_backward/pallas_call | solution.py:427
  518.8 7.4 %add_input_gradients.3 = bf16[1024,768]{1,0:T(8,128)(2,1)} custom-call(s32[7]{0:T(128)} %pad_add_fusion.info_ref.refs_0_.rank_ref, f32[1024,768]{1,0:T(8,128)} %add_input_gradients.2.sum_ref, bf16[4,640,768]{2,1,0:T(8,128)(2,1)} %all-gather.7.cloned.1.call-done.w_ref, bf16[1024,384]{1,0:T(8,128)(2,1)} %bitcast.197, bf16[192,1024]{1,0:T(8,128)(2,1)} %copy-done.31, ...), custom_call_target="tpu_custom_call" | custom-call | flops 1 | bytes 1 | tf_op jit(solution)/shard_map/add_input_gradients/pallas_call | solution.py:461
  536.7 18.1 %collective-permute-done.25 = bf16[576,896]{1,0:T(8,128)(2,1)} collective-permute-done((bf16[576,896]{1,0:T(8,128)(2,1)S(1)}, bf16[576,896]{1,0:T(8,128)(2,1)}, u32[]{:S(2)}, u32[]{:S(2)}) %collective-permute-start.25) | collective-permute-done | bytes 1032224 | tf_op jit(solution)/shard_map/ppermute | solution.py:728
  554.7 10.0 %collective-permute-done.26 = bf16[1024,768]{1,0:T(8,128)(2,1)} collective-permute-done((bf16[1024,768]{1,0:T(8,128)(2,1)}, bf16[1024,768]{1,0:T(8,128)(2,1)}, u32[]{:S(2)}, u32[]{:S(2)}) %collective-permute-start.26) | collective-permute-done | bytes 1572896 | tf_op jit(solution)/shard_map/ppermute | solution.py:711
  580.9 12.3 %collective-permute-done.30 = bf16[576,896]{1,0:T(8,128)(2,1)S(1)} collective-permute-done((bf16[576,896]{1,0:T(8,128)(2,1)S(1)}, bf16[576,896]{1,0:T(8,128)(2,1)S(1)}, u32[]{:S(2)}, u32[]{:S(2)}) %collective-permute-start.30) | collective-permute-done | bytes 1032224 | tf_op jit(solution)/shard_map/ppermute | solution.py:728
  593.2 11.4 %collective-permute-done.31 = bf16[1024,768]{1,0:T(8,128)(2,1)} collective-permute-done((bf16[1024,768]{1,0:T(8,128)(2,1)}, bf16[1024,768]{1,0:T(8,128)(2,1)}, u32[]{:S(2)}, u32[]{:S(2)}) %collective-permute-start.31) | collective-permute-done | bytes 1572896 | tf_op jit(solution)/shard_map/ppermute | solution.py:711
  619.8 25.6 %collective-permute-done.32 = bf16[1024,768]{1,0:T(8,128)(2,1)S(1)} collective-permute-done((bf16[1024,768]{1,0:T(8,128)(2,1)}, bf16[1024,768]{1,0:T(8,128)(2,1)S(1)}, u32[]{:S(2)}, u32[]{:S(2)}) %collective-permute-start.32) | collective-permute-done | bytes 1572896 | tf_op jit(solution)/shard_map/ppermute | solution.py:711
  (312 shorter events, 136.1 us)
Async XLA Ops:
  7.3 114.4 %all-gather.5.cloned.1.call-start = ((), (), s32[]{:S(2)}) async-start(), calls=%async_computation.2 | async-start | bytes 12386304 | tf_op jit(solution)/shard_map/all_gather | solution.py:832
  8.9 26.2 %collective-permute-start.1 = (bf16[224,768]{1,0:T(8,128)(2,1)S(1)}, bf16[224,768]{1,0:T(8,128)(2,1)S(1)}, u32[]{:S(2)}, u32[]{:S(2)}) collective-permute-start(bf16[224,768]{1,0:T(8,128)(2,1)S(1)} %fusion.13), channel_id=1, source_target_pairs={{0,1},{1,2},{2,3},{3,0},{4,5},{5,6},{6,7},{7,4},{8,9},{9,10},{10,1... | collective-permute-start | bytes 1032200 | tf_op jit(solution)/shard_map/ppermute | solution.py:711
  12.0 25.0 %collective-permute-start.2 = (bf16[224,768]{1,0:T(8,128)(2,1)S(1)}, bf16[224,768]{1,0:T(8,128)(2,1)S(1)}, u32[]{:S(2)}, u32[]{:S(2)}) collective-permute-start(bf16[224,768]{1,0:T(8,128)(2,1)S(1)} %fusion.13), channel_id=1, source_target_pairs={{0,2},{1,3},{2,0},{3,1},{4,6},{5,7},{6,4},{7,5},{8,10},{9,11},{10,... | collective-permute-start | bytes 1032200 | tf_op jit(solution)/shard_map/ppermute | solution.py:711
  14.5 22.4 %collective-permute-start.3 = (bf16[224,768]{1,0:T(8,128)(2,1)S(1)}, bf16[224,768]{1,0:T(8,128)(2,1)S(1)}, u32[]{:S(2)}, u32[]{:S(2)}) collective-permute-start(bf16[224,768]{1,0:T(8,128)(2,1)S(1)} %fusion.13), channel_id=1, source_target_pairs={{0,3},{1,0},{2,1},{3,2},{4,7},{5,4},{6,5},{7,6},{8,11},{9,8},{10,9... | collective-permute-start | bytes 1032200 | tf_op jit(solution)/shard_map/ppermute | solution.py:711
  39.8 193.9 %all-gather.7.cloned.1.call-start = ((), (), s32[]{:S(2)}) async-start(), calls=%async_computation.3 | async-start | bytes 4423680 | tf_op jit(solution)/shard_map/all_gather | solution.py:837
  40.1 40.9 %collective-permute-start.5 = (bf16[128,768]{1,0:T(8,128)(2,1)S(1)}, bf16[128,768]{1,0:T(8,128)(2,1)S(1)}, u32[]{:S(2)}, u32[]{:S(2)}) collective-permute-start(bf16[128,768]{1,0:T(8,128)(2,1)S(1)} %concatenate.30), channel_id=1, source_target_pairs={{0,1},{1,2},{2,3},{3,0},{4,5},{5,6},{6,7},{7,4},{8,9},{9,10},{10,1... | collective-permute-start | bytes 589832 | tf_op jit(solution)/shard_map/ppermute | solution.py:711
  48.0 33.0 %collective-permute-start.6 = (bf16[128,768]{1,0:T(8,128)(2,1)S(1)}, bf16[128,768]{1,0:T(8,128)(2,1)S(1)}, u32[]{:S(2)}, u32[]{:S(2)}) collective-permute-start(bf16[128,768]{1,0:T(8,128)(2,1)S(1)} %concatenate.30), channel_id=1, source_target_pairs={{0,2},{1,3},{2,0},{3,1},{4,6},{5,7},{6,4},{7,5},{8,10},{9,11},{10,... | collective-permute-start | bytes 589832 | tf_op jit(solution)/shard_map/ppermute | solution.py:711
  49.6 31.4 %collective-permute-start.7 = (bf16[128,768]{1,0:T(8,128)(2,1)S(1)}, bf16[128,768]{1,0:T(8,128)(2,1)S(1)}, u32[]{:S(2)}, u32[]{:S(2)}) collective-permute-start(bf16[128,768]{1,0:T(8,128)(2,1)S(1)} %concatenate.30), channel_id=1, source_target_pairs={{0,3},{1,0},{2,1},{3,2},{4,7},{5,4},{6,5},{7,6},{8,11},{9,8},{10,9... | collective-permute-start | bytes 589832 | tf_op jit(solution)/shard_map/ppermute | solution.py:711
  65.2 36.2 %collective-permute-start = (bf16[192,1024]{1,0:T(8,128)(2,1)}, bf16[192,1024]{1,0:T(8,128)(2,1)S(1)}, u32[]{:S(2)}, u32[]{:S(2)}) collective-permute-start(bf16[192,1024]{1,0:T(8,128)(2,1)} %get-tuple-element.131), channel_id=1, source_target_pairs={{0,2},{1,3},{2,0},{3,1},{4,6},{5,7},{6,4},{7,5},{8,10},{9,11},{10,... | collective-permute-start | bytes 1179656 | tf_op jit(solution)/shard_map/ppermute | solution.py:711
  97.6 23.2 %collective-permute-start.8 = (bf16[192,1024]{1,0:T(8,128)(2,1)}, bf16[192,1024]{1,0:T(8,128)(2,1)S(1)}, u32[]{:S(2)}, u32[]{:S(2)}) collective-permute-start(bf16[192,1024]{1,0:T(8,128)(2,1)} %get-tuple-element.143), channel_id=1, source_target_pairs={{0,3},{1,0},{2,1},{3,2},{4,7},{5,4},{6,5},{7,6},{8,11},{9,8},{10,9... | collective-permute-start | bytes 1179656 | tf_op jit(solution)/shard_map/ppermute | solution.py:711
  129.4 273.0 %reduce-scatter.3.cloned.1.call-start = ((), (), s32[]{:S(2)}) async-start(), calls=%async_computation.4 | async-start | bytes 12386304 | tf_op jit(solution)/shard_map/reduce_scatter | solution.py:966
  161.7 36.0 %collective-permute-start.12 = (bf16[1024,768]{1,0:T(8,128)(2,1)}, bf16[1024,768]{1,0:T(8,128)(2,1)}, u32[]{:S(2)}, u32[]{:S(2)}) collective-permute-start(bf16[1024,768]{1,0:T(8,128)(2,1)} %copy-done.7), channel_id=1, source_target_pairs={{0,1},{1,2},{2,3},{3,0},{4,5},{5,6},{6,7},{7,4},{8,9},{9,10},{10,1... | collective-permute-start | bytes 4718600 | tf_op jit(solution)/shard_map/ppermute | solution.py:711
  207.1 26.6 %collective-permute-start.13 = (bf16[192,1024]{1,0:T(8,128)(2,1)S(1)}, bf16[192,1024]{1,0:T(8,128)(2,1)S(1)}, u32[]{:S(2)}, u32[]{:S(2)}) collective-permute-start(bf16[192,1024]{1,0:T(8,128)(2,1)S(1)} %get-tuple-element.275), channel_id=1, source_target_pairs={{0,3},{1,0},{2,1},{3,2},{4,7},{5,4},{6,5},{7,6},{8,11},{9,8},{10,9... | collective-permute-start | bytes 1179656 | tf_op jit(solution)/shard_map/ppermute | solution.py:711
  210.3 35.6 %collective-permute-start.14 = (bf16[192,1024]{1,0:T(8,128)(2,1)S(1)}, bf16[192,1024]{1,0:T(8,128)(2,1)S(1)}, u32[]{:S(2)}, u32[]{:S(2)}) collective-permute-start(bf16[192,1024]{1,0:T(8,128)(2,1)S(1)} %get-tuple-element.274), channel_id=1, source_target_pairs={{0,2},{1,3},{2,0},{3,1},{4,6},{5,7},{6,4},{7,5},{8,10},{9,11},{10,... | collective-permute-start | bytes 1179656 | tf_op jit(solution)/shard_map/ppermute | solution.py:711
  210.6 35.4 %collective-permute-start.15 = (bf16[192,1024]{1,0:T(8,128)(2,1)S(1)}, bf16[192,1024]{1,0:T(8,128)(2,1)S(1)}, u32[]{:S(2)}, u32[]{:S(2)}) collective-permute-start(bf16[192,1024]{1,0:T(8,128)(2,1)S(1)} %get-tuple-element.273), channel_id=1, source_target_pairs={{0,1},{1,2},{2,3},{3,0},{4,5},{5,6},{6,7},{7,4},{8,9},{9,10},{10,1... | collective-permute-start | bytes 1179656 | tf_op jit(solution)/shard_map/ppermute | solution.py:711
  246.7 254.3 %reduce-scatter.5.cloned.1.call-start = ((), (), s32[]{:S(2)}) async-start(), calls=%async_computation.5 | async-start | bytes 1720320 | tf_op jit(solution)/shard_map/reduce_scatter | solution.py:998
  246.7 31.1 %collective-permute-start.16 = (bf16[1024,768]{1,0:T(8,128)(2,1)}, bf16[1024,768]{1,0:T(8,128)(2,1)S(1)}, u32[]{:S(2)}, u32[]{:S(2)}) collective-permute-start(bf16[1024,768]{1,0:T(8,128)(2,1)} %collective-permute-done.12), channel_id=1, source_target_pairs={{0,1},{1,2},{2,3},{3,0},{4,5},{5,6},{6,7},{7,4},{8,9},{9,10},{10,1... | collective-permute-start | bytes 4718600 | tf_op jit(solution)/shard_map/ppermute | solution.py:711
  277.8 90.6 %collective-permute-start.17 = (bf16[1024,768]{1,0:T(8,128)(2,1)S(1)}, bf16[1024,768]{1,0:T(8,128)(2,1)}, u32[]{:S(2)}, u32[]{:S(2)}) collective-permute-start(bf16[1024,768]{1,0:T(8,128)(2,1)S(1)} %collective-permute-done.16), channel_id=1, source_target_pairs={{0,1},{1,2},{2,3},{3,0},{4,5},{5,6},{6,7},{7,4},{8,9},{9,10},{10,1... | collective-permute-start | bytes 4718600 | tf_op jit(solution)/shard_map/ppermute | solution.py:711
  312.3 56.1 %collective-permute-start.18 = (bf16[1024,384]{1,0:T(8,128)(2,1)}, bf16[1024,384]{1,0:T(8,128)(2,1)S(1)}, u32[]{:S(2)}, u32[]{:S(2)}) collective-permute-start(bf16[1024,384]{1,0:T(8,128)(2,1)} %bitcast.229), channel_id=1, source_target_pairs={{0,2},{1,3},{2,0},{3,1},{4,6},{5,7},{6,4},{7,5},{8,10},{9,11},{10,... | collective-permute-start | bytes 2359304 | tf_op jit(solution)/shard_map/ppermute | solution.py:711
  402.4 162.4 %all-gather.9.cloned.1.call-start = ((), (), s32[]{:S(2)}) async-start(), calls=%async_computation.6 | async-start | bytes 3096576 | tf_op jit(solution)/shard_map/all_gather | solution.py:1030
  402.4 48.2 %collective-permute-start.19 = (bf16[1024,384]{1,0:T(8,128)(2,1)}, bf16[1024,384]{1,0:T(8,128)(2,1)S(1)}, u32[]{:S(2)}, u32[]{:S(2)}) collective-permute-start(bf16[1024,384]{1,0:T(8,128)(2,1)} %bitcast.227), channel_id=1, source_target_pairs={{0,1},{1,2},{2,3},{3,0},{4,5},{5,6},{6,7},{7,4},{8,9},{9,10},{10,1... | collective-permute-start | bytes 2359304 | tf_op jit(solution)/shard_map/ppermute | solution.py:711
  435.8 32.3 %collective-permute-start.20 = (bf16[1024,384]{1,0:T(8,128)(2,1)}, bf16[1024,384]{1,0:T(8,128)(2,1)S(1)}, u32[]{:S(2)}, u32[]{:S(2)}) collective-permute-start(bf16[1024,384]{1,0:T(8,128)(2,1)} %bitcast.228), channel_id=1, source_target_pairs={{0,3},{1,0},{2,1},{3,2},{4,7},{5,4},{6,5},{7,6},{8,11},{9,8},{10,9... | collective-permute-start | bytes 2359304 | tf_op jit(solution)/shard_map/ppermute | solution.py:711
  464.6 25.1 %collective-permute-start.22 = (bf16[192,1024]{1,0:T(8,128)(2,1)}, bf16[192,1024]{1,0:T(8,128)(2,1)S(1)}, u32[]{:S(2)}, u32[]{:S(2)}) collective-permute-start(bf16[192,1024]{1,0:T(8,128)(2,1)} %bitcast.231), channel_id=1, source_target_pairs={{0,1},{1,2},{2,3},{3,0},{4,5},{5,6},{6,7},{7,4},{8,9},{9,10},{10,1... | collective-permute-start | bytes 1179656 | tf_op jit(solution)/shard_map/ppermute | solution.py:711
  464.7 25.4 %collective-permute-start.21 = (bf16[192,1024]{1,0:T(8,128)(2,1)}, bf16[192,1024]{1,0:T(8,128)(2,1)S(1)}, u32[]{:S(2)}, u32[]{:S(2)}) collective-permute-start(bf16[192,1024]{1,0:T(8,128)(2,1)} %bitcast.230), channel_id=1, source_target_pairs={{0,2},{1,3},{2,0},{3,1},{4,6},{5,7},{6,4},{7,5},{8,10},{9,11},{10,... | collective-permute-start | bytes 1179656 | tf_op jit(solution)/shard_map/ppermute | solution.py:711
  526.2 38.5 %collective-permute-start.26 = (bf16[1024,768]{1,0:T(8,128)(2,1)}, bf16[1024,768]{1,0:T(8,128)(2,1)}, u32[]{:S(2)}, u32[]{:S(2)}) collective-permute-start(bf16[1024,768]{1,0:T(8,128)(2,1)} %add_input_gradients.3), channel_id=1, source_target_pairs={{0,1},{1,2},{2,3},{3,0},{4,5},{5,6},{6,7},{7,4},{8,9},{9,10},{10,1... | collective-permute-start | bytes 4718600 | tf_op jit(solution)/shard_map/ppermute | solution.py:711
  530.0 24.7 %collective-permute-start.25 = (bf16[576,896]{1,0:T(8,128)(2,1)S(1)}, bf16[576,896]{1,0:T(8,128)(2,1)}, u32[]{:S(2)}, u32[]{:S(2)}) collective-permute-start(bf16[576,896]{1,0:T(8,128)(2,1)S(1)} %add_convert_fusion.4), channel_id=1, source_target_pairs={{0,8},{4,12},{8,0},{12,4},{16,24},{20,28},{24,16},{28,20},{1,9},{5... | collective-permute-start | bytes 3096584 | tf_op jit(solution)/shard_map/ppermute | solution.py:728
  565.7 38.9 %collective-permute-start.31 = (bf16[1024,768]{1,0:T(8,128)(2,1)}, bf16[1024,768]{1,0:T(8,128)(2,1)}, u32[]{:S(2)}, u32[]{:S(2)}) collective-permute-start(bf16[1024,768]{1,0:T(8,128)(2,1)} %collective-permute-done.26), channel_id=1, source_target_pairs={{0,1},{1,2},{2,3},{3,0},{4,5},{5,6},{6,7},{7,4},{8,9},{9,10},{10,1... | collective-permute-start | bytes 4718600 | tf_op jit(solution)/shard_map/ppermute | solution.py:711
  567.4 25.8 %collective-permute-start.30 = (bf16[576,896]{1,0:T(8,128)(2,1)S(1)}, bf16[576,896]{1,0:T(8,128)(2,1)S(1)}, u32[]{:S(2)}, u32[]{:S(2)}) collective-permute-start(bf16[576,896]{1,0:T(8,128)(2,1)S(1)} %add_convert_fusion.3), channel_id=1, source_target_pairs={{0,16},{4,20},{8,24},{12,28},{16,0},{20,4},{24,8},{28,12},{1,17},{... | collective-permute-start | bytes 3096584 | tf_op jit(solution)/shard_map/ppermute | solution.py:728
  570.9 33.9 %collective-permute-start.27 = (bf16[32,512]{1,0:T(8,128)(2,1)S(1)}, bf16[32,512]{1,0:T(8,128)(2,1)S(1)}, u32[]{:S(2)}, u32[]{:S(2)}) collective-permute-start(bf16[32,512]{1,0:T(8,128)(2,1)S(1)} %slice.129), channel_id=1, source_target_pairs={{0,1},{1,2},{2,3},{3,0},{4,5},{5,6},{6,7},{7,4},{8,9},{9,10},{10,1... | collective-permute-start | bytes 98312 | tf_op jit(solution)/shard_map/ppermute | solution.py:711
  572.6 32.9 %collective-permute-start.28 = (bf16[32,512]{1,0:T(8,128)(2,1)S(1)}, bf16[32,512]{1,0:T(8,128)(2,1)S(1)}, u32[]{:S(2)}, u32[]{:S(2)}) collective-permute-start(bf16[32,512]{1,0:T(8,128)(2,1)S(1)} %slice.129), channel_id=1, source_target_pairs={{0,2},{1,3},{2,0},{3,1},{4,6},{5,7},{6,4},{7,5},{8,10},{9,11},{10,... | collective-permute-start | bytes 98312 | tf_op jit(solution)/shard_map/ppermute | solution.py:711
  573.8 31.8 %collective-permute-start.29 = (bf16[32,512]{1,0:T(8,128)(2,1)S(1)}, bf16[32,512]{1,0:T(8,128)(2,1)S(1)}, u32[]{:S(2)}, u32[]{:S(2)}) collective-permute-start(bf16[32,512]{1,0:T(8,128)(2,1)S(1)} %slice.129), channel_id=1, source_target_pairs={{0,3},{1,0},{2,1},{3,2},{4,7},{5,4},{6,5},{7,6},{8,11},{9,8},{10,9... | collective-permute-start | bytes 98312 | tf_op jit(solution)/shard_map/ppermute | solution.py:711
  607.1 38.3 %collective-permute-start.32 = (bf16[1024,768]{1,0:T(8,128)(2,1)}, bf16[1024,768]{1,0:T(8,128)(2,1)S(1)}, u32[]{:S(2)}, u32[]{:S(2)}) collective-permute-start(bf16[1024,768]{1,0:T(8,128)(2,1)} %collective-permute-done.31), channel_id=1, source_target_pairs={{0,1},{1,2},{2,3},{3,0},{4,5},{5,6},{6,7},{7,4},{8,9},{9,10},{10,1... | collective-permute-start | bytes 4718600 | tf_op jit(solution)/shard_map/ppermute | solution.py:711
  (61 other events, 918.7 us)
Sparse Core Ops, SparseCore 0:
  39.9 71.9 all-gather.4
  129.5 89.7 all-gather.6
  246.1 156.1 reduce-scatter.2
  404.5 49.7 reduce-scatter.4
  501.2 31.6 all-gather.8
